TPU v7x, 32 devices: a whole 2x2x4 slice. The times are simulated.
32 devices in a mesh: dp: 2 (over x), ctx: 16 (over z, y, core).
Axes of the slice: x: 2, y: 2, z: 4, core: 2. Of those that a mesh axis runs over, the one named last changes fastest.
Arguments:
- layer_in: bfloat16 [4, 1024, 1600], P('dp', 'ctx'), may hold values from -6 to 6
- out_grad: bfloat16 [4, 1024, 1600], P('dp', 'ctx'), may hold values from -6 to 6
- block_order: int32 [4, 32], P('dp'), may hold values from 0 to 31, as said below
- ln1_gain: float32 [1600], replicated, may hold values from 0.5 to 1.5
- ln1_bias: float32 [1600], replicated, may hold values from -3 to 3
- w_qkv: bfloat16 [1600, 4800], P(None, 'dp'), may hold values from -5 to 5
- qv_bias: float32 [2, 1600], replicated, may hold values from -3 to 3
- w_out: bfloat16 [1600, 1600], P(None, 'dp'), may hold values from -1.5 to 1.5
- out_bias: float32 [1600], replicated, may hold values from -3 to 3
- ln2_gain: float32 [1600], replicated, may hold values from 0.5 to 1.5
- ln2_bias: float32 [1600], replicated, may hold values from -3 to 3
- w_up: bfloat16 [1600, 6400], P(None, 'dp'), may hold values from -0.15625 to 0.15625
- up_bias: float32 [6400], replicated, may hold values from -3 to 3
- w_down: bfloat16 [6400, 1600], P(None, 'dp'), may hold values from -0.078125 to 0.078125
- down_bias: float32 [1600], replicated, may hold values from -3 to 3
Outputs:
- layer_out: bfloat16 [4, 1024, 1600], P('dp', 'ctx')
- input_grad: bfloat16 [4, 1024, 1600], P('dp', 'ctx')
- ln1_gain_grad: float32 [1600], replicated
- ln1_bias_grad: float32 [1600], replicated
- w_qkv_grad: float32 [1600, 4800], P('dp', 'ctx')
- qv_bias_grad: float32 [2, 1600], replicated
- w_out_grad: float32 [1600, 1600], P('ctx', 'dp')
- out_bias_grad: float32 [1600], replicated
- ln2_gain_grad: float32 [1600], replicated
- ln2_bias_grad: float32 [1600], replicated
- w_up_grad: float32 [1600, 6400], P('dp', 'ctx')
- up_bias_grad: float32 [6400], replicated
- w_down_grad: float32 [6400, 1600], P('ctx', 'dp')
- down_bias_grad: float32 [1600], replicated
Inputs may be any that keep to these rules, and one draw needn't show every extreme that they name: `block_order`: each row is a permutation of the half-blocks. Slots 2c and 2c + 1 together hold one unit p (the same p for no two c): in a row of the contiguous form half-blocks 2p and 2p + 1, in a row of the paired form half-blocks p and 31 - p. Each sequence has one form.
All inputs are finite; a program needn't handle non-finite values.
Results may differ from a plain program's by a relative error of at most 0.015.
The roundings to bfloat16 on the way count: a program that leaves them out, or rounds other values in their place, can miss the bound.
Values may be sent and summed in bfloat16 or wider, within the bound.
No kernel may reach another device: no remote copies, remote signals or barrier semaphores. Data moves between devices by JAX's collectives and lax.ppermute only.
A program may use at most 576 MiB of HBM per device.

v0:
```python
from functools import partial
import math

import jax
import jax.numpy as jnp
from jax import lax
from jax.sharding import PartitionSpec as P

HEADS = 25


EPS = 1e-05
GELU_C = 0.7978845608028654
NEG_FILL = -1e30


def shortened(x):
    return jax.tree.map(lambda a: a.astype(jnp.bfloat16) if a.dtype == jnp.float32 else a, x)


def normalize(row_data):
    centre = jnp.mean(row_data, axis=-1, keepdims=True)
    shifted = row_data - centre
    inverse = lax.rsqrt(jnp.mean(shifted * shifted, axis=-1, keepdims=True) + EPS)
    return (shifted * inverse, inverse)


def norm_back(grad_hat, normed, inverse):
    first_mean = jnp.mean(grad_hat, axis=-1, keepdims=True)
    second = jnp.mean(grad_hat * normed, axis=-1, keepdims=True)
    return inverse * (grad_hat - first_mean - normed * second)


def gelu_parts(values):
    cubic_term = 0.044715 * values * values * values
    tangent = jnp.tanh(GELU_C * (values + cubic_term))
    output = 0.5 * values * (1.0 + tangent)
    gelu_slope = 0.5 * (1.0 + tangent) + 0.5 * values * (1.0 - tangent * tangent) * GELU_C * (
        1.0 + 3.0 * 0.044715 * values * values
    )
    return (output, gelu_slope)


def choose_rows(row_count, unit_rows):
    best_rows = unit_rows
    for multiple in range(1, row_count // unit_rows + 1):
        if row_count // unit_rows % multiple == 0 and multiple * unit_rows <= max(unit_rows, 512):
            best_rows = multiple * unit_rows
    return best_rows


def positions(row_ids, order_row, half_rows):
    slot_ids = row_ids // half_rows
    slot_table = slot_ids[:, None] == jnp.arange(order_row.shape[0], dtype=jnp.int32)[None, :]
    slot_base = jnp.sum(jnp.where(slot_table, order_row[None, :], 0), axis=1)
    return slot_base * half_rows + row_ids % half_rows


def split_blocks(members, unit_rows):
    seq_count = members[0].shape[0]
    row_count = members[0].shape[1]
    step_rows = choose_rows(row_count, unit_rows)
    blocks = row_count // step_rows
    pieces = tuple(
        (
            jnp.swapaxes(member.reshape((seq_count, blocks, step_rows) + member.shape[2:]), 0, 1)
            for member in members
        )
    )
    firsts = step_rows * jnp.arange(blocks, dtype=jnp.int32)
    return (pieces, firsts, step_rows)


def keep_state(current):
    return current


def forward_update(query_heads, key_block, value_block, query_pos, key_pos, score_scale, current):
    run_max, run_total, run_acc = current
    scores = (
        jnp.einsum("qhd,khd->hqk", query_heads, key_block, preferred_element_type=jnp.float32)
        * score_scale
    )
    visible = (key_pos[None, :] <= query_pos[:, None])[None]
    new_max = jnp.maximum(run_max, jnp.max(jnp.where(visible, scores, NEG_FILL), axis=-1))
    factor = jnp.exp(run_max - new_max)
    weights = jnp.where(visible, jnp.exp(scores - new_max[:, :, None]), 0.0)
    new_total = run_total * factor + jnp.sum(weights, axis=-1)
    update = jnp.einsum(
        "hqk,khd->qhd", weights, value_block.astype(jnp.float32), precision=lax.Precision.HIGHEST
    )
    return (new_max, new_total, run_acc * factor.T[:, :, None] + update)


def query_update(
    query_heads,
    grad_heads,
    log_rows,
    delta_heads,
    key_block,
    value_block,
    query_pos,
    key_pos,
    score_scale,
    current,
):
    scores = (
        jnp.einsum("qhd,khd->hqk", query_heads, key_block, preferred_element_type=jnp.float32)
        * score_scale
    )
    visible = (key_pos[None, :] <= query_pos[:, None])[None]
    probabilities = jnp.where(visible, jnp.exp(scores - log_rows[:, :, None]), 0.0)
    grad_probs = jnp.einsum(
        "qhd,khd->hqk", grad_heads, value_block, preferred_element_type=jnp.float32
    )
    grad_scores = (probabilities * (grad_probs - delta_heads[:, :, None]) * score_scale).astype(
        jnp.bfloat16
    )
    return current + jnp.einsum(
        "hqk,khd->qhd", grad_scores, key_block, preferred_element_type=jnp.float32
    )


def key_update(
    query_block,
    grad_block,
    log_block,
    delta_block,
    key_heads,
    value_heads,
    query_pos,
    key_pos,
    score_scale,
    current,
):
    grad_keys, grad_values = current
    scores = (
        jnp.einsum("qhd,khd->hqk", query_block, key_heads, preferred_element_type=jnp.float32)
        * score_scale
    )
    visible = (key_pos[None, :] <= query_pos[:, None])[None]
    probabilities = jnp.where(visible, jnp.exp(scores - log_block.T[:, :, None]), 0.0)
    grad_values = grad_values + jnp.einsum(
        "hqk,qhd->khd",
        probabilities.astype(jnp.bfloat16),
        grad_block,
        preferred_element_type=jnp.float32,
    )
    grad_probs = jnp.einsum(
        "qhd,khd->hqk", grad_block, value_heads, preferred_element_type=jnp.float32
    )
    grad_scores = (probabilities * (grad_probs - delta_block.T[:, :, None]) * score_scale).astype(
        jnp.bfloat16
    )
    grad_keys = grad_keys + jnp.einsum(
        "hqk,qhd->khd", grad_scores, query_block, preferred_element_type=jnp.float32
    )
    return (grad_keys, grad_values)


def restack(states, members):
    return tuple((jnp.stack([state[index] for state in states]) for index in range(members)))


def grad_fold(narrows, totals, pieces):
    updated = []
    for total, narrow, piece in zip(totals, narrows, pieces):
        updated.append(jnp.einsum("std,stc->dc", piece, narrow, preferred_element_type=jnp.float32))
    return tuple(updated)


def grad_start(narrows, model_width):
    return tuple((jnp.zeros((model_width, narrow.shape[2]), jnp.float32) for narrow in narrows))


def shards(
    layer_in,
    out_grad,
    block_order,
    ln1_gain,
    ln1_bias,
    w_qkv,
    qv_bias,
    w_out,
    out_bias,
    ln2_gain,
    ln2_bias,
    w_up,
    up_bias,
    w_down,
    down_bias,
):
    seq_count = layer_in.shape[0]
    tok_rows = layer_in.shape[1]
    model_width = layer_in.shape[2]
    all_rows = seq_count * tok_rows
    head_count = HEADS
    head_width = model_width // head_count
    half_rows = tok_rows // 2
    score_scale = 1.0 / math.sqrt(head_width)
    order_rows = [block_order[seq] for seq in range(seq_count)]
    own_ids = lax.axis_index("ctx") * tok_rows + jnp.arange(tok_rows, dtype=jnp.int32)
    own_pos = [positions(own_ids, order_rows[seq], half_rows) for seq in range(seq_count)]
    own_low = [jnp.min(own_pos[seq]) for seq in range(seq_count)]
    own_high = [jnp.max(own_pos[seq]) for seq in range(seq_count)]
    qkv_full, out_full, up_full, down_full = (
        lax.all_gather(w_qkv, "dp", axis=1, tiled=True),
        lax.all_gather(w_out, "dp", axis=1, tiled=True),
        lax.all_gather(w_up, "dp", axis=1, tiled=True),
        lax.all_gather(w_down, "dp", axis=1, tiled=True),
    )
    hidden_units = up_full.shape[1]
    stream = layer_in.reshape(all_rows, model_width).astype(jnp.float32)
    normed_one, inverse_one = normalize(stream)
    hidden_one = (normed_one * ln1_gain + ln1_bias).astype(jnp.bfloat16)
    projected = jnp.dot(hidden_one, qkv_full, preferred_element_type=jnp.float32)
    queries = (projected[:, :model_width] + qv_bias[0]).astype(jnp.bfloat16)
    keys_own = projected[:, model_width : 2 * model_width].astype(jnp.bfloat16)
    values_own = (projected[:, 2 * model_width :] + qv_bias[1]).astype(jnp.bfloat16)
    query_heads = queries.reshape(seq_count, tok_rows, head_count, head_width)
    key_heads = keys_own.reshape(seq_count, tok_rows, head_count, head_width)
    value_heads = values_own.reshape(seq_count, tok_rows, head_count, head_width)
    keys_seq = keys_own.reshape(seq_count, tok_rows, model_width)
    values_seq = values_own.reshape(seq_count, tok_rows, model_width)
    start_state = (
        jnp.full((seq_count, head_count, tok_rows), NEG_FILL, jnp.float32),
        jnp.zeros((seq_count, head_count, tok_rows), jnp.float32),
        jnp.zeros((seq_count, tok_rows, head_count, head_width), jnp.float32),
    )
    accumulated = start_state
    pieces, firsts, step_rows = split_blocks(
        (
            lax.all_gather(keys_seq, "ctx", axis=1, tiled=True),
            lax.all_gather(values_seq, "ctx", axis=1, tiled=True),
        ),
        tok_rows,
    )

    def forward_visit_block(running, element):
        key_block, value_block, first_row = element
        block_ids = first_row + jnp.arange(step_rows, dtype=jnp.int32)
        states = []
        for seq in range(seq_count):
            key_pos = positions(block_ids, order_rows[seq], half_rows)
            update = partial(
                forward_update,
                query_heads[seq],
                key_block[seq].reshape(step_rows, head_count, head_width),
                value_block[seq].reshape(step_rows, head_count, head_width),
                own_pos[seq],
                key_pos,
                score_scale,
            )
            current = (running[0][seq], running[1][seq], running[2][seq])
            states.append(lax.cond(jnp.min(key_pos) > own_high[seq], keep_state, update, current))
        return (restack(states, 3), None)

    accumulated, unused = lax.scan(forward_visit_block, accumulated, (pieces[0], pieces[1], firsts))
    run_max, run_total, run_acc = accumulated
    attended = (
        (run_acc / jnp.swapaxes(run_total, 1, 2)[:, :, :, None])
        .reshape(all_rows, model_width)
        .astype(jnp.bfloat16)
    )
    log_total = run_max + jnp.log(run_total)
    residual = stream + jnp.dot(attended, out_full, preferred_element_type=jnp.float32) + out_bias
    normed_two, inverse_two = normalize(residual)
    hidden_two = (normed_two * ln2_gain + ln2_bias).astype(jnp.bfloat16)
    pre_act = jnp.dot(hidden_two, up_full, preferred_element_type=jnp.float32) + up_bias
    activated_wide, gelu_slope = gelu_parts(pre_act)
    activated = activated_wide.astype(jnp.bfloat16)
    layer_out = (
        residual + jnp.dot(activated, down_full, preferred_element_type=jnp.float32) + down_bias
    ).astype(jnp.bfloat16)
    grad_rows = out_grad.reshape(all_rows, model_width)
    grad_out = grad_rows.astype(jnp.float32)
    grad_pre = (
        jnp.einsum("td,fd->tf", grad_rows, down_full, preferred_element_type=jnp.float32)
        * gelu_slope
    ).astype(jnp.bfloat16)
    activated_seq = activated.reshape(seq_count, tok_rows, hidden_units)
    pre_seq = grad_pre.reshape(seq_count, tok_rows, hidden_units)
    hidden_two_seq = hidden_two.reshape(seq_count, tok_rows, model_width)
    grad_hidden_two = jnp.einsum("tf,df->td", grad_pre, up_full, preferred_element_type=jnp.float32)
    grad_residual = grad_out + norm_back(grad_hidden_two * ln2_gain, normed_two, inverse_two)
    grad_mixed = grad_residual.astype(jnp.bfloat16)
    grad_attended = jnp.einsum(
        "tb,ab->ta", grad_mixed, out_full, preferred_element_type=jnp.float32
    ).astype(jnp.bfloat16)
    grad_heads = grad_attended.reshape(seq_count, tok_rows, head_count, head_width)
    attended_heads = attended.reshape(seq_count, tok_rows, head_count, head_width)
    delta_rows = jnp.sum(
        grad_heads.astype(jnp.float32) * attended_heads.astype(jnp.float32), axis=-1
    )
    delta_heads = jnp.swapaxes(delta_rows, 1, 2)
    zero_heads = jnp.zeros((seq_count, tok_rows, head_count, head_width), jnp.float32)
    accumulated = zero_heads
    pieces, firsts, query_step_rows = split_blocks(
        (
            lax.all_gather(keys_seq, "ctx", axis=1, tiled=True),
            lax.all_gather(values_seq, "ctx", axis=1, tiled=True),
        ),
        tok_rows,
    )

    def query_visit_block(running, element):
        key_block, value_block, first_row = element
        block_ids = first_row + jnp.arange(query_step_rows, dtype=jnp.int32)
        states = []
        for seq in range(seq_count):
            key_pos = positions(block_ids, order_rows[seq], half_rows)
            update = partial(
                query_update,
                query_heads[seq],
                grad_heads[seq],
                log_total[seq],
                delta_heads[seq],
                key_block[seq].reshape(query_step_rows, head_count, head_width),
                value_block[seq].reshape(query_step_rows, head_count, head_width),
                own_pos[seq],
                key_pos,
                score_scale,
            )
            states.append(
                lax.cond(jnp.min(key_pos) > own_high[seq], keep_state, update, running[seq])
            )
        return (jnp.stack(states), None)

    accumulated, unused = lax.scan(query_visit_block, accumulated, (pieces[0], pieces[1], firsts))
    grad_queries = accumulated
    outgoing = (
        queries.reshape(seq_count, tok_rows, model_width).astype(jnp.float32),
        grad_attended.reshape(seq_count, tok_rows, model_width).astype(jnp.float32),
        jnp.swapaxes(log_total, 1, 2),
        delta_rows,
    )
    accumulated = (zero_heads, zero_heads)
    pieces, firsts, key_step_rows = split_blocks(
        (
            lax.all_gather(outgoing[0], "ctx", axis=1, tiled=True),
            lax.all_gather(outgoing[1], "ctx", axis=1, tiled=True),
            lax.all_gather(outgoing[2], "ctx", axis=1, tiled=True),
            lax.all_gather(outgoing[3], "ctx", axis=1, tiled=True),
        ),
        tok_rows,
    )

    def key_visit_block(running, element):
        query_block, grad_block, log_block, delta_block, first_row = element
        block_ids = first_row + jnp.arange(key_step_rows, dtype=jnp.int32)
        states = []
        for seq in range(seq_count):
            query_pos = positions(block_ids, order_rows[seq], half_rows)
            update = partial(
                key_update,
                query_block[seq]
                .astype(jnp.bfloat16)
                .reshape(key_step_rows, head_count, head_width),
                grad_block[seq].astype(jnp.bfloat16).reshape(key_step_rows, head_count, head_width),
                log_block[seq],
                delta_block[seq],
                key_heads[seq],
                value_heads[seq],
                query_pos,
                own_pos[seq],
                score_scale,
            )
            current = (running[0][seq], running[1][seq])
            states.append(lax.cond(jnp.max(query_pos) < own_low[seq], keep_state, update, current))
        return (restack(states, 2), None)

    accumulated, unused = lax.scan(
        key_visit_block, accumulated, (pieces[0], pieces[1], pieces[2], pieces[3], firsts)
    )
    grad_keys, grad_values = accumulated
    grad_proj = jnp.concatenate(
        [
            grad_queries.reshape(all_rows, model_width).astype(jnp.bfloat16),
            grad_keys.reshape(all_rows, model_width).astype(jnp.bfloat16),
            grad_values.reshape(all_rows, model_width).astype(jnp.bfloat16),
        ],
        axis=1,
    )
    grad_hidden_one = jnp.einsum(
        "te,de->td", grad_proj, qkv_full, preferred_element_type=jnp.float32
    )
    input_grad = (
        grad_residual + norm_back(grad_hidden_one * ln1_gain, normed_one, inverse_one)
    ).astype(jnp.bfloat16)
    proj_wide = grad_proj.astype(jnp.float32)
    qv_terms = jnp.stack(
        [
            jnp.sum(proj_wide[:, :model_width], axis=0),
            jnp.sum(proj_wide[:, 2 * model_width :], axis=0),
        ]
    )
    small_sums = lax.psum(
        (
            jnp.sum(grad_hidden_one * normed_one, axis=0),
            jnp.sum(grad_hidden_one, axis=0),
            qv_terms,
            jnp.sum(grad_mixed.astype(jnp.float32), axis=0),
            jnp.sum(grad_hidden_two * normed_two, axis=0),
            jnp.sum(grad_hidden_two, axis=0),
            jnp.sum(grad_pre.astype(jnp.float32), axis=0),
            jnp.sum(grad_out, axis=0),
        ),
        ("dp", "ctx"),
    )
    attended_seq = attended.reshape(seq_count, tok_rows, model_width)
    proj_seq = grad_proj.reshape(seq_count, tok_rows, 3 * model_width)
    mixed_seq = grad_mixed.reshape(seq_count, tok_rows, model_width)
    hidden_one_seq = hidden_one.reshape(seq_count, tok_rows, model_width)
    narrow_all = (
        lax.all_to_all(proj_seq, "ctx", split_axis=2, concat_axis=1, tiled=True),
        lax.all_to_all(attended_seq, "ctx", split_axis=2, concat_axis=1, tiled=True),
        lax.all_to_all(pre_seq, "ctx", split_axis=2, concat_axis=1, tiled=True),
        lax.all_to_all(activated_seq, "ctx", split_axis=2, concat_axis=1, tiled=True),
    )
    terms = grad_fold(
        narrow_all,
        grad_start(narrow_all, model_width),
        (
            lax.all_gather(hidden_one_seq, "ctx", axis=1, tiled=True),
            lax.all_gather(mixed_seq, "ctx", axis=1, tiled=True),
            lax.all_gather(hidden_two_seq, "ctx", axis=1, tiled=True),
            lax.all_gather(out_grad, "ctx", axis=1, tiled=True),
        ),
    )
    reduced = jax.tree.map(
        lambda part: part.astype(jnp.float32),
        lax.psum_scatter(shortened(terms), "dp", scatter_dimension=0, tiled=True),
    )
    qkv_grad = reduced[0]
    out_grad_block = reduced[1].T
    up_grad = reduced[2]
    down_grad = reduced[3].T
    layer_out = layer_out.reshape(seq_count, tok_rows, model_width)
    input_grad = input_grad.reshape(seq_count, tok_rows, model_width)
    return (
        layer_out,
        input_grad,
        small_sums[0],
        small_sums[1],
        qkv_grad,
        small_sums[2],
        out_grad_block,
        small_sums[3],
        small_sums[4],
        small_sums[5],
        up_grad,
        small_sums[6],
        down_grad,
        small_sums[7],
    )


def solution(mesh):
    placed = (
        P("dp", "ctx", None),
        P("dp", "ctx", None),
        P("dp", None),
        P(),
        P(),
        P(None, "dp"),
        P(),
        P(None, "dp"),
        P(),
        P(),
        P(),
        P(None, "dp"),
        P(),
        P(None, "dp"),
        P(),
    )
    return jax.shard_map(
        shards,
        mesh=mesh,
        in_specs=placed,
        out_specs=(
            P("dp", "ctx", None),
            P("dp", "ctx", None),
            P(),
            P(),
            P("dp", "ctx"),
            P(),
            P("ctx", "dp"),
            P(),
            P(),
            P(),
            P("dp", "ctx"),
            P(),
            P("ctx", "dp"),
            P(),
        ),
        check_vma=False,
    )
```

profile of v0, /device:TPU:25, one launch (start us, length us, event | category | flops | bytes accessed | tf_op | source)
XLA Modules:
  0.0 1633.9 jit_solution(8118224483249551954)
XLA Ops:
  9.0 186.6 %all-gather.36.cloned.1.call-done = bf16[2,2400,1600]{1,2,0:T(8,128)(2,1)} async-done(((bf16[1,2400,1600]{1,2,0:T(8,128)(2,1)}), bf16[2,2400,1600]{1,2,0:T(8,128)(2,1)}) %all-gather.36.cloned.1.call-update) | async-done | bytes 15360016 | tf_op jit(solution)/shard_map/all_gather | solution.py:207
  195.6 22.0 %copy.243 = bf16[2,2400,1600]{2,1,0:T(8,128)(2,1)} copy(bf16[2,2400,1600]{1,2,0:T(8,128)(2,1)} %all-gather.36.cloned.1.call-done) | data formatting | bytes 30720000 | tf_op jit(solution)/shard_map/all_gather | solution.py:207
  217.6 8.1 fusion.135
  237.1 53.6 %all-gather.14.cloned.1.call-done = bf16[2,1024,1600]{2,1,0:T(8,128)(2,1)} async-done(((bf16[2,64,1600]{2,1,0:T(8,128)(2,1)}), bf16[2,1024,1600]{2,1,0:T(8,128)(2,1)}) %all-gather.14.cloned.1.call-update) | async-done | bytes 6553616 | tf_op jit(solution)/shard_map/all_gather | solution.py:233
  290.7 9.8 copy.246
  300.6 56.3 %all-gather.16.cloned.1.call-done = bf16[2,1024,1600]{2,1,0:T(8,128)(2,1)} async-done(((bf16[2,64,1600]{2,1,0:T(8,128)(2,1)}), bf16[2,1024,1600]{2,1,0:T(8,128)(2,1)}) %all-gather.16.cloned.1.call-update) | async-done | bytes 6553616 | tf_op jit(solution)/shard_map/all_gather | solution.py:234
  356.8 9.8 copy.247
  368.0 59.0 %while.42 = (s32[]{:T(128)}, f32[2,25,64]{2,1,0:T(8,128)S(1)}, f32[2,25,64]{2,1,0:T(8,128)S(1)}, f32[2,64,25,64]{3,1,2,0:T(8,128)}, s32[2]{0:T(128)S(1)}, /*inde...) while((s32[]{:T(128)}, f32[2,25,64]{2,1,0:T(8,128)S(1)}, ...), condition=%wide.region_19.20_spmd, body=%wide.region_6.19_spmd.sunk | while | flops 1485184640 | bytes 68559160 | solution.py:258
  379.0 7.6 conditional.12
  387.9 6.9 conditional.13
  408.3 7.6 conditional.12
  417.3 6.9 conditional.13
  436.6 233.9 %all-gather.20.cloned.1.call-done = bf16[1600,6400]{1,0:T(8,128)(2,1)} async-done(((bf16[1600,3200]{1,0:T(8,128)(2,1)}), bf16[1600,6400]{1,0:T(8,128)(2,1)}) %all-gather.20.cloned.1.call-update) | async-done | bytes 20480016 | tf_op jit(solution)/shard_map/all_gather | solution.py:209
  670.4 13.5 multiply_convert_fusion.4
  683.9 229.9 %all-gather.22.cloned.1.call-done = bf16[6400,1600]{0,1:T(8,128)(2,1)} async-done(((bf16[6400,800]{0,1:T(8,128)(2,1)}), bf16[6400,1600]{0,1:T(8,128)(2,1)}) %all-gather.22.cloned.1.call-update) | async-done | bytes 20480016 | tf_op jit(solution)/shard_map/all_gather | solution.py:210
  913.9 10.6 convert_reduce_fusion
  924.4 13.2 multiply_reduce_fusion.2
  955.8 55.5 %all_to_all.72 = bf16[16,2,25600]{2,1,0:T(2,128)(2,1)} all-to-all(bf16[16,2,25600]{2,1,0:T(2,128)(2,1)S(1)} %reshape.551), channel_id=1, replica_groups=mesh['dp'=2,'ctx'=16] {'ctx'}, dimensions={0} | all-to-all | bytes 3276800 | tf_op jit(solution)/shard_map/all_to_all | solution.py:418
  1015.0 6.6 copy.314
  1021.6 6.8 fusion.128
  1033.3 6.4 all-to-all-start.1
  1060.0 7.7 all-to-all-start.2
  1070.2 73.9 %while.43 = (s32[]{:T(128)}, f32[2,64,25,64]{3,1,2,0:T(8,128)}, s32[2]{0:T(128)S(1)}, s32[1,32]{1,0:T(1,128)S(1)}, s32[]{:T(128)}, /*index=5*/bf16[2,2,512,1600]...) while((s32[]{:T(128)}, f32[2,64,25,64]{3,1,2,0:T(8,128)}, ...), condition=%wide.region_34.35_spmd, body=%wide.region_25.34_spmd.sunk | while | flops 641187840 | bytes 79694328 | solution.py:329
  1081.0 10.9 conditional.14
  1093.2 10.9 conditional.15
  1117.8 11.0 conditional.14
  1130.1 10.9 conditional.15
  1148.3 9.8 copy.267
  1158.1 25.9 %all_gather.51 = f32[2,1024,25]{2,0,1:T(2,128)S(1)} all-gather(f32[2,64,25]{2,0,1:T(2,128)S(1)} %bitcast.442), channel_id=1, replica_groups=mesh['dp'=2,'ctx'=16] {'ctx'}, dimensions={1}, use_global_device_ids=true | all-gather | bytes 217600 | tf_op jit(solution)/shard_map/all_gather | solution.py:342
  1185.1 27.6 %all_gather.53 = f32[2,1024,25]{2,0,1:T(2,128)S(1)} all-gather(f32[2,64,25]{2,0,1:T(2,128)S(1)} %copy.265), channel_id=1, replica_groups=mesh['dp'=2,'ctx'=16] {'ctx'}, dimensions={1}, use_global_device_ids=true | all-gather | bytes 217600 | tf_op jit(solution)/shard_map/all_gather | solution.py:343
  1223.6 6.8 copy.312
  1230.4 9.8 copy.269
  1242.9 93.1 %while.44 = (s32[]{:T(128)}, f32[2,64,25,64]{3,1,2,0:T(8,128)}, f32[2,64,25,64]{3,1,2,0:T(8,128)}, s32[2]{0:T(128)S(1)}, s32[1,32]{1,0:T(1,128)S(1)}, /*index=5*...) while((s32[]{:T(128)}, f32[2,64,25,64]{3,1,2,0:T(8,128)}, ...), condition=%wide.region_46.47_spmd, body=%wide.region_37.46_spmd.sunk | while | flops 857866240 | bytes 126947112 | solution.py:372
  1253.2 15.7 conditional.16
  1270.1 14.9 conditional.17
  1276.1 5.7 fusion.66
  1299.8 15.4 conditional.16
  1304.8 6.0 fusion.95
  1316.4 14.9 conditional.17
  1322.4 5.7 fusion.66
  1353.6 6.4 all-to-all-start
  1365.6 7.2 fusion.125
  1376.5 11.0 fusion.131
  1420.4 5.8 fusion.127
  1428.1 13.9 multiply_reduce_fusion.3
  1449.2 10.9 reduce-scatter.17.cloned.1.call-done
  1462.8 21.8 %reduce-scatter.13.cloned.1.call-done = bf16[800,300]{1,0:T(8,128)(2,1)} async-done(((bf16[1600,300]{1,0:T(8,128)(2,1)}), bf16[800,300]{1,0:T(8,128)(2,1)}) %reduce-scatter.13.cloned.1.call-update) | async-done | bytes 480016
  1487.0 129.6 %all-reduce.3.cloned.1.call-done = (f32[1600]{0:T(1024)}, f32[1600]{0:T(1024)}, f32[2,1600]{1,0:T(2,128)}, f32[1600]{0:T(1024)}, f32[1600]{0:T(1024)}, /*index=5*/f32[1600]{0:T(1024)}, f32[6400]{0:T(1024)}, f32[1600]{0:T(1024)}) async-done(((f32[1600]{0:T(1024)}, f32[1600]{0:T(1024)}, f32[2,1600]{1,0:T(2,128)}, f32[1600]{0:T(1024)}, f32[1600]{0:T(1024)}, /*index=5*/f32[1600]{0:T(1024)}, f32[6400]{0:T(1024)}, ...) | async-done | bytes 76816 | tf_op jit(solution)/shard_map/psum | solution.py:397
  (577 shorter events, 367.3 us)
Async XLA Ops:
  7.2 188.4 %all-gather.36.cloned.1.call-start = ((), (), s32[]{:S(2)}) async-start(), calls=%async_computation.19 | async-start | bytes 23347200 | tf_op jit(solution)/shard_map/all_gather | solution.py:207
  7.9 282.8 %all-gather.14.cloned.1.call-start = ((), (), s32[]{:S(2)}) async-start(), calls=%async_computation.8 | async-start | bytes 7241728 | tf_op jit(solution)/shard_map/all_gather | solution.py:233
  8.4 209.1 %copy-start.24 = (f32[128,1600]{0,1:T(8,128)}, f32[128,1600]{0,1:T(8,128)S(1)}, u32[]{:S(2)}) copy-start(f32[128,1600]{0,1:T(8,128)S(1)} %copy.250) | copy-start | bytes 2457604
  8.6 209.0 %copy-start.79 = (f32[2,64]{1,0:T(2,128)}, f32[2,64]{1,0:T(2,128)S(1)}, u32[]{:S(2)}) copy-start(f32[2,64]{1,0:T(2,128)S(1)} %broadcast_multiply_fusion) | copy-start | bytes 1540
  8.7 208.9 %copy-start.86 = (f32[128]{0:T(128)}, f32[128]{0:T(128)S(1)}, u32[]{:S(2)}) copy-start(f32[128]{0:T(128)S(1)} %div.91) | copy-start | bytes 1540
  8.9 208.6 %copy-start.90 = (f32[2,64]{1,0:T(2,128)}, f32[2,64]{1,0:T(2,128)S(1)}, u32[]{:S(2)}) copy-start(f32[2,64]{1,0:T(2,128)S(1)} %add_rsqrt_fusion) | copy-start | bytes 1540
  9.0 208.6 %copy-start.88 = (f32[128]{0:T(128)}, f32[128]{0:T(128)S(1)}, u32[]{:S(2)}) copy-start(f32[128]{0:T(128)S(1)} %rsqrt.21) | copy-start | bytes 1540
  9.0 208.6 %copy-start.60 = (f32[1600]{0:T(1024)S(1)}, f32[1600]{0:T(1024)}, u32[]{:S(2)}) copy-start(f32[1600]{0:T(1024)} %param.36) | copy-start | bytes 19204
  9.0 208.6 %copy-start.73 = (f32[1600]{0:T(1024)S(1)}, f32[1600]{0:T(1024)}, u32[]{:S(2)}) copy-start(f32[1600]{0:T(1024)} %param.37) | copy-start | bytes 19204
  226.8 130.0 %all-gather.16.cloned.1.call-start = ((), (), s32[]{:S(2)}) async-start(), calls=%async_computation.9 | async-start | bytes 7241728 | tf_op jit(solution)/shard_map/all_gather | solution.py:234
  229.1 202.5 %all-gather.18.cloned.1.call-start = ((), (), s32[]{:S(2)}) async-start(), calls=%async_computation.10 | async-start | bytes 7987200 | tf_op jit(solution)/shard_map/all_gather | solution.py:208
  229.7 440.7 %all-gather.20.cloned.1.call-start = ((), (), s32[]{:S(2)}) async-start(), calls=%async_computation.11 | async-start | bytes 30720000 | tf_op jit(solution)/shard_map/all_gather | solution.py:209
  230.3 683.5 %all-gather.22.cloned.1.call-start = ((), (), s32[]{:S(2)}) async-start(), calls=%async_computation.12 | async-start | bytes 30720000 | tf_op jit(solution)/shard_map/all_gather | solution.py:210
  230.9 790.7 %all-gather.34.cloned.1.call-start = ((), (), s32[]{:S(2)}) async-start(), calls=%async_computation.18 | async-start | bytes 7241728 | tf_op jit(solution)/shard_map/all_gather | solution.py:427
  231.7 916.6 %all-gather.24.cloned.1.call-start = ((), (), s32[]{:S(2)}) async-start(), calls=%async_computation.13 | async-start | bytes 7241728 | tf_op jit(solution)/shard_map/all_gather | solution.py:340
  232.7 997.7 %all-gather.26.cloned.1.call-start = ((), (), s32[]{:S(2)}) async-start(), calls=%async_computation.14 | async-start | bytes 7241728 | tf_op jit(solution)/shard_map/all_gather | solution.py:341
  431.6 238.8 %copy-start.75 = (f32[6400]{0:T(1024)S(1)}, f32[6400]{0:T(1024)}, u32[]{:S(2)}) copy-start(f32[6400]{0:T(1024)} %param.45) | copy-start | bytes 76804
  435.8 501.9 %copy-start.20 = (f32[128,1600]{0,1:T(8,128)}, f32[128,1600]{0,1:T(8,128)S(1)}, u32[]{:S(2)}) copy-start(f32[128,1600]{0,1:T(8,128)S(1)} %get-tuple-element.1376) | copy-start | bytes 2457604
  435.8 501.9 %copy-start.77 = (f32[128]{0:T(128)}, f32[128]{0:T(128)S(1)}, u32[]{:S(2)}) copy-start(f32[128]{0:T(128)S(1)} %broadcast_multiply_fusion.5) | copy-start | bytes 1540
  436.0 501.7 %copy-start.84 = (f32[128]{0:T(128)}, f32[128]{0:T(128)S(1)}, u32[]{:S(2)}) copy-start(f32[128]{0:T(128)S(1)} %add_rsqrt_fusion.1) | copy-start | bytes 1540
  436.6 477.3 %copy-start.43 = (bf16[2,64,1600]{2,1,0:T(8,128)(2,1)S(1)}, bf16[2,64,1600]{2,1,0:T(8,128)(2,1)}, u32[]{:S(2)}) copy-start(bf16[2,64,1600]{2,1,0:T(8,128)(2,1)} %param.34) | copy-start | bytes 1228804
  683.9 262.9 %copy-start.27 = (bf16[128,6400]{1,0:T(8,128)(2,1)}, bf16[128,6400]{1,0:T(8,128)(2,1)S(1)}, u32[]{:S(2)}) copy-start(bf16[128,6400]{1,0:T(8,128)(2,1)S(1)} %get-tuple-element.1377) | copy-start | bytes 4915204
  924.4 13.2 copy-start.29
  924.4 13.3 copy-start.50
  944.6 415.5 %all-gather.30.cloned.1.call-start = ((), (), s32[]{:S(2)}) async-start(), calls=%async_computation.16 | async-start | bytes 7241728 | tf_op jit(solution)/shard_map/all_gather | solution.py:425
  945.7 419.9 %all-gather.32.cloned.1.call-start = ((), (), s32[]{:S(2)}) async-start(), calls=%async_computation.17 | async-start | bytes 7241728 | tf_op jit(solution)/shard_map/all_gather | solution.py:426
  946.8 445.7 %reduce-scatter.19.cloned.1.call-start = ((), (), s32[]{:S(2)}) async-start(), calls=%async_computation.23 | async-start | bytes 2457600
  1028.5 11.2 copy-start.44
  1030.7 9.6 copy-start.53
  1030.7 10.9 copy-start.46
  1030.7 389.6 %all-gather.28.cloned.1.call-start = ((), (), s32[]{:S(2)}) async-start(), calls=%async_computation.15 | async-start | bytes 7241728 | tf_op jit(solution)/shard_map/all_gather | solution.py:424
  1033.3 26.8 %all-to-all-start.1 = ((bf16[16,2,6400]{2,1,0:T(2,128)(2,1)}), bf16[16,2,6400]{2,1,0:T(2,128)(2,1)}, u32[]{:S(2)}, u32[]{:S(2)}) async-start(bf16[16,2,6400]{2,1,0:T(2,128)(2,1)} %reshape.547), calls=%async_computation.1 | async-start | bytes 819200 | tf_op jit(solution)/shard_map/all_to_all | solution.py:416
  1054.4 13.3 copy-start.11
  1059.4 10.8 copy-start.98
  1060.0 159.8 %all-to-all-start.2 = ((bf16[16,2,25600]{2,1,0:T(2,128)(2,1)}), bf16[16,2,25600]{2,1,0:T(2,128)(2,1)}, u32[]{:S(2)}, u32[]{:S(2)}) async-start(bf16[16,2,25600]{2,1,0:T(2,128)(2,1)} %reshape.549), calls=%async_computation.2 | async-start | bytes 3276800 | tf_op jit(solution)/shard_map/all_to_all | solution.py:417
  1107.0 9.4 copy-start.63
  1353.6 57.2 %all-to-all-start = ((bf16[16,2,19200]{2,1,0:T(2,128)(2,1)}), bf16[16,2,19200]{2,1,0:T(2,128)(2,1)}, u32[]{:S(2)}, u32[]{:S(2)}) async-start(bf16[16,2,19200]{2,1,0:T(2,128)(2,1)} %reshape.545), calls=%async_computation | async-start | bytes 2457600 | tf_op jit(solution)/shard_map/all_to_all | solution.py:415
  1360.0 87.3 %reduce-scatter.15.cloned.1.call-start = ((), (), s32[]{:S(2)}) async-start(), calls=%async_computation.21 | async-start | bytes 614400
  1365.5 94.6 %reduce-scatter.17.cloned.1.call-start = ((), (), s32[]{:S(2)}) async-start(), calls=%async_computation.22 | async-start | bytes 2457600
  1376.4 108.2 %reduce-scatter.13.cloned.1.call-start = ((), (), s32[]{:S(2)}) async-start(), calls=%async_computation.20 | async-start | bytes 1843200
  1428.0 14.0 copy-start.36
  1428.0 14.0 copy-start.51
  1428.0 14.0 copy-start.72
  1428.0 14.0 copy-start.78
  1428.0 14.0 copy-start.85
  1428.0 14.0 copy-start.93
  1428.0 14.0 copy-start.95
  1428.0 188.6 %all-reduce.3.cloned.1.call-start = ((), (), s32[]{:S(2)}) async-start(), calls=%async_computation.24 | async-start | bytes 182272 | tf_op jit(solution)/shard_map/psum | solution.py:397
  (110 other events, 378.5 us)
Sparse Core Ops, SparseCore 0:
  9.5 186.0 all-gather.35
  226.9 63.7 all-gather.13
  293.6 63.1 all-gather.15
  358.2 68.8 all-gather.17
  428.5 241.8 all-gather.19
  671.9 241.9 all-gather.21
  916.1 82.4 all-gather.33
  1000.9 69.7 all-gather.23
  1073.5 79.7 all-gather.25
  1155.5 75.6 all-gather.29
  1233.5 63.6 all-gather.31
  1299.3 26.2 reduce-scatter.18
  1327.9 86.6 all-gather.27
  1416.7 14.2 reduce-scatter.14
  1433.2 26.8 reduce-scatter.16
  1462.2 22.3 reduce-scatter.12
  1492.0 124.6 all-reduce.2
where the time goes:
time: 1650 us; the launch traced here: 1630 us
  waiting for transfers between devices  932 us (56%)
  local copies, waits for them, and re-layouts  279 us (17%)
  matrix products  199 us (12%)
  blocking collectives  109 us (7%)
  other arithmetic  61.4 us (4%)
  starting transfers between devices  21.3 us (1%)
  loops' own time  17.1 us (1%)
    all_gather x1, waiting for transfers between devices, shards(): lax.all_gather(w_up, 'dp', axis=1, tiled=True)  234 us
    all_gather x1, waiting for transfers between devices, shards(): lax.all_gather(w_down, 'dp', axis=1, tiled=True)  230 us
    all_gather x1, waiting for transfers between devices, shards(): lax.all_gather(w_qkv, 'dp', axis=1, tiled=True)  187 us
    psum x1, waiting for transfers between devices, shards(): lax.psum((jnp.sum(grad_hidden_one * normed_one, axis=0), jnp.sum(grad_hid...  130 us
    all_gather x1, waiting for transfers between devices, shards(): lax.all_gather(values_seq, 'ctx', axis=1, tiled=True)  56.3 us
    all_to_all x1, blocking collectives, shards(): lax.all_to_all(activated_seq, 'ctx', split_axis=2, concat_axis=1, tiled=T...  55.5 us
    unnamed x158, local copies, waits for them, and re-layouts  55 us
    all_gather x1, waiting for transfers between devices, shards(): lax.all_gather(keys_seq, 'ctx', axis=1, tiled=True)  53.6 us
  transfers between devices with their start and end apart: 20, of which 10 were waited for; matrix products, arithmetic and copies ran while one was open for 30% of the time, Pallas kernels for 0%

commit v1 on v0

v1 whole, which is shorter than its diff:
```python
from functools import partial
import math

import jax
import jax.numpy as jnp
from jax import lax
from jax.experimental import pallas as pl
from jax.experimental.pallas import tpu as pltpu
from jax.sharding import PartitionSpec as P

HEADS = 25


EPS = 1e-05
GELU_C = 0.7978845608028654
NEG_FILL = -1e30
BF16 = jnp.bfloat16
F32 = jnp.float32


def normalize(row_data):
    centre = jnp.mean(row_data, axis=-1, keepdims=True)
    shifted = row_data - centre
    inverse = lax.rsqrt(jnp.mean(shifted * shifted, axis=-1, keepdims=True) + EPS)
    return (shifted * inverse, inverse)


def norm_back(grad_hat, normed, inverse):
    first_mean = jnp.mean(grad_hat, axis=-1, keepdims=True)
    second = jnp.mean(grad_hat * normed, axis=-1, keepdims=True)
    return inverse * (grad_hat - first_mean - normed * second)


def gelu_parts(values):
    cubic_term = 0.044715 * values * values * values
    tangent = jnp.tanh(GELU_C * (values + cubic_term))
    output = 0.5 * values * (1.0 + tangent)
    gelu_slope = 0.5 * (1.0 + tangent) + 0.5 * values * (1.0 - tangent * tangent) * GELU_C * (
        1.0 + 3.0 * 0.044715 * values * values
    )
    return (output, gelu_slope)


def head_parts(value, head_width):
    heads = value.shape[1] // head_width
    if heads == 1:
        return [value]
    lane = lax.broadcasted_iota(jnp.int32, value.shape, 1) // head_width
    return [jnp.where(lane == h, value, jnp.zeros_like(value)) for h in range(heads)]


def by_head(columns, shape, head_width):
    if len(columns) == 1:
        return jnp.broadcast_to(columns[0], shape)
    lane = lax.broadcasted_iota(jnp.int32, shape, 1) // head_width
    result = jnp.broadcast_to(columns[-1], shape)
    for h in range(len(columns) - 2, -1, -1):
        result = jnp.where(lane == h, columns[h], result)
    return result


def dot(a, b, contract):
    return lax.dot_general(a, b, (contract, ((), ())), preferred_element_type=F32)


def each_query_block(length, block, visit):
    if length // block <= 4:
        for index in range(length // block):
            chunks = [(0, index * block, False)] if index else []
            visit(index * block, chunks + [(index * block, block, True)])
    else:

        def step(index, carry):
            visit(pl.multiple_of(index * block, block), [(0, length, True)])
            return carry

        lax.fori_loop(0, length // block, step, 0)


def visible_mask(first_row, rows, first_key, keys):
    row_ids = first_row + lax.broadcasted_iota(jnp.int32, (rows, keys), 0)
    key_ids = first_key + lax.broadcasted_iota(jnp.int32, (rows, keys), 1)
    return key_ids <= row_ids


def forward_kernel(
    half, block, head_width, score_scale, order, qkv, slot_out, natural, out_rows, log_rows
):
    seq = pl.program_id(0)
    sources = qkv.shape[0]
    length = natural.shape[2]

    def place(source, carry):
        for part in range(2):
            first = pl.multiple_of(order[seq, 2 * source + part] * half, half)
            for kind in range(3):
                natural[kind, 0, pl.ds(first, half), :] = qkv[
                    source, kind, 0, part * half : (part + 1) * half, :
                ]
        return carry

    lax.fori_loop(0, sources, place, 0)

    def visit(first_row, chunks):
        rows = pl.ds(first_row, block)
        queries = natural[0, 0, rows, :] * jnp.asarray(score_scale, BF16)
        outputs = []
        logs = []
        for query in head_parts(queries, head_width):
            scores = []
            for first_key, keys, masked in chunks:
                part = dot(query, natural[1, 0, first_key : first_key + keys, :], ((1,), (1,)))
                if masked:
                    part = jnp.where(
                        visible_mask(first_row, block, first_key, keys), part, NEG_FILL
                    )
                scores.append(part)
            top = jnp.max(scores[0], axis=1, keepdims=True)
            for part in scores[1:]:
                top = jnp.maximum(top, jnp.max(part, axis=1, keepdims=True))
            total = jnp.zeros((block, 1), F32)
            summed = jnp.zeros((block, queries.shape[1]), F32)
            for (first_key, keys, masked), part in zip(chunks, scores):
                weights = jnp.exp(part - top)
                total = total + jnp.sum(weights, axis=1, keepdims=True)
                coarse = weights.astype(BF16)
                fine = (weights - coarse.astype(F32)).astype(BF16)
                values = natural[2, 0, first_key : first_key + keys, :]
                summed = summed + dot(coarse, values, ((1,), (0,))) + dot(fine, values, ((1,), (0,)))
            outputs.append(summed / total)
            logs.append(top + jnp.log(total))
        result = outputs[0]
        if len(outputs) > 1:
            lane = lax.broadcasted_iota(jnp.int32, result.shape, 1) // head_width
            for h in range(1, len(outputs)):
                result = jnp.where(lane == h, outputs[h], result)
        out_rows[0, rows, :] = result.astype(BF16)
        log_rows[0, rows, :] = by_head(logs, result.shape, head_width)

    each_query_block(length, block, visit)

    def give(source, carry):
        for part in range(2):
            first = pl.multiple_of(order[seq, 2 * source + part] * half, half)
            slot_out[source, 0, part * half : (part + 1) * half, :] = out_rows[
                0, pl.ds(first, half), :
            ]
        return carry

    lax.fori_loop(0, sources, give, 0)


def backward_kernel(
    half,
    block,
    head_width,
    score_scale,
    order,
    natural,
    out_rows,
    log_rows,
    grad_slots,
    slot_out,
    grad_rows,
    grad_queries,
    grad_keys,
    grad_values,
):
    seq = pl.program_id(0)
    sources = grad_slots.shape[0]
    length = natural.shape[2]

    def place(source, carry):
        for part in range(2):
            first = pl.multiple_of(order[seq, 2 * source + part] * half, half)
            grad_rows[pl.ds(first, half), :] = grad_slots[
                source, 0, part * half : (part + 1) * half, :
            ]
        return carry

    lax.fori_loop(0, sources, place, 0)
    grad_keys[...] = jnp.zeros_like(grad_keys)
    grad_values[...] = jnp.zeros_like(grad_values)

    def visit(first_row, chunks):
        rows = pl.ds(first_row, block)
        queries = natural[0, 0, rows, :] * jnp.asarray(score_scale, BF16)
        grads = grad_rows[rows, :]
        products = grads.astype(F32) * out_rows[0, rows, :].astype(F32)
        logs = log_rows[0, rows, :]
        query_sum = jnp.zeros(products.shape, F32)
        parts = zip(
            head_parts(queries, head_width),
            head_parts(grads, head_width),
            head_parts(products, head_width),
        )
        for h, (query, grad, product) in enumerate(parts):
            delta = jnp.sum(product, axis=1, keepdims=True)
            log_total = logs[:, h * head_width : h * head_width + 1]
            for first_key, keys, masked in chunks:
                span = slice(first_key, first_key + keys)
                key_block = natural[1, 0, span, :]
                scores = dot(query, key_block, ((1,), (1,)))
                probs = jnp.exp(scores - log_total)
                if masked:
                    probs = jnp.where(
                        visible_mask(first_row, block, first_key, keys), probs, 0.0
                    )
                grad_probs = dot(grad, natural[2, 0, span, :], ((1,), (1,)))
                grad_scores = (probs * (grad_probs - delta)).astype(BF16)
                grad_values[span, :] += dot(probs.astype(BF16), grad, ((0,), (0,)))
                grad_keys[span, :] += dot(grad_scores, query, ((0,), (0,)))
                query_sum = query_sum + dot(
                    grad_scores, head_parts(key_block, head_width)[h], ((1,), (0,))
                )
        grad_queries[rows, :] = query_sum * score_scale

    each_query_block(length, block, visit)

    def give(source, carry):
        for part in range(2):
            first = pl.multiple_of(order[seq, 2 * source + part] * half, half)
            to_rows = slice(part * half, (part + 1) * half)
            for kind, rows in enumerate((grad_queries, grad_keys, grad_values)):
                slot_out[source, kind, 0, to_rows, :] = rows[pl.ds(first, half), :].astype(BF16)
        return carry

    lax.fori_loop(0, sources, give, 0)


def attend_forward(qkv, order, head_width, score_scale):
    sources, kinds, seqs, rows, lanes = qkv.shape
    length = sources * rows
    block = math.gcd(length, 256)
    return pl.pallas_call(
        partial(forward_kernel, rows // 2, block, head_width, score_scale),
        grid_spec=pltpu.PrefetchScalarGridSpec(
            num_scalar_prefetch=1,
            grid=(seqs,),
            in_specs=[pl.BlockSpec((sources, 3, 1, rows, lanes), lambda s, o: (0, 0, s, 0, 0))],
            out_specs=[
                pl.BlockSpec((sources, 1, rows, lanes), lambda s, o: (0, s, 0, 0)),
                pl.BlockSpec((3, 1, length, lanes), lambda s, o: (0, s, 0, 0)),
                pl.BlockSpec((1, length, lanes), lambda s, o: (s, 0, 0)),
                pl.BlockSpec((1, length, lanes), lambda s, o: (s, 0, 0)),
            ],
        ),
        out_shape=[
            jax.ShapeDtypeStruct((sources, seqs, rows, lanes), BF16),
            jax.ShapeDtypeStruct((3, seqs, length, lanes), BF16),
            jax.ShapeDtypeStruct((seqs, length, lanes), BF16),
            jax.ShapeDtypeStruct((seqs, length, lanes), F32),
        ],
        name="attend_forward",
    )(order, qkv)


def attend_backward(natural, out_rows, log_rows, grad_slots, order, head_width, score_scale):
    sources, seqs, rows, lanes = grad_slots.shape
    length = sources * rows
    block = math.gcd(length, 256)
    return pl.pallas_call(
        partial(backward_kernel, rows // 2, block, head_width, score_scale),
        grid_spec=pltpu.PrefetchScalarGridSpec(
            num_scalar_prefetch=1,
            grid=(seqs,),
            in_specs=[
                pl.BlockSpec((3, 1, length, lanes), lambda s, o: (0, s, 0, 0)),
                pl.BlockSpec((1, length, lanes), lambda s, o: (s, 0, 0)),
                pl.BlockSpec((1, length, lanes), lambda s, o: (s, 0, 0)),
                pl.BlockSpec((sources, 1, rows, lanes), lambda s, o: (0, s, 0, 0)),
            ],
            out_specs=[
                pl.BlockSpec((sources, 3, 1, rows, lanes), lambda s, o: (0, 0, s, 0, 0)),
            ],
            scratch_shapes=[
                pltpu.VMEM((length, lanes), BF16),
                pltpu.VMEM((length, lanes), F32),
                pltpu.VMEM((length, lanes), F32),
                pltpu.VMEM((length, lanes), F32),
            ],
        ),
        out_shape=[jax.ShapeDtypeStruct((sources, 3, seqs, rows, lanes), BF16)],
        name="attend_backward",
    )(order, natural, out_rows, log_rows, grad_slots)[0]


def to_heads(rows, devices, seqs, lanes):
    tokens, width = rows.shape
    padded = jnp.pad(rows, ((0, 0), (0, devices * lanes - width)))
    return jnp.transpose(padded.reshape(seqs, tokens // seqs, devices, lanes), (2, 0, 1, 3))


def from_heads(blocks, width):
    devices, seqs, rows, lanes = blocks.shape
    joined = jnp.transpose(blocks, (1, 2, 0, 3)).reshape(seqs * rows, devices * lanes)
    return joined[:, :width]


def shards(
    ctx,
    layer_in,
    out_grad,
    block_order,
    ln1_gain,
    ln1_bias,
    w_qkv,
    qv_bias,
    w_out,
    out_bias,
    ln2_gain,
    ln2_bias,
    w_up,
    up_bias,
    w_down,
    down_bias,
):
    seqs, tok_rows, width = layer_in.shape
    tokens = seqs * tok_rows
    head_width = width // HEADS
    score_scale = 1.0 / math.sqrt(head_width)
    lanes = -(-HEADS // ctx) * head_width
    half_units = w_up.shape[1]
    half_cols = w_out.shape[1]
    half_proj = w_qkv.shape[1]
    my_dp = lax.axis_index("dp")
    my_core = lax.axis_index("ctx") % 2
    core_swap = [(i, i ^ 1) for i in range(ctx)]

    def across(x):
        return lax.ppermute(x, "dp", [(0, 1), (1, 0)])

    def after(x, *earlier):
        return lax.optimization_barrier((x,) + earlier)[0]

    def by_dp(mine, other):
        return jnp.where(my_dp == 0, mine, other), jnp.where(my_dp == 0, other, mine)

    def fetch(send):
        rows = send.shape[0] // 2
        part = across(lax.dynamic_slice_in_dim(send, my_core * rows, rows, 0))
        rest = lax.ppermute(part, "ctx", core_swap)
        low = jnp.where(my_core == 0, part, rest)
        high = jnp.where(my_core == 0, rest, part)
        return jnp.concatenate([low, high], axis=0)

    own_in = layer_in.reshape(tokens, width)
    own_out_grad = out_grad.reshape(tokens, width)
    other_in = across(own_in)
    stream = own_in.astype(F32)
    normed_one, inverse_one = normalize(stream)
    hidden_one = (normed_one * ln1_gain + ln1_bias).astype(BF16)
    hidden_one_other = (normalize(other_in.astype(F32))[0] * ln1_gain + ln1_bias).astype(BF16)
    proj_bias = jnp.concatenate([qv_bias[0], jnp.zeros_like(qv_bias[0]), qv_bias[1]])
    proj_bias = lax.dynamic_slice_in_dim(proj_bias, my_dp * half_proj, half_proj, 0)
    proj_other = (
        jnp.dot(hidden_one_other, w_qkv, preferred_element_type=F32) + proj_bias
    ).astype(BF16)
    proj_got = across(proj_other)
    proj_own = (jnp.dot(hidden_one, w_qkv, preferred_element_type=F32) + proj_bias).astype(BF16)
    low, high = by_dp(proj_own, proj_got)
    queries = low[:, :width]
    keys = jnp.concatenate([low[:, width:], high[:, : 2 * width - half_proj]], axis=1)
    values = high[:, 2 * width - half_proj :]
    send = jnp.stack([to_heads(x, ctx, seqs, lanes) for x in (queries, keys, values)], axis=1)
    qkv_heads = lax.all_to_all(send, "ctx", 0, 0, tiled=True)

    other_out_grad = across(after(own_out_grad, proj_got))
    w_out_other = fetch(after(w_out, proj_got))
    out_low, out_high = by_dp(w_out, w_out_other)
    unit_rows = w_down.shape[0] // 2
    down_mine = lax.dynamic_slice_in_dim(w_down, my_dp * unit_rows, unit_rows, 0)
    down_send = lax.dynamic_slice_in_dim(w_down, (1 - my_dp) * unit_rows, unit_rows, 0)
    down_other = fetch(after(down_send, w_out_other))
    down_low, down_high = by_dp(down_mine, down_other)

    hidden_one_all = lax.all_gather(after(hidden_one, qkv_heads), "ctx", axis=0, tiled=True)

    attended_slots, natural, out_rows, log_rows = attend_forward(
        qkv_heads, block_order, head_width, score_scale
    )
    attended = from_heads(lax.all_to_all(attended_slots, "ctx", 0, 0, tiled=True), width)

    mixed = jnp.concatenate(
        [
            jnp.dot(attended, out_low, preferred_element_type=F32),
            jnp.dot(attended, out_high, preferred_element_type=F32),
        ],
        axis=1,
    )
    residual = stream + mixed + out_bias
    normed_two, inverse_two = normalize(residual)
    hidden_two = (normed_two * ln2_gain + ln2_bias).astype(BF16)
    hidden_two_pair = jnp.concatenate([hidden_two, across(hidden_two)], axis=0)
    out_grad_pair = jnp.concatenate([own_out_grad, other_out_grad], axis=0)

    up_half = lax.dynamic_slice_in_dim(up_bias, my_dp * half_units, half_units, 0)
    grad_active = jnp.einsum(
        "td,fd->tf", out_grad_pair[:, :half_cols], down_low, preferred_element_type=F32
    ) + jnp.einsum("td,fd->tf", out_grad_pair[:, half_cols:], down_high, preferred_element_type=F32)
    pre_act = jnp.dot(hidden_two_pair, w_up, preferred_element_type=F32) + up_half
    activated_wide, gelu_slope = gelu_parts(pre_act)
    activated = activated_wide.astype(BF16)
    grad_pre = (grad_active * gelu_slope).astype(BF16)
    grad_two = jnp.einsum("tf,df->td", grad_pre, w_up, preferred_element_type=F32)
    grad_two_got = across(grad_two[tokens:].astype(BF16))
    grad_hidden_two = grad_two[:tokens] + grad_two_got.astype(F32)
    down_sum = jnp.concatenate(
        [
            jnp.dot(activated, down_low, preferred_element_type=F32),
            jnp.dot(activated, down_high, preferred_element_type=F32),
        ],
        axis=1,
    )
    down_got = across(after(down_sum[tokens:].astype(BF16), grad_two_got))
    layer_out = (residual + (down_sum[:tokens] + down_got.astype(F32)) + down_bias).astype(BF16)

    blocks = ctx // 2
    unit_block = half_units // blocks
    down_part = jnp.einsum("tf,td->fd", activated, out_grad_pair, preferred_element_type=F32)
    down_part = jnp.transpose(
        down_part.astype(BF16).reshape(blocks, unit_block, 2, half_cols), (2, 0, 1, 3)
    ).reshape(ctx, unit_block, half_cols)
    up_part = jnp.einsum("td,tf->df", hidden_two_pair, grad_pre, preferred_element_type=F32)
    up_part = jnp.transpose(
        up_part.astype(BF16).reshape(2, half_cols, blocks, unit_block), (0, 2, 1, 3)
    ).reshape(ctx, half_cols, unit_block)
    owner = [
        (d * ctx + e * blocks + j, e * ctx + d * blocks + j)
        for d in range(2)
        for e in range(2)
        for j in range(blocks)
    ]
    down_grad = lax.psum_scatter(down_part, "ctx", scatter_dimension=0, tiled=False)
    up_grad = lax.psum_scatter(up_part, "ctx", scatter_dimension=0, tiled=False)
    down_grad = lax.ppermute(down_grad, ("dp", "ctx"), owner).astype(F32)
    up_grad = lax.ppermute(up_grad, ("dp", "ctx"), owner).astype(F32)

    grad_out = own_out_grad.astype(F32)
    grad_residual = grad_out + norm_back(grad_hidden_two * ln2_gain, normed_two, inverse_two)
    grad_mixed = grad_residual.astype(BF16)
    grad_attended = (
        jnp.einsum("tb,ab->ta", grad_mixed[:, :half_cols], out_low, preferred_element_type=F32)
        + jnp.einsum("tb,ab->ta", grad_mixed[:, half_cols:], out_high, preferred_element_type=F32)
    ).astype(BF16)
    grad_slots = lax.all_to_all(
        to_heads(grad_attended, ctx, seqs, lanes), "ctx", 0, 0, tiled=True
    )
    mixed_all = lax.all_gather(after(grad_mixed, grad_slots), "ctx", axis=0, tiled=True)
    qkv_other = fetch(after(w_qkv.T, grad_two_got))
    qkv_low, qkv_high = by_dp(w_qkv.T, qkv_other)
    proj_slots = attend_backward(
        natural, out_rows, log_rows, grad_slots, block_order, head_width, score_scale
    )
    proj_back = lax.all_to_all(proj_slots, "ctx", 0, 0, tiled=True)
    grad_proj = jnp.concatenate(
        [from_heads(proj_back[:, kind], width) for kind in range(3)], axis=1
    )
    grad_hidden_one = jnp.dot(
        grad_proj[:, :half_proj], qkv_low, preferred_element_type=F32
    ) + jnp.dot(grad_proj[:, half_proj:], qkv_high, preferred_element_type=F32)
    input_grad = (
        grad_residual + norm_back(grad_hidden_one * ln1_gain, normed_one, inverse_one)
    ).astype(BF16)

    def columns(rows):
        return jnp.transpose(rows.reshape(tokens, ctx, -1), (1, 0, 2))

    proj_cols = lax.all_to_all(columns(grad_proj), "ctx", 0, 0, tiled=True)
    proj_cols = proj_cols.reshape(ctx * tokens, -1)
    attended_cols = lax.all_to_all(columns(attended), "ctx", 0, 0, tiled=True)
    attended_cols = attended_cols.reshape(ctx * tokens, -1)
    qkv_part = jnp.einsum("td,tc->dc", hidden_one_all, proj_cols, preferred_element_type=F32)
    out_part = jnp.einsum("tc,td->cd", attended_cols, mixed_all, preferred_element_type=F32)

    def keep_and_send(part, axis):
        size = part.shape[axis] // 2
        kept = lax.dynamic_slice_in_dim(part, my_dp * size, size, axis)
        sent = lax.dynamic_slice_in_dim(part, (1 - my_dp) * size, size, axis).astype(BF16)
        return kept + across(sent).astype(F32)

    qkv_grad = keep_and_send(qkv_part, 0)
    out_weight_grad = keep_and_send(out_part, 1)

    up_sums = jnp.sum(grad_pre.astype(F32), axis=0)
    none = jnp.zeros_like(up_sums)
    up_sums = jnp.concatenate(
        [jnp.where(my_dp == 0, up_sums, none), jnp.where(my_dp == 0, none, up_sums)]
    )
    proj_sums = jnp.sum(grad_proj.astype(F32), axis=0)
    sums = [
        jnp.sum(grad_hidden_one * normed_one, axis=0),
        jnp.sum(grad_hidden_one, axis=0),
        proj_sums[:width],
        proj_sums[2 * width :],
        jnp.sum(grad_mixed.astype(F32), axis=0),
        jnp.sum(grad_hidden_two * normed_two, axis=0),
        jnp.sum(grad_hidden_two, axis=0),
        jnp.sum(grad_out, axis=0),
        up_sums,
    ]
    packed = jnp.concatenate(sums)
    devices = 2 * ctx
    size = -(-packed.shape[0] // (devices * 128)) * 128
    count = packed.shape[0]
    packed = jnp.pad(packed, (0, devices * size - count)).reshape(devices, size // 128, 128)
    mine = jnp.sum(lax.all_to_all(packed, ("dp", "ctx"), 0, 0, tiled=True), axis=0)
    spread = jnp.broadcast_to(mine[None], (devices,) + mine.shape)
    totals = lax.all_to_all(spread, ("dp", "ctx"), 0, 0, tiled=True).reshape(-1)
    pieces = []
    first = 0
    for item in sums:
        pieces.append(totals[first : first + item.shape[0]])
        first += item.shape[0]

    return (
        layer_out.reshape(layer_in.shape),
        input_grad.reshape(layer_in.shape),
        pieces[0],
        pieces[1],
        qkv_grad,
        jnp.stack([pieces[2], pieces[3]]),
        out_weight_grad,
        pieces[4],
        pieces[5],
        pieces[6],
        up_grad,
        pieces[8],
        down_grad,
        pieces[7],
    )


def solution(mesh):
    placed = (
        P("dp", "ctx", None),
        P("dp", "ctx", None),
        P("dp", None),
        P(),
        P(),
        P(None, "dp"),
        P(),
        P(None, "dp"),
        P(),
        P(),
        P(),
        P(None, "dp"),
        P(),
        P(None, "dp"),
        P(),
    )
    return jax.shard_map(
        partial(shards, mesh.shape["ctx"]),
        mesh=mesh,
        in_specs=placed,
        out_specs=(
            P("dp", "ctx", None),
            P("dp", "ctx", None),
            P(),
            P(),
            P("dp", "ctx"),
            P(),
            P("ctx", "dp"),
            P(),
            P(),
            P(),
            P("dp", "ctx"),
            P(),
            P("ctx", "dp"),
            P(),
        ),
        check_vma=False,
    )
```

time: 1650 us -> 803 us (0.49)
  waiting for transfers between devices: 932 us -> 287 us
  matrix products: 199 us -> 103 us
  local copies, waits for them, and re-layouts: 279 us -> 210 us
  blocking collectives: 109 us -> 43.2 us
  starting transfers between devices: 21.3 us -> 75.7 us
  other arithmetic: 61.4 us -> 30.9 us
  Pallas kernels: 0 us -> 27 us
  loops' own time: 17.1 us -> 0 us
    all_gather x12 -> x2, waiting for transfers between devices: 760 us -> 0.02 us  [the longest x1 0.02 us: shards(): lax.all_gather(after(grad_mixed, grad_slots), 'ctx', axis=0, tiled=True)]
    ppermute x0 -> x16, waiting for transfers between devices: none -> 217 us  [the longest x11 160 us: across(): return lax.ppermute(x, 'dp', [(0, 1), (1, 0)])]
    psum x1 -> x0, waiting for transfers between devices: 130 us -> none  [shards(): lax.psum((jnp.sum(grad_hidden_one * normed_one, axis=0), jnp.sum(grad_hid...]
    reshape x7 -> x18, local copies, waits for them, and re-layouts: 13.4 us -> 130 us  [the longest x2 58.8 us: shards(): down_part.astype(BF16).reshape(blocks, unit_block, 2, half_cols)]
    dot_general x40 -> x18, matrix products: 199 us -> 103 us  [the longest x1 9.03 us: shards(): jnp.einsum('td,fd->tf', out_grad_pair[:, :half_cols], down_low, preferred...]
    all_to_all x3 -> x7, waiting for transfers between devices: 5.92 us -> 70.4 us  [the longest x1 30.7 us: shards(): proj_back = lax.all_to_all(proj_slots, 'ctx', 0, 0, tiled=True)]
    all_gather x2 -> x0, blocking collectives: 53.5 us -> none  [the longest x1 27.6 us: shards(): lax.all_gather(outgoing[3], 'ctx', axis=1, tiled=True)]
    while x112 -> x0, local copies, waits for them, and re-layouts: 52.1 us -> none  [the longest x6 27 us: shards(): lax.scan(key_visit_block, accumulated, (pieces[0], pieces[1], pieces[2],...]
  transfers between devices with their start and end apart: 20 -> 27, of which waited for: 10 -> 17; matrix products, arithmetic and copies ran while one was open for 30% -> 40% of each run, Pallas kernels for 0% -> 3%
where the time goes in v1:
time: 803 us; the launch traced here: 792 us
  waiting for transfers between devices  287 us (36%)
  local copies, waits for them, and re-layouts  210 us (26%)
  matrix products  103 us (13%)
  starting transfers between devices  75.7 us (9%)
  blocking collectives  43.2 us (5%)
  other arithmetic  30.9 us (4%)
  Pallas kernels  27 us (3%)
  between operations  15.2 us (2%)
    ppermute x11, waiting for transfers between devices, across(): return lax.ppermute(x, 'dp', [(0, 1), (1, 0)])  160 us
    reshape x2, local copies, waits for them, and re-layouts, shards(): down_part.astype(BF16).reshape(blocks, unit_block, 2, half_cols)  58.8 us
    reshape x2, local copies, waits for them, and re-layouts, shards(): up_part.astype(BF16).reshape(2, half_cols, blocks, unit_block)  58.8 us
    all_to_all x1, blocking collectives, shards(): qkv_heads = lax.all_to_all(send, 'ctx', 0, 0, tiled=True)  43.2 us
    ppermute x1, waiting for transfers between devices, shards(): down_grad = lax.ppermute(down_grad, ('dp', 'ctx'), owner).astype(F32)  39.4 us
    all_to_all x1, waiting for transfers between devices, shards(): proj_back = lax.all_to_all(proj_slots, 'ctx', 0, 0, tiled=True)  30.7 us
    unnamed x97, local copies, waits for them, and re-layouts  21.4 us
    all_to_all x1, waiting for transfers between devices, shards(): lax.all_to_all(attended_slots, 'ctx', 0, 0, tiled=True)  16.1 us
  transfers between devices with their start and end apart: 27, of which 17 were waited for; matrix products, arithmetic and copies ran while one was open for 40% of the time, Pallas kernels for 3%

profile of v1, /device:TPU:25, one launch (start us, length us, event | category | flops | bytes accessed | tf_op | source)
XLA Modules:
  0.0 791.8 jit_solution(15416050547801579963)
XLA Ops:
  13.3 5.6 collective-permute-done
  19.4 6.9 fusion.9
  28.2 12.0 %collective-permute-done.1 = bf16[128,2400]{0,1:T(8,128)(2,1)S(1)} collective-permute-done((bf16[128,2400]{0,1:T(8,128)(2,1)S(1)}, bf16[128,2400]{0,1:T(8,128)(2,1)S(1)}, u32[]{:S(2)}, u32[]{:S(2)}) %collective-permute-start.1) | collective-permute-done | bytes 614432 | tf_op jit(solution)/shard_map/ppermute | solution.py:331
  40.2 6.4 broadcast_select_fusion.15
  52.4 43.2 %all_to_all.40.qkv = bf16[16,3,2,64,128]{4,3,2,1,0:T(8,128)(2,1)} all-to-all(bf16[16,3,2,64,128]{4,3,2,1,0:T(8,128)(2,1)S(1)} %pad_maximum_fusion.5), channel_id=1, replica_groups=mesh['dp'=2,'ctx'=16] {'ctx'}, dimensions={0} | all-to-all | bytes 3145728 | tf_op jit(solution)/shard_map/all_to_all | solution.py:366
  99.0 32.0 %collective-permute-done.2 = bf16[800,800]{0,1:T(8,128)(2,1)S(1)} collective-permute-done((bf16[800,800]{0,1:T(8,128)(2,1)S(1)}, bf16[800,800]{0,1:T(8,128)(2,1)S(1)}, u32[]{:S(2)}, u32[]{:S(2)}) %collective-permute-start.2) | collective-permute-done | bytes 1280032 | tf_op jit(solution)/shard_map/ppermute | solution.py:331
  131.6 11.4 %attend_forward.1 = (bf16[16,2,64,128]{3,2,1,0:T(8,128)(2,1)}, bf16[3,2,1024,128]{3,2,1,0:T(8,128)(2,1)}, bf16[2,1024,128]{2,1,0:T(8,128)(2,1)}, f32[2,1024,128]{2,1,0:T(8,128)}) custom-call(s32[2,32]{1,0:T(2,128)} %order.3, bf16[16,3,2,64,128]{4,3,2,1,0:T(8,128)(2,1)} %all_to_all.40.qkv), custom_call_target="tpu_custom_call" | custom-call | tf_op jit(solution)/shard_map/attend_forward/pallas_call | solution.py:235
  143.0 5.9 all-to-all-start.1
  153.0 16.1 %all-to-all-done.1 = bf16[16,2,64,128]{3,2,1,0:T(8,128)(2,1)S(1)} async-done(((bf16[16,2,64,128]{3,2,1,0:T(8,128)(2,1)}), bf16[16,2,64,128]{3,2,1,0:T(8,128)(2,1)S(1)}, u32[]{:S(2)}, u32[]{:S(2)}) %all-to-all-start.1) | async-done | bytes 524320 | tf_op jit(solution)/shard_map/all_to_all | solution.py:382
  179.7 9.1 %collective-permute-done.4 = bf16[128,1600]{0,1:T(8,128)(2,1)S(1)} collective-permute-done((bf16[128,1600]{0,1:T(8,128)(2,1)S(1)}, bf16[128,1600]{0,1:T(8,128)(2,1)S(1)}, u32[]{:S(2)}, u32[]{:S(2)}) %collective-permute-start.4) | collective-permute-done | bytes 409632 | tf_op jit(solution)/shard_map/ppermute | solution.py:331
  188.8 6.2 convolution_add_fusion.1
  197.9 7.0 convolution_convert_fusion.1
  204.9 33.5 %reshape.235 = bf16[8,400,2,800]{1,0,3,2:T(8,128)(2,1)} reshape(bf16[3200,1600]{0,1:T(8,128)(2,1)} %convolution_convert_fusion.1) | data formatting | bytes 20480000 | tf_op jit(solution)/shard_map/reshape | solution.py:422
  238.4 25.4 %copy.126 = bf16[8,400,2,800]{3,2,1,0:T(2,128)(2,1)} copy(bf16[8,400,2,800]{1,0,3,2:T(8,128)(2,1)} %reshape.235) | data formatting | bytes 20480000 | tf_op jit(solution)/shard_map/reshape | solution.py:422
  263.8 11.9 %copy.116 = bf16[2,8,400,800]{3,2,1,0:T(8,128)(2,1)} copy(bf16[2,8,400,800]{3,0,2,1:T(2,128)(2,1)} %bitcast.109) | data formatting | bytes 20480000 | tf_op jit(solution)/shard_map/transpose | solution.py:421
  281.3 57.0 %collective-permute-done.5 = bf16[1600,800]{0,1:T(8,128)(2,1)S(1)} collective-permute-done((bf16[1600,800]{0,1:T(8,128)(2,1)S(1)}, bf16[1600,800]{0,1:T(8,128)(2,1)S(1)}, u32[]{:S(2)}, u32[]{:S(2)}) %collective-permute-start.5) | collective-permute-done | bytes 2560032 | tf_op jit(solution)/shard_map/ppermute | solution.py:331
  340.2 4.6 collective-permute-done.6
  349.9 9.0 %convert_reduce_fusion = (f32[3200]{0:T(1024)S(1)}, bf16[256,3200]{1,0:T(8,128)(2,1)S(1)}) fusion(f32[256,3200]{1,0:T(8,128)S(1)} %copy-done.8, f32[256,3200]{1,0:T(8,128)} %fusion.59, pred[]{:T(512)S(6)} %eq.6, bf16[6400,800]{0,1:T(8,128)(2,1)S(1)} %bitcast.123, s32[]{:T(128)S(6)} %select_n.140, bf16[1600,800]{0,1:T(8,128)(2,1)S(1)} %get-tuple-element.68, ...), kind=kOutput, calls=%fused_computation.29 | convolution fusion | flops 1342358400 | bytes 19501572 | tf_op jit(solution)/shard_map/td,fd->tf/dot_general | solution.py:398
  360.1 5.4 convolution_convert_fusion
  365.5 33.5 %reshape.234 = bf16[2,800,8,400]{3,2,1,0:T(8,128)(2,1)} reshape(bf16[1600,3200]{1,0:T(8,128)(2,1)} %convolution_convert_fusion) | data formatting | bytes 20480000 | tf_op jit(solution)/shard_map/reshape | solution.py:426
  398.9 25.4 %copy.125 = bf16[2,800,8,400]{1,0,3,2:T(2,128)(2,1)} copy(bf16[2,800,8,400]{3,2,1,0:T(8,128)(2,1)} %reshape.234) | data formatting | bytes 20480000 | tf_op jit(solution)/shard_map/reshape | solution.py:426
  424.3 12.0 %copy.114 = bf16[2,8,800,400]{2,3,1,0:T(8,128)(2,1)} copy(bf16[2,8,800,400]{2,0,3,1:T(2,128)(2,1)} %bitcast.110) | data formatting | bytes 20480000 | tf_op jit(solution)/shard_map/transpose | solution.py:425
  436.3 6.3 fusion.87
  445.3 9.2 %collective-permute-done.8 = bf16[128,1600]{0,1:T(8,128)(2,1)S(1)} collective-permute-done((bf16[128,1600]{0,1:T(8,128)(2,1)S(1)}, bf16[128,1600]{0,1:T(8,128)(2,1)S(1)}, u32[]{:S(2)}, u32[]{:S(2)}) %collective-permute-start.8) | collective-permute-done | bytes 409632 | tf_op jit(solution)/shard_map/ppermute | solution.py:331
  467.8 7.9 all-to-all-start.2
  475.7 11.8 %copy.106 = bf16[1600,2400]{0,1:T(8,128)(2,1)} copy(bf16[1600,2400]{1,0:T(8,128)(2,1)} %param.20) | data formatting | bytes 15360000 | tf_op args[5]
  487.5 10.0 %all-to-all-done.2.grad_slots = bf16[16,2,64,128]{3,2,1,0:T(8,128)(2,1)S(1)} async-done(((bf16[16,2,64,128]{3,2,1,0:T(8,128)(2,1)}), bf16[16,2,64,128]{3,2,1,0:T(8,128)(2,1)S(1)}, u32[]{:S(2)}, u32[]{:S(2)}) %all-to-all-start.2) | async-done | bytes 524320 | tf_op jit(solution)/shard_map/all_to_all | solution.py:446
  498.3 15.6 %attend_backward.1 = bf16[16,3,2,64,128]{4,3,2,1,0:T(8,128)(2,1)} custom-call(s32[2,32]{1,0:T(2,128)} %order.3, bf16[3,2,1024,128]{3,2,1,0:T(8,128)(2,1)} %get-tuple-element.30.natural, bf16[2,1024,128]{2,1,0:T(8,128)(2,1)} %get-tuple-element.31.out_rows, f32[2,1024,128]{2,1,0:T(8,128)} %get-tuple-element.32.log_rows, bf16[16,2,64,128]{3,2,1,0:T(8,128)(2,1)} %copy-done.15), custom_call_target="tpu_custom_call" | custom-call | tf_op jit(solution)/shard_map/attend_backward/pallas_call | solution.py:262
  513.9 11.3 %all-to-all-start.3 = ((bf16[16,3,2,64,128]{4,3,2,1,0:T(8,128)(2,1)}), bf16[16,3,2,64,128]{4,3,2,1,0:T(8,128)(2,1)}, u32[]{:S(2)}, u32[]{:S(2)}) async-start(bf16[16,3,2,64,128]{4,3,2,1,0:T(8,128)(2,1)} %attend_backward.1), calls=%async_computation.3 | async-start | bytes 3145728 | tf_op jit(solution)/shard_map/all_to_all | solution.py:455
  525.4 4.6 constant_dynamic-slice_fusion
  532.4 30.7 %all-to-all-done.3 = bf16[16,3,2,64,128]{4,3,2,1,0:T(8,128)(2,1)} async-done(((bf16[16,3,2,64,128]{4,3,2,1,0:T(8,128)(2,1)}), bf16[16,3,2,64,128]{4,3,2,1,0:T(8,128)(2,1)}, u32[]{:S(2)}, u32[]{:S(2)}) %all-to-all-start.3) | async-done | bytes 1572896 | tf_op jit(solution)/shard_map/all_to_all | solution.py:455
  563.1 8.1 %all-to-all-start.7 = ((bf16[16,128,100]{1,2,0:T(8,128)(2,1)}), bf16[16,128,100]{1,2,0:T(8,128)(2,1)}, u32[]{:S(2)}, u32[]{:S(2)}) async-start(bf16[16,128,100]{1,2,0:T(8,128)(2,1)} %bitcast.22), calls=%async_computation.7 | async-start | bytes 851968 | tf_op jit(solution)/shard_map/all_to_all | solution.py:471
  582.9 7.6 all-to-all-done.7
  590.5 7.7 all-to-all-start.6
  598.2 19.5 %collective-permute-done.10 = bf16[1200,1600]{1,0:T(8,128)(2,1)} collective-permute-done((bf16[1200,1600]{1,0:T(8,128)(2,1)}, bf16[1200,1600]{1,0:T(8,128)(2,1)}, u32[]{:S(2)}, u32[]{:S(2)}) %collective-permute-start.10) | collective-permute-done | bytes 3840032 | tf_op jit(solution)/shard_map/ppermute | solution.py:331
  622.1 8.5 %fusion.82 = f32[256,800]{0,1:T(8,128)S(1)} fusion(pred[]{:T(512)S(6)} %eq.6, bf16[6400,800]{0,1:T(8,128)(2,1)} %param.28, s32[]{:T(128)S(6)} %select_n.140, bf16[1600,800]{0,1:T(8,128)(2,1)} %copy-done.12, bf16[1600,800]{0,1:T(8,128)(2,1)} %copy-done.10, f32[256,3200]{1,0:T(8,128)} %copy-done.7), kind=kOutput, calls=%fused_computation.169 | convolution fusion | flops 1330892800 | bytes 14540805 | tf_op jit(solution)/shard_map/dot_general | solution.py:411
  630.6 5.7 fusion.81
  641.3 5.6 fusion.88
  648.9 12.4 %collective-permute-done.12 = bf16[800,300]{0,1:T(8,128)(2,1)S(1)} collective-permute-done((bf16[800,300]{0,1:T(8,128)(2,1)S(1)}, bf16[800,300]{0,1:T(8,128)(2,1)S(1)}, u32[]{:S(2)}, u32[]{:S(2)}) %collective-permute-start.12) | collective-permute-done | bytes 480032 | tf_op jit(solution)/shard_map/ppermute | solution.py:331
  662.6 6.9 broadcast_select_fusion.3
  670.7 7.6 fusion
  678.4 8.4 %fusion.45 = (f32[1600]{0:T(1024)S(1)}, f32[128]{0:T(128)S(1)}, f32[128]{0:T(128)S(1)}, f32[1600]{0:T(1024)S(1)}, f32[128,1600]{0,1:T(8,128)}) fusion(bf16[128,1600]{0,1:T(8,128)(2,1)S(1)} %copy-done.2, f32[128]{0:T(128)S(1)} %copy-done.38, f32[128]{0:T(128)S(1)} %copy-done.36, f32[1600]{0:T(1024)S(1)} %copy-done.29, f32[128,1600]{0,1:T(8,128)S(1)} %fusion, ...), kind=kOutput, calls=%fused_computation.89 | convolution fusion | flops 1005718144 | bytes 18248448 | tf_op jit(solution)/shard_map/dot_general | solution.py:459
  687.6 8.0 %all-to-all-start.4 = ((f32[32,5,128]{2,1,0:T(8,128)}), f32[32,5,128]{2,1,0:T(8,128)S(1)}, u32[]{:S(2)}, u32[]{:S(2)}) async-start(f32[32,5,128]{2,1,0:T(8,128)} %reshape.220), calls=%async_computation.4 | async-start | bytes 262144 | tf_op jit(solution)/shard_map/all_to_all | solution.py:507
  695.6 5.9 all-to-all-done.4
  702.2 4.9 all-to-all-start.5
  722.9 5.2 fusion.89
  728.9 39.4 %collective-permute-done.15 = bf16[400,800]{1,0:T(8,128)(2,1)S(1)} collective-permute-done((bf16[400,800]{1,0:T(8,128)(2,1)}, bf16[400,800]{1,0:T(8,128)(2,1)S(1)}, u32[]{:S(2)}, u32[]{:S(2)}) %collective-permute-start.15) | collective-permute-done | bytes 640032 | tf_op jit(solution)/shard_map/ppermute | solution.py:436
  770.4 13.3 %collective-permute-done.14 = bf16[800,400]{0,1:T(8,128)(2,1)S(1)} collective-permute-done((bf16[800,400]{0,1:T(8,128)(2,1)}, bf16[800,400]{0,1:T(8,128)(2,1)S(1)}, u32[]{:S(2)}, u32[]{:S(2)}) %collective-permute-start.14) | collective-permute-done | bytes 640032 | tf_op jit(solution)/shard_map/ppermute | solution.py:437
  (235 shorter events, 115.0 us)
Async XLA Ops:
  7.2 634.1 %all-gather.3.cloned.1.call-start = ((), (), s32[]{:S(2)}) async-start(), calls=%async_computation.10 | async-start | bytes 6963200 | tf_op jit(solution)/shard_map/all_gather | solution.py:377
  8.5 167.9 %copy-start.1 = (bf16[128,1600]{0,1:T(8,128)(2,1)}, bf16[128,1600]{0,1:T(8,128)(2,1)S(1)}, u32[]{:S(2)}) copy-start(bf16[128,1600]{0,1:T(8,128)(2,1)S(1)} %copy.89) | copy-start | bytes 1228804
  8.5 10.4 %collective-permute-start = (bf16[128,1600]{0,1:T(8,128)(2,1)S(1)}, bf16[128,1600]{0,1:T(8,128)(2,1)S(1)}, u32[]{:S(2)}, u32[]{:S(2)}) collective-permute-start(bf16[128,1600]{0,1:T(8,128)(2,1)S(1)} %copy.89), channel_id=1, source_target_pairs={{0,16},{16,0},{1,17},{17,1},{2,18},{18,2},{3,19},{19,3},{4,20},{20... | collective-permute-start | bytes 1228808 | tf_op jit(solution)/shard_map/ppermute | solution.py:331
  11.0 16.6 %copy-start.35 = (f32[128]{0:T(128)}, f32[128]{0:T(128)S(1)}, u32[]{:S(2)}) copy-start(f32[128]{0:T(128)S(1)} %div.35) | copy-start | bytes 1540
  19.4 8.3 %copy-start.28 = (f32[1600]{0:T(1024)S(1)}, f32[1600]{0:T(1024)}, u32[]{:S(2)}) copy-start(f32[1600]{0:T(1024)} %param.18) | copy-start | bytes 19204
  19.4 8.3 %copy-start.31 = (f32[1600]{0:T(1024)S(1)}, f32[1600]{0:T(1024)}, u32[]{:S(2)}) copy-start(f32[1600]{0:T(1024)} %param.19) | copy-start | bytes 19204
  26.3 13.9 %collective-permute-start.1 = (bf16[128,2400]{0,1:T(8,128)(2,1)S(1)}, bf16[128,2400]{0,1:T(8,128)(2,1)S(1)}, u32[]{:S(2)}, u32[]{:S(2)}) collective-permute-start(bf16[128,2400]{0,1:T(8,128)(2,1)S(1)} %fusion.9), channel_id=1, source_target_pairs={{0,16},{16,0},{1,17},{17,1},{2,18},{18,2},{3,19},{19,3},{4,20},{20... | collective-permute-start | bytes 1843208 | tf_op jit(solution)/shard_map/ppermute | solution.py:331
  27.7 19.0 %copy-start.37 = (f32[128]{0:T(128)}, f32[128]{0:T(128)S(1)}, u32[]{:S(2)}) copy-start(f32[128]{0:T(128)S(1)} %rsqrt.31) | copy-start | bytes 1540
  28.2 18.5 %copy-start.3 = (bf16[128,1600]{0,1:T(8,128)(2,1)}, bf16[128,1600]{0,1:T(8,128)(2,1)S(1)}, u32[]{:S(2)}) copy-start(bf16[128,1600]{0,1:T(8,128)(2,1)S(1)} %fusion.39) | copy-start | bytes 1228804
  28.2 19.3 %copy-start.34 = (pred[2048]{0:T(1024)(128)(4,1)S(1)}, pred[2048]{0:T(1024)(128)(4,1)}, u32[]{:S(2)}) copy-start(pred[2048]{0:T(1024)(128)(4,1)} %constant.23.clone.1) | copy-start | bytes 6148
  97.7 33.3 %collective-permute-start.2 = (bf16[800,800]{0,1:T(8,128)(2,1)S(1)}, bf16[800,800]{0,1:T(8,128)(2,1)S(1)}, u32[]{:S(2)}, u32[]{:S(2)}) collective-permute-start(bf16[800,800]{0,1:T(8,128)(2,1)S(1)} %constant_dynamic-slice_fusion.3), channel_id=1, source_target_pairs={{0,16},{16,0},{1,17},{17,1},{2,18},{18,2},{3,19},{19,3},{4,20},{20... | collective-permute-start | bytes 3840008 | tf_op jit(solution)/shard_map/ppermute | solution.py:331
  131.0 18.0 %collective-permute-start.3 = (bf16[800,800]{0,1:T(8,128)(2,1)S(1)}, bf16[800,800]{0,1:T(8,128)(2,1)}, u32[]{:S(2)}, u32[]{:S(2)}) collective-permute-start(bf16[800,800]{0,1:T(8,128)(2,1)S(1)} %collective-permute-done.2), channel_id=1, source_target_pairs={{0,1},{1,0},{2,3},{3,2},{4,5},{5,4},{6,7},{7,6},{8,9},{9,8},{10,11... | collective-permute-start | bytes 3840008 | tf_op jit(solution)/shard_map/ppermute | solution.py:342
  143.0 26.0 %all-to-all-start.1 = ((bf16[16,2,64,128]{3,2,1,0:T(8,128)(2,1)}), bf16[16,2,64,128]{3,2,1,0:T(8,128)(2,1)S(1)}, u32[]{:S(2)}, u32[]{:S(2)}) async-start(bf16[16,2,64,128]{3,2,1,0:T(8,128)(2,1)} %get-tuple-element.25), calls=%async_computation.1 | async-start | bytes 1048576 | tf_op jit(solution)/shard_map/all_to_all | solution.py:382
  149.0 566.8 %reduce-scatter.5.cloned.1.call-start = ((), (), s32[]{:S(2)}) async-start(), calls=%async_computation.13 | async-start | bytes 12185600 | tf_op jit(solution)/shard_map/reduce_scatter | solution.py:434
  178.1 10.7 %collective-permute-start.4 = (bf16[128,1600]{0,1:T(8,128)(2,1)S(1)}, bf16[128,1600]{0,1:T(8,128)(2,1)S(1)}, u32[]{:S(2)}, u32[]{:S(2)}) collective-permute-start(bf16[128,1600]{0,1:T(8,128)(2,1)S(1)} %get-tuple-element.63), channel_id=1, source_target_pairs={{0,16},{16,0},{1,17},{17,1},{2,18},{18,2},{3,19},{19,3},{4,20},{20... | collective-permute-start | bytes 1228808 | tf_op jit(solution)/shard_map/ppermute | solution.py:331
  179.5 18.5 %collective-permute-start.7 = (bf16[128,1600]{1,0:T(8,128)(2,1)S(1)}, bf16[128,1600]{1,0:T(8,128)(2,1)S(1)}, u32[]{:S(2)}, u32[]{:S(2)}) collective-permute-start(bf16[128,1600]{1,0:T(8,128)(2,1)S(1)} %bitcast.139), channel_id=1, source_target_pairs={{0,16},{16,0},{1,17},{17,1},{2,18},{18,2},{3,19},{19,3},{4,20},{20... | collective-permute-start | bytes 1228808 | tf_op jit(solution)/shard_map/ppermute | solution.py:331
  275.7 443.0 %reduce-scatter.3.cloned.1.call-start = ((), (), s32[]{:S(2)}) async-start(), calls=%async_computation.12 | async-start | bytes 12185600 | tf_op jit(solution)/shard_map/reduce_scatter | solution.py:435
  275.8 69.6 %slice-start.2 = ((s8[10240000]{0:T(1024)(128)(4,1)}), s8[4194304]{0:T(1024)(128)(4,1)S(1)}, s32[]{:S(2)}) async-start(s8[10240000]{0:T(1024)(128)(4,1)} %bitcast.122), calls=%async_computation.16 | async-start | bytes 8388608
  275.8 69.6 %slice-start.3 = ((s8[10240000]{0:T(1024)(128)(4,1)}), s8[4194304]{0:T(1024)(128)(4,1)S(1)}, s32[]{:S(2)}) async-start(s8[10240000]{0:T(1024)(128)(4,1)} %bitcast.122), calls=%async_computation.17 | async-start | bytes 8388608
  280.0 65.4 %slice-start.4 = ((s8[10240000]{0:T(1024)(128)(4,1)}), s8[1851392]{0:T(1024)(128)(4,1)S(1)}, s32[]{:S(2)}) async-start(s8[10240000]{0:T(1024)(128)(4,1)} %bitcast.122), calls=%async_computation.18 | async-start | bytes 3702784
  280.0 58.2 %collective-permute-start.5 = (bf16[1600,800]{0,1:T(8,128)(2,1)S(1)}, bf16[1600,800]{0,1:T(8,128)(2,1)S(1)}, u32[]{:S(2)}, u32[]{:S(2)}) collective-permute-start(bf16[1600,800]{0,1:T(8,128)(2,1)S(1)} %constant_dynamic-slice_fusion.1), channel_id=1, source_target_pairs={{0,16},{16,0},{1,17},{17,1},{2,18},{18,2},{3,19},{19,3},{4,20},{20... | collective-permute-start | bytes 7680008 | tf_op jit(solution)/shard_map/ppermute | solution.py:331
  338.3 6.6 collective-permute-start.6
  443.9 10.6 %collective-permute-start.8 = (bf16[128,1600]{0,1:T(8,128)(2,1)S(1)}, bf16[128,1600]{0,1:T(8,128)(2,1)S(1)}, u32[]{:S(2)}, u32[]{:S(2)}) collective-permute-start(bf16[128,1600]{0,1:T(8,128)(2,1)S(1)} %slice.223), channel_id=1, source_target_pairs={{0,16},{16,0},{1,17},{17,1},{2,18},{18,2},{3,19},{19,3},{4,20},{20... | collective-permute-start | bytes 1228808 | tf_op jit(solution)/shard_map/ppermute | solution.py:331
  467.8 29.7 %all-to-all-start.2 = ((bf16[16,2,64,128]{3,2,1,0:T(8,128)(2,1)}), bf16[16,2,64,128]{3,2,1,0:T(8,128)(2,1)S(1)}, u32[]{:S(2)}, u32[]{:S(2)}) async-start(bf16[16,2,64,128]{3,2,1,0:T(8,128)(2,1)} %bitcast.124), calls=%async_computation.2 | async-start | bytes 1048576 | tf_op jit(solution)/shard_map/all_to_all | solution.py:446
  513.9 49.2 %all-to-all-start.3 = ((bf16[16,3,2,64,128]{4,3,2,1,0:T(8,128)(2,1)}), bf16[16,3,2,64,128]{4,3,2,1,0:T(8,128)(2,1)}, u32[]{:S(2)}, u32[]{:S(2)}) async-start(bf16[16,3,2,64,128]{4,3,2,1,0:T(8,128)(2,1)} %attend_backward.1), calls=%async_computation.3 | async-start | bytes 3145728 | tf_op jit(solution)/shard_map/all_to_all | solution.py:455
  525.2 197.7 %all-gather.5.cloned.1.call-start = ((), (), s32[]{:S(2)}) async-start(), calls=%async_computation.11 | async-start | bytes 6963200 | tf_op jit(solution)/shard_map/all_gather | solution.py:449
  530.0 87.7 %collective-permute-start.10 = (bf16[1200,1600]{1,0:T(8,128)(2,1)}, bf16[1200,1600]{1,0:T(8,128)(2,1)}, u32[]{:S(2)}, u32[]{:S(2)}) collective-permute-start(bf16[1200,1600]{1,0:T(8,128)(2,1)} %constant_dynamic-slice_fusion), channel_id=1, source_target_pairs={{0,16},{16,0},{1,17},{17,1},{2,18},{18,2},{3,19},{19,3},{4,20},{20... | collective-permute-start | bytes 11520008 | tf_op jit(solution)/shard_map/ppermute | solution.py:331
  563.1 27.4 %all-to-all-start.7 = ((bf16[16,128,100]{1,2,0:T(8,128)(2,1)}), bf16[16,128,100]{1,2,0:T(8,128)(2,1)}, u32[]{:S(2)}, u32[]{:S(2)}) async-start(bf16[16,128,100]{1,2,0:T(8,128)(2,1)} %bitcast.22), calls=%async_computation.7 | async-start | bytes 851968 | tf_op jit(solution)/shard_map/all_to_all | solution.py:471
  590.5 47.6 %all-to-all-start.6 = ((bf16[16,128,300]{1,2,0:T(8,128)(2,1)}), bf16[16,128,300]{1,2,0:T(8,128)(2,1)}, u32[]{:S(2)}, u32[]{:S(2)}) async-start(bf16[16,128,300]{1,2,0:T(8,128)(2,1)} %bitcast.115), calls=%async_computation.6 | async-start | bytes 2490368 | tf_op jit(solution)/shard_map/all_to_all | solution.py:469
  617.8 44.9 %collective-permute-start.11 = (bf16[1200,1600]{1,0:T(8,128)(2,1)}, bf16[1200,1600]{1,0:T(8,128)(2,1)}, u32[]{:S(2)}, u32[]{:S(2)}) collective-permute-start(bf16[1200,1600]{1,0:T(8,128)(2,1)} %collective-permute-done.10), channel_id=1, source_target_pairs={{0,1},{1,0},{2,3},{3,2},{4,5},{5,4},{6,7},{7,6},{8,9},{9,8},{10,11... | collective-permute-start | bytes 11520008 | tf_op jit(solution)/shard_map/ppermute | solution.py:342
  622.1 8.5 %copy-start.9 = (f32[256,3200]{1,0:T(8,128)S(1)}, f32[256,3200]{1,0:T(8,128)}, u32[]{:S(2)}) copy-start(f32[256,3200]{1,0:T(8,128)} %copy-done.7) | copy-start | bytes 9830404
  622.1 8.5 %copy-start.11 = (bf16[1600,800]{0,1:T(8,128)(2,1)S(1)}, bf16[1600,800]{0,1:T(8,128)(2,1)}, u32[]{:S(2)}) copy-start(bf16[1600,800]{0,1:T(8,128)(2,1)} %copy-done.10) | copy-start | bytes 7680004
  622.1 8.5 %copy-start.13 = (bf16[1600,800]{0,1:T(8,128)(2,1)S(1)}, bf16[1600,800]{0,1:T(8,128)(2,1)}, u32[]{:S(2)}) copy-start(bf16[1600,800]{0,1:T(8,128)(2,1)} %copy-done.12) | copy-start | bytes 7680004
  647.1 14.2 %collective-permute-start.12 = (bf16[800,300]{0,1:T(8,128)(2,1)S(1)}, bf16[800,300]{0,1:T(8,128)(2,1)S(1)}, u32[]{:S(2)}, u32[]{:S(2)}) collective-permute-start(bf16[800,300]{0,1:T(8,128)(2,1)S(1)} %dynamic-slice_convert_fusion), channel_id=1, source_target_pairs={{0,16},{16,0},{1,17},{17,1},{2,18},{18,2},{3,19},{19,3},{4,20},{20... | collective-permute-start | bytes 1440008 | tf_op jit(solution)/shard_map/ppermute | solution.py:331
  648.4 58.7 %collective-permute-start.9 = (bf16[128,1600]{0,1:T(8,128)(2,1)}, bf16[128,1600]{0,1:T(8,128)(2,1)}, u32[]{:S(2)}, u32[]{:S(2)}) collective-permute-start(bf16[128,1600]{0,1:T(8,128)(2,1)} %fusion.52), channel_id=1, source_target_pairs={{0,16},{16,0},{1,17},{17,1},{2,18},{18,2},{3,19},{19,3},{4,20},{20... | collective-permute-start | bytes 1228808 | tf_op jit(solution)/shard_map/ppermute | solution.py:331
  661.3 8.3 %slice-start = ((s8[7987200]{0:T(1024)(128)(4,1)}), s8[4194304]{0:T(1024)(128)(4,1)S(1)}, s32[]{:S(2)}) async-start(s8[7987200]{0:T(1024)(128)(4,1)} %bitcast.112), calls=%async_computation.14 | async-start | bytes 8388608
  662.6 7.8 copy-start.19
  662.6 8.0 %copy-start.20 = (bf16[128,1600]{1,0:T(8,128)(2,1)S(1)}, bf16[128,1600]{1,0:T(8,128)(2,1)}, u32[]{:S(2)}) copy-start(bf16[128,1600]{1,0:T(8,128)(2,1)} %slice.165) | copy-start | bytes 1228804
  670.7 7.7 copy-start.29
  670.7 7.7 copy-start.36
  670.7 7.7 copy-start.38
  678.4 28.7 %copy-start.5 = (f32[256,800]{0,1:T(8,128)S(1)}, f32[256,800]{0,1:T(8,128)}, u32[]{:S(2)}) copy-start(f32[256,800]{0,1:T(8,128)} %copy-done.4) | copy-start | bytes 2457604
  678.4 28.7 %copy-start.33 = (f32[1600]{0:T(1024)S(1)}, f32[1600]{0:T(1024)}, u32[]{:S(2)}) copy-start(f32[1600]{0:T(1024)} %param.29) | copy-start | bytes 19204
  687.6 13.9 %all-to-all-start.4 = ((f32[32,5,128]{2,1,0:T(8,128)}), f32[32,5,128]{2,1,0:T(8,128)S(1)}, u32[]{:S(2)}, u32[]{:S(2)}) async-start(f32[32,5,128]{2,1,0:T(8,128)} %reshape.220), calls=%async_computation.4 | async-start | bytes 262144 | tf_op jit(solution)/shard_map/all_to_all | solution.py:507
  702.2 12.2 %all-to-all-start.5 = ((f32[32,5,128]{2,1,0:T(8,128)}), f32[32,5,128]{2,1,0:T(8,128)S(1)}, u32[]{:S(2)}, u32[]{:S(2)}) async-start(f32[32,5,128]{2,1,0:T(8,128)} %broadcast_in_dim.8), calls=%async_computation.5 | async-start | bytes 262144 | tf_op jit(solution)/shard_map/all_to_all | solution.py:509
  715.8 52.5 %collective-permute-start.15 = (bf16[400,800]{1,0:T(8,128)(2,1)}, bf16[400,800]{1,0:T(8,128)(2,1)S(1)}, u32[]{:S(2)}, u32[]{:S(2)}) collective-permute-start(bf16[400,800]{1,0:T(8,128)(2,1)} %bitcast.150), channel_id=1, source_target_pairs={{0,0},{1,1},{2,2},{3,3},{4,4},{5,5},{6,6},{7,7},{8,16},{9,17},{10,... | collective-permute-start | bytes 1920008 | tf_op jit(solution)/shard_map/ppermute | solution.py:436
  718.8 64.9 %collective-permute-start.14 = (bf16[800,400]{0,1:T(8,128)(2,1)}, bf16[800,400]{0,1:T(8,128)(2,1)S(1)}, u32[]{:S(2)}, u32[]{:S(2)}) collective-permute-start(bf16[800,400]{0,1:T(8,128)(2,1)} %bitcast.151), channel_id=1, source_target_pairs={{0,0},{1,1},{2,2},{3,3},{4,4},{5,5},{6,6},{7,7},{8,16},{9,17},{10,... | collective-permute-start | bytes 1920008 | tf_op jit(solution)/shard_map/ppermute | solution.py:437
  728.2 41.3 %collective-permute-start.13 = (bf16[100,800]{1,0:T(8,128)(2,1)S(1)}, bf16[100,800]{1,0:T(8,128)(2,1)S(1)}, u32[]{:S(2)}, u32[]{:S(2)}) collective-permute-start(bf16[100,800]{1,0:T(8,128)(2,1)S(1)} %dynamic-slice_convert_fusion.1), channel_id=1, source_target_pairs={{0,16},{16,0},{1,17},{17,1},{2,18},{18,2},{3,19},{19,3},{4,20},{20... | collective-permute-start | bytes 480008 | tf_op jit(solution)/shard_map/ppermute | solution.py:331
  (23 other events, 86.9 us)
Sparse Core Ops, SparseCore 0:
  95.8 75.8 all-gather.2
  275.8 130.9 reduce-scatter.4
  436.4 170.5 reduce-scatter.2
  609.0 76.2 all-gather.4

commit v2 on v1

v2 whole, which is shorter than its diff:
```python
from functools import partial
import math

import jax
import jax.numpy as jnp
from jax import lax
from jax.experimental import pallas as pl
from jax.experimental.pallas import tpu as pltpu
from jax.sharding import PartitionSpec as P

from jax.experimental.layout import Layout, with_layout_constraint

HEADS = 25


EPS = 1e-05
GELU_C = 0.7978845608028654
NEG_FILL = -1e30
BF16 = jnp.bfloat16
F32 = jnp.float32


def normalize(data):
    centre = jnp.mean(data, axis=0, keepdims=True)
    shifted = data - centre
    inverse = lax.rsqrt(jnp.mean(shifted * shifted, axis=0, keepdims=True) + EPS)
    return (shifted * inverse, inverse)


def norm_back(grad_hat, normed, inverse):
    first_mean = jnp.mean(grad_hat, axis=0, keepdims=True)
    second = jnp.mean(grad_hat * normed, axis=0, keepdims=True)
    return inverse * (grad_hat - first_mean - normed * second)


def gelu_parts(values):
    cubic_term = 0.044715 * values * values * values
    tangent = jnp.tanh(GELU_C * (values + cubic_term))
    output = 0.5 * values * (1.0 + tangent)
    gelu_slope = 0.5 * (1.0 + tangent) + 0.5 * values * (1.0 - tangent * tangent) * GELU_C * (
        1.0 + 3.0 * 0.044715 * values * values
    )
    return (output, gelu_slope)


def head_parts(value, head_width):
    heads = value.shape[1] // head_width
    if heads == 1:
        return [value]
    lane = lax.broadcasted_iota(jnp.int32, value.shape, 1) // head_width
    return [jnp.where(lane == h, value, jnp.zeros_like(value)) for h in range(heads)]


def by_head(columns, shape, head_width):
    if len(columns) == 1:
        return jnp.broadcast_to(columns[0], shape)
    lane = lax.broadcasted_iota(jnp.int32, shape, 1) // head_width
    result = jnp.broadcast_to(columns[-1], shape)
    for h in range(len(columns) - 2, -1, -1):
        result = jnp.where(lane == h, columns[h], result)
    return result


def dot(a, b, contract):
    return lax.dot_general(a, b, (contract, ((), ())), preferred_element_type=F32)


def each_query_block(length, block, visit):
    if length // block <= 4:
        for index in range(length // block):
            chunks = [(0, index * block, False)] if index else []
            visit(index * block, chunks + [(index * block, block, True)])
    else:

        def step(index, carry):
            visit(pl.multiple_of(index * block, block), [(0, length, True)])
            return carry

        lax.fori_loop(0, length // block, step, 0)


def visible_mask(first_row, rows, first_key, keys):
    row_ids = first_row + lax.broadcasted_iota(jnp.int32, (rows, keys), 0)
    key_ids = first_key + lax.broadcasted_iota(jnp.int32, (rows, keys), 1)
    return key_ids <= row_ids


def slot_rows(order, seq, source, half):
    return [pl.multiple_of(order[seq, 2 * source + part] * half, half) for part in range(2)]


def forward_kernel(
    half, block, head_width, score_scale, order, qkv, slot_out, natural, out_rows, log_rows
):
    sources = qkv.shape[0]
    kinds, seqs, length, lanes = natural.shape

    def place(source, carry):
        for kind in range(kinds):
            rows = qkv[source, kind].T
            for seq in range(seqs):
                for part, first in enumerate(slot_rows(order, seq, source, half)):
                    begin = (2 * seq + part) * half
                    natural[kind, seq, pl.ds(first, half), :] = rows[begin : begin + half, :]
        return carry

    lax.fori_loop(0, sources, place, 0)

    def visit(seq, first_row, chunks):
        rows = pl.ds(first_row, block)
        queries = natural[0, seq, rows, :] * jnp.asarray(score_scale, BF16)
        outputs = []
        logs = []
        for query in head_parts(queries, head_width):
            scores = []
            for first_key, keys, masked in chunks:
                part = dot(query, natural[1, seq, first_key : first_key + keys, :], ((1,), (1,)))
                if masked:
                    part = jnp.where(
                        visible_mask(first_row, block, first_key, keys), part, NEG_FILL
                    )
                scores.append(part)
            top = jnp.max(scores[0], axis=1, keepdims=True)
            for part in scores[1:]:
                top = jnp.maximum(top, jnp.max(part, axis=1, keepdims=True))
            total = jnp.zeros((block, 1), F32)
            summed = jnp.zeros((block, lanes), F32)
            for (first_key, keys, masked), part in zip(chunks, scores):
                weights = jnp.exp(part - top)
                total = total + jnp.sum(weights, axis=1, keepdims=True)
                coarse = weights.astype(BF16)
                fine = (weights - coarse.astype(F32)).astype(BF16)
                values = natural[2, seq, first_key : first_key + keys, :]
                summed = summed + dot(coarse, values, ((1,), (0,))) + dot(fine, values, ((1,), (0,)))
            outputs.append(summed / total)
            logs.append(top + jnp.log(total))
        result = outputs[0]
        if len(outputs) > 1:
            lane = lax.broadcasted_iota(jnp.int32, result.shape, 1) // head_width
            for h in range(1, len(outputs)):
                result = jnp.where(lane == h, outputs[h], result)
        out_rows[seq, rows, :] = result.astype(BF16)
        log_rows[seq, rows, :] = by_head(logs, result.shape, head_width)

    def one_sequence(seq, carry):
        each_query_block(length, block, partial(visit, seq))
        return carry

    lax.fori_loop(0, seqs, one_sequence, 0)

    def give(source, carry):
        rows = [
            out_rows[seq, pl.ds(first, half), :]
            for seq in range(seqs)
            for first in slot_rows(order, seq, source, half)
        ]
        slot_out[source] = jnp.concatenate(rows, axis=0).T
        return carry

    lax.fori_loop(0, sources, give, 0)


def backward_kernel(
    half,
    block,
    head_width,
    score_scale,
    order,
    natural,
    out_rows,
    log_rows,
    grad_slots,
    slot_out,
    grad_rows,
    grad_natural,
):
    sources = grad_slots.shape[0]
    kinds, seqs, length, lanes = natural.shape

    def place(source, carry):
        rows = grad_slots[source].T
        for seq in range(seqs):
            for part, first in enumerate(slot_rows(order, seq, source, half)):
                begin = (2 * seq + part) * half
                grad_rows[seq, pl.ds(first, half), :] = rows[begin : begin + half, :]
        return carry

    lax.fori_loop(0, sources, place, 0)
    grad_natural[1:] = jnp.zeros((kinds - 1, seqs, length, lanes), F32)

    def visit(seq, first_row, chunks):
        rows = pl.ds(first_row, block)
        queries = natural[0, seq, rows, :] * jnp.asarray(score_scale, BF16)
        grads = grad_rows[seq, rows, :]
        products = grads.astype(F32) * out_rows[seq, rows, :].astype(F32)
        logs = log_rows[seq, rows, :]
        query_sum = jnp.zeros(products.shape, F32)
        parts = zip(
            head_parts(queries, head_width),
            head_parts(grads, head_width),
            head_parts(products, head_width),
        )
        for h, (query, grad, product) in enumerate(parts):
            delta = jnp.sum(product, axis=1, keepdims=True)
            log_total = logs[:, h * head_width : h * head_width + 1]
            for first_key, keys, masked in chunks:
                span = slice(first_key, first_key + keys)
                key_block = natural[1, seq, span, :]
                scores = dot(query, key_block, ((1,), (1,)))
                probs = jnp.exp(scores - log_total)
                if masked:
                    probs = jnp.where(
                        visible_mask(first_row, block, first_key, keys), probs, 0.0
                    )
                grad_probs = dot(grad, natural[2, seq, span, :], ((1,), (1,)))
                grad_scores = (probs * (grad_probs - delta)).astype(BF16)
                grad_natural[2, seq, span, :] += dot(probs.astype(BF16), grad, ((0,), (0,)))
                grad_natural[1, seq, span, :] += dot(grad_scores, query, ((0,), (0,)))
                query_sum = query_sum + dot(
                    grad_scores, head_parts(key_block, head_width)[h], ((1,), (0,))
                )
        grad_natural[0, seq, rows, :] = query_sum * score_scale

    def one_sequence(seq, carry):
        each_query_block(length, block, partial(visit, seq))
        return carry

    lax.fori_loop(0, seqs, one_sequence, 0)

    def give(source, carry):
        for kind in range(kinds):
            rows = [
                grad_natural[kind, seq, pl.ds(first, half), :]
                for seq in range(seqs)
                for first in slot_rows(order, seq, source, half)
            ]
            slot_out[source, kind] = jnp.concatenate(rows, axis=0).astype(BF16).T
        return carry

    lax.fori_loop(0, sources, give, 0)


def in_vmem(count):
    return [pl.BlockSpec(memory_space=pltpu.VMEM)] * count


def attend_forward(qkv, order, head_width, score_scale):
    sources, kinds, lanes, tokens = qkv.shape
    seqs = order.shape[0]
    length = sources * tokens // seqs
    block = math.gcd(length, 256)
    return pl.pallas_call(
        partial(forward_kernel, tokens // seqs // 2, block, head_width, score_scale),
        in_specs=[pl.BlockSpec(memory_space=pltpu.SMEM)] + in_vmem(1),
        out_specs=in_vmem(4),
        out_shape=[
            jax.ShapeDtypeStruct((sources, lanes, tokens), BF16),
            jax.ShapeDtypeStruct((kinds, seqs, length, lanes), BF16),
            jax.ShapeDtypeStruct((seqs, length, lanes), BF16),
            jax.ShapeDtypeStruct((seqs, length, lanes), F32),
        ],
        name="attf",
    )(order, qkv)


def attend_backward(natural, out_rows, log_rows, grad_slots, order, head_width, score_scale):
    sources, lanes, tokens = grad_slots.shape
    kinds, seqs, length, lanes = natural.shape
    block = math.gcd(length, 256)
    return pl.pallas_call(
        partial(backward_kernel, tokens // seqs // 2, block, head_width, score_scale),
        in_specs=[pl.BlockSpec(memory_space=pltpu.SMEM)] + in_vmem(4),
        out_specs=in_vmem(1)[0],
        scratch_shapes=[
            pltpu.VMEM((seqs, length, lanes), BF16),
            pltpu.VMEM((kinds, seqs, length, lanes), F32),
        ],
        out_shape=jax.ShapeDtypeStruct((sources, kinds, lanes, tokens), BF16),
        name="attb",
    )(order, natural, out_rows, log_rows, grad_slots)


def product_kernel(kept, got, own, side, core, parts):
    units, tokens = kept.shape[0], own.shape[1]
    halves, _, width = parts.shape
    block = own.shape[0] // halves
    pairs = (
        (kept, 0, own, 0),
        (kept, tokens, core, 0),
        (got, 0, side, 0),
        (got, tokens, core, tokens),
    )
    step = units // 2

    def one_half(half, carry):
        for first in range(0, units, step):
            total = jnp.zeros((step, block), F32)
            for left, left_at, right, right_at in pairs:
                a = left[first : first + step, left_at : left_at + tokens]
                rows = pl.ds(pl.multiple_of(half * block, 16), block)
                b = right[rows, right_at : right_at + tokens]
                total = total + dot(a, b, ((1,), (1,)))
            parts[half, first : first + step, :block] = total.astype(BF16)
            if width > block:
                blank = jnp.zeros((step, width - block), BF16)
                parts[half, first : first + step, block:] = blank
        return carry

    lax.fori_loop(0, halves, one_half, 0)


def tokens_product(units, rows):
    kept, got = units
    own, side, core = rows
    width = own.shape[0] // 2
    return pl.pallas_call(
        product_kernel,
        in_specs=in_vmem(5),
        out_specs=in_vmem(1)[0],
        out_shape=jax.ShapeDtypeStruct((2, kept.shape[0], width + -width % 128), BF16),
        name="prod",
    )(kept, got, own, side, core)


def rounds_of(edges):
    at_source, at_target = {}, {}
    for source, target, item in edges:
        sends, gets = at_source.setdefault(source, {}), at_target.setdefault(target, {})
        first = next(r for r in range(len(edges)) if r not in sends)
        last = next(r for r in range(len(edges)) if r not in gets)
        if first != last:
            path, node, side, look = [], target, at_target, first
            while look in side.setdefault(node, {}):
                edge = side[node][look]
                path.append((edge, look))
                node = edge[0] if side is at_target else edge[1]
                side = at_source if side is at_target else at_target
                look = first + last - look
            for edge, was in path:
                del at_source[edge[0]][was], at_target[edge[1]][was]
            for edge, was in path:
                now = first + last - was
                at_source[edge[0]][now] = at_target[edge[1]][now] = edge
        sends[first] = gets[first] = (source, target, item)
    count = 1 + max(r for sends in at_source.values() for r in sends)
    return [[sends[r] for sends in at_source.values() if r in sends] for r in range(count)]


def to_heads(data, devices, lanes):
    width, tokens = data.shape
    return jnp.pad(data, ((0, devices * lanes - width), (0, 0))).reshape(devices, lanes, tokens)


def from_heads(blocks, width):
    devices, lanes, tokens = blocks.shape
    return blocks.reshape(devices * lanes, tokens)[:width]


def shards(
    ctx,
    layer_in,
    out_grad,
    block_order,
    ln1_gain,
    ln1_bias,
    w_qkv,
    qv_bias,
    w_out,
    out_bias,
    ln2_gain,
    ln2_bias,
    w_up,
    up_bias,
    w_down,
    down_bias,
):
    seqs, tok_rows, width = layer_in.shape
    tokens = seqs * tok_rows
    head_width = width // HEADS
    score_scale = 1.0 / math.sqrt(head_width)
    lanes = -(-HEADS // ctx) * head_width
    half_units = w_up.shape[1]
    half_cols = w_out.shape[1]
    half_proj = w_qkv.shape[1]
    planes = ctx // 4
    my_dp = lax.axis_index("dp")
    my_ctx = lax.axis_index("ctx")
    my_core = my_ctx % 2
    my_side = (my_ctx // 2) % 2
    core_swap = [(i, i ^ 1) for i in range(ctx)]
    side_swap = [(i, i ^ 2) for i in range(ctx)]
    lines = [[q + 4 * z for z in range(planes)] for q in range(4)]

    def across(x):
        return lax.ppermute(x, "dp", [(0, 1), (1, 0)])

    def to_core(x):
        return lax.ppermute(x, "ctx", core_swap)

    def to_side(x):
        return lax.ppermute(x, "ctx", side_swap)

    def exchange(x):
        return lax.all_to_all(x, "ctx", 0, 0, tiled=True)

    def after(x, *earlier):
        return lax.optimization_barrier((x,) + earlier)[0]

    def pick(x, index, axis, count=2):
        size = x.shape[axis] // count
        return lax.dynamic_slice_in_dim(x, index * size, size, axis)

    def split(x, index, axis):
        return pick(x, index, axis), pick(x, 1 - index, axis)

    def joined(index, mine, other, axis=0):
        return jnp.where(
            index == 0,
            jnp.concatenate([mine, other], axis=axis),
            jnp.concatenate([other, mine], axis=axis),
        )

    def dot32(a, b, spec):
        return jnp.einsum(spec, a, b, preferred_element_type=F32)

    column = lambda vector: vector[:, None]

    own_in = layer_in.reshape(tokens, width).T
    own_out_grad = out_grad.reshape(tokens, width).T
    other_in = across(own_in)
    stream = own_in.astype(F32)
    normed_one, inverse_one = normalize(stream)
    gain_one, bias_one = column(ln1_gain), column(ln1_bias)
    hidden_one = (normed_one * gain_one + bias_one).astype(BF16)
    hidden_one_other = (normalize(other_in.astype(F32))[0] * gain_one + bias_one).astype(BF16)
    proj_bias = jnp.concatenate([qv_bias[0], jnp.zeros_like(qv_bias[0]), qv_bias[1]])
    proj_bias = column(pick(proj_bias, my_dp, 0))
    proj_other = (dot32(w_qkv, hidden_one_other, "de,dt->et") + proj_bias).astype(BF16)
    proj_got = across(proj_other)
    proj_own = (dot32(w_qkv, hidden_one, "de,dt->et") + proj_bias).astype(BF16)
    proj_own = lax.optimization_barrier(proj_own)
    low = jnp.where(my_dp == 0, proj_own, proj_got)
    high = jnp.where(my_dp == 0, proj_got, proj_own)
    queries = low[:width]
    keys = jnp.concatenate([low[width:], high[: 2 * width - half_proj]], axis=0)
    values = high[2 * width - half_proj :]
    send = jnp.stack([to_heads(x, ctx, lanes) for x in (queries, keys, values)], axis=1)
    qkv_heads = exchange(send)

    out_mine = across(after(pick(w_out, my_core, 0), proj_got))
    other_out_grad = across(after(own_out_grad, proj_got))
    down_rows = pick(w_down, my_dp, 0)
    down_send = pick(pick(w_down, 1 - my_dp, 0), my_core, 1)
    down_mine = across(after(down_send, proj_got))
    out_rest = to_core(after(out_mine, qkv_heads))

    hidden_one_all = lax.all_gather(after(hidden_one.T, qkv_heads), "ctx", axis=0, tiled=True)

    attended_slots, natural, out_rows, log_rows = attend_forward(
        qkv_heads, block_order, head_width, score_scale
    )
    attended = from_heads(exchange(attended_slots), width)
    down_rest = to_core(after(down_mine, attended))

    attended_mine, attended_rest = split(attended, my_core, 0)
    mixed = joined(
        my_dp,
        dot32(w_out, attended, "ab,at->bt"),
        dot32(out_mine, attended_mine, "ab,at->bt") + dot32(out_rest, attended_rest, "ab,at->bt"),
    )
    residual = stream + mixed + column(out_bias)
    normed_two, inverse_two = normalize(residual)
    gain_two = column(ln2_gain)
    hidden_two = (normed_two * gain_two + column(ln2_bias)).astype(BF16)
    hidden_two_pair = jnp.concatenate([hidden_two, across(hidden_two)], axis=1)

    out_grad_pair = after(
        jnp.concatenate([own_out_grad, after(other_out_grad, attended)], axis=1), hidden_two
    )
    out_grad_own, out_grad_rest = split(out_grad_pair, my_dp, 0)
    rest_mine, rest_rest = split(out_grad_rest, my_core, 0)
    grad_active = (
        dot32(down_rows, out_grad_own, "fd,dt->ft")
        + dot32(down_mine, rest_mine, "fd,dt->ft")
        + dot32(down_rest, rest_rest, "fd,dt->ft")
    )
    pre_act = dot32(w_up, hidden_two_pair, "df,dt->ft") + column(pick(up_bias, my_dp, 0))
    activated_wide, gelu_slope = gelu_parts(pre_act)
    activated = with_layout_constraint(activated_wide.astype(BF16), Layout((0, 1)))
    grad_pre = with_layout_constraint((grad_active * gelu_slope).astype(BF16), Layout((0, 1)))
    grad_two = dot32(grad_pre, w_up, "ft,df->dt")
    two_send = grad_two[:, tokens:].astype(BF16)
    grad_two_got = across(two_send)
    grad_hidden_two = grad_two[:, :tokens] + grad_two_got.astype(F32)

    grad_out = own_out_grad.astype(F32)
    grad_residual = grad_out + norm_back(grad_hidden_two * gain_two, normed_two, inverse_two)
    grad_mixed = grad_residual.astype(BF16)
    mixed_own, mixed_other = split(grad_mixed, my_dp, 0)
    grad_attended = (
        dot32(w_out, mixed_own, "ab,bt->at")
        + joined(
            my_core,
            dot32(out_mine, mixed_other, "ab,bt->at"),
            dot32(out_rest, mixed_other, "ab,bt->at"),
        )
    ).astype(BF16)
    middle_sums = [
        jnp.sum(grad_mixed.astype(F32), axis=1),
        jnp.sum(grad_hidden_two * normed_two, axis=1),
        jnp.sum(grad_hidden_two, axis=1),
        jnp.sum(grad_out, axis=1),
        jnp.sum(grad_pre.astype(F32), axis=1),
    ]
    grad_send, *middle_sums = lax.optimization_barrier(
        [to_heads(grad_attended, ctx, lanes)] + middle_sums
    )
    grad_slots = exchange(grad_send)

    def plane_rows(data, later):
        side = after(to_side(data), *later)
        return data, side, to_core(jnp.concatenate([data, side], axis=-1))

    def all_rows(own, side, core):
        size = own.shape[-1]
        return jnp.concatenate([own, core[..., :size], side, core[..., size:]], axis=-1)

    def plane_units(units, later):
        size = units.shape[0] // (planes // 2 * 4)
        grid = units.reshape(planes // 2, 2, 2, size, units.shape[1])
        kept, sent = split(grid, my_core, 2)
        both = jnp.concatenate([kept, after(to_core(sent), *later)], axis=-1)
        kept, sent = split(both, my_side, 1)
        return kept, to_side(sent)

    def all_units(kept, got):
        return jnp.concatenate([kept, got], axis=-1).reshape(-1, 2 * kept.shape[-1])

    def flat(units):
        return units.reshape(-1, units.shape[-1])

    def line_sum(parts):
        return lax.psum_scatter(
            parts, "ctx", scatter_dimension=0, axis_index_groups=lines, tiled=False
        )

    active_kept, active_got = plane_units(activated, (grad_two,))
    pre_kept, pre_got = plane_units(grad_pre, (two_send,))
    out_grad_early = jnp.concatenate([own_out_grad, after(other_out_grad, qkv_heads)], axis=1)
    out_grad_all = plane_rows(out_grad_early, (two_send,))

    down_parts = tokens_product((flat(active_kept), flat(after(active_got, two_send))), out_grad_all)
    down_parts = down_parts.reshape(planes, -1, down_parts.shape[2])
    hidden_two_all = plane_rows(hidden_two_pair, (two_send,))
    up_parts = tokens_product((flat(pre_kept), flat(after(pre_got, down_parts))), hidden_two_all)
    up_kept, up_sent = [x[0] for x in split(up_parts, my_dp, 0)]
    up_got = across(up_sent)

    line_ready = after(down_parts, hidden_one_all)
    down_sums = line_sum(line_ready)[:, :half_cols]
    owner = [
        (d * ctx + (e * planes // 2 + z) * 4 + q, e * ctx + (d * planes // 2 + z) * 4 + q)
        for d in range(2)
        for e in range(2)
        for z in range(planes // 2)
        for q in range(4)
    ]

    proj_slots = attend_backward(
        natural,
        out_rows,
        log_rows,
        after(grad_slots, line_ready),
        block_order,
        head_width,
        score_scale,
    )
    proj_back = exchange(proj_slots)
    grad_proj = jnp.concatenate(
        [from_heads(proj_back[:, kind], width) for kind in range(3)], axis=0
    )
    down_grad = lax.ppermute(after(down_sums, proj_slots), ("dp", "ctx"), owner).astype(F32)

    attended_late = after(attended, hidden_two)
    attended_got = after(across(attended_late), proj_slots)
    attended_pair = jnp.concatenate([attended_late, attended_got], axis=1)
    size = width // ctx
    grid = attended_pair.reshape(planes, 2, 2, size, 2 * tokens)
    kept, sent = split(grid, my_core, 2)
    both = jnp.concatenate([kept, to_core(sent)], axis=-1)
    kept, sent = split(both, my_side, 1)
    out_units = (kept, after(to_side(sent), proj_slots))
    mixed_pair = jnp.concatenate([mixed_own, after(across(mixed_other), grad_send)], axis=1)
    mixed_all = all_rows(*plane_rows(mixed_pair, (proj_slots,)))
    out_part = dot32(all_units(*out_units), mixed_all, "ct,dt->cd").astype(BF16)
    out_part = out_part.reshape(planes, size, half_cols)
    unit_block = 2 * half_units // ctx
    up_parts = joined(my_dp, up_kept, after(up_got, proj_slots))
    up_parts = up_parts.reshape(planes, unit_block, -1)
    up_sums = line_sum(up_parts)
    out_sums = line_sum(after(out_part, up_parts))

    proj_mine, proj_rest = split(grad_proj, my_dp, 0)
    proj_pair = jnp.concatenate([proj_mine, across(proj_rest)], axis=1)
    grad_one = dot32(w_qkv, proj_pair, "de,et->dt")
    one_send = grad_one[:, tokens:].astype(BF16)
    grad_one_got = across(one_send)
    grad_hidden_one = grad_one[:, :tokens] + grad_one_got.astype(F32)
    input_grad = grad_residual + norm_back(grad_hidden_one * gain_one, normed_one, inverse_one)
    input_grad = input_grad.astype(BF16).T

    qkv_part = dot32(
        proj_slots, hidden_one_all.reshape(ctx, tokens, width), "sklt,std->kld"
    )
    qkv_kept, qkv_send = split(qkv_part, my_dp, 2)
    qkv_send = qkv_send.astype(BF16)
    qkv_sums = qkv_kept + across(qkv_send).astype(F32)
    qkv_sums = qkv_sums.astype(BF16)
    block = 2 * half_proj // ctx
    edges = []
    for source in range(ctx):
        for kind in range(3):
            first = kind * width + source * lanes
            last = min(first + lanes, (kind + 1) * width)
            if first < last:
                for target in range(first // block, (last - 1) // block + 1):
                    edges.append((source, target, kind))
    rounds = rounds_of(edges)
    kinds = [[0] * ctx for _ in rounds]
    offsets = [[-lanes] * ctx for _ in rounds]
    for number, edges_now in enumerate(rounds):
        for source, target, kind in edges_now:
            kinds[number][source] = kind
            offsets[number][target] = kind * width + source * lanes - target * block
    mine = jnp.arange(ctx, dtype=jnp.int32)[None, :] == my_ctx
    kinds = jnp.sum(jnp.where(mine, jnp.asarray(kinds, jnp.int32), 0), axis=1)[:, None, None]
    offsets = jnp.sum(jnp.where(mine, jnp.asarray(offsets, jnp.int32), 0), axis=1)
    place = offsets[:, None] + jnp.arange(lanes, dtype=jnp.int32)[None, :]
    targets = jnp.arange(block, dtype=jnp.int32)[:, None]
    chosen = (targets == place.reshape(1, -1)).astype(BF16)
    pieces = jnp.where(kinds == 0, qkv_sums[:1], jnp.where(kinds == 1, qkv_sums[1:2], qkv_sums[2:]))
    received = []
    for number, edges_now in enumerate(rounds):
        piece = lax.ppermute(pieces[number], "ctx", [edge[:2] for edge in edges_now])
        received.append(after(piece, grad_one_got))
    received = jnp.concatenate(received, axis=0)
    qkv_grad = dot32(chosen, received, "cr,rd->cd").T

    activated_late = after(activated, grad_one_got)
    down_sum = joined(
        my_dp,
        dot32(activated_late, down_rows, "ft,fd->dt"),
        joined(
            my_core,
            dot32(activated_late, down_mine, "ft,fd->dt"),
            dot32(activated_late, down_rest, "ft,fd->dt"),
        ),
    )
    down_got = across(down_sum[:, tokens:].astype(BF16))
    layer_out = residual + (down_sum[:, :tokens] + down_got.astype(F32)) + column(down_bias)
    layer_out = layer_out.astype(BF16).T

    def at_dp(vector):
        none = jnp.zeros_like(vector)
        return joined(my_dp, vector, none)

    devices = 2 * ctx

    def everywhere(packed):
        return lax.all_to_all(packed, ("dp", "ctx"), 0, 0, tiled=True)

    def pieces_of(totals, items):
        first = 0
        for item in items:
            yield totals[first : first + item.shape[0]]
            first += item.shape[0]

    early = middle_sums[:4] + [at_dp(middle_sums[4])]
    packed = after(jnp.concatenate(early), grad_slots)
    size = -(-packed.shape[0] // (devices * 128)) * 128
    packed = jnp.pad(packed, (0, devices * size - packed.shape[0]))
    mine = everywhere(packed.reshape(devices, size // 128, 128))
    mine = jnp.sum(mine, axis=0).reshape(-1)
    head_sums = jnp.sum(proj_slots.astype(F32), axis=(0, 3))
    packed = jnp.concatenate([mine, head_sums[0], head_sums[2]])
    packed = jnp.pad(packed, (0, -packed.shape[0] % 128)).reshape(1, -1, 128)
    packed = jnp.broadcast_to(packed, (devices,) + packed.shape[1:])
    totals = after(everywhere(packed), grad_one_got).reshape(devices, -1)
    pieces = list(pieces_of(totals[:, :size].reshape(-1), early))
    head_sums = totals[:, size : size + 2 * lanes].reshape(2, ctx, 2, lanes)
    head_sums = jnp.transpose(jnp.sum(head_sums, axis=0), (1, 0, 2)).reshape(2, -1)[:, :width]
    late = [jnp.sum(grad_hidden_one * normed_one, axis=1), jnp.sum(grad_hidden_one, axis=1)]
    packed = jnp.concatenate(late).reshape(1, -1, 128)
    packed = jnp.broadcast_to(packed, (devices,) + packed.shape[1:])
    totals = jnp.sum(everywhere(packed), axis=0)
    ln1 = list(pieces_of(totals.reshape(-1), late))
    up_grad = after(up_sums, totals)[:, :half_cols].astype(F32).T
    out_weight_grad = after(out_sums, totals).astype(F32)

    return (
        layer_out.reshape(layer_in.shape),
        input_grad.reshape(layer_in.shape),
        ln1[0],
        ln1[1],
        qkv_grad,
        head_sums,
        out_weight_grad,
        pieces[0],
        pieces[1],
        pieces[2],
        up_grad,
        pieces[4],
        down_grad,
        pieces[3],
    )


def layer(ctx, *arrays):
    return shards(ctx, *arrays)


def solution(mesh):
    placed = (
        P("dp", "ctx", None),
        P("dp", "ctx", None),
        P("dp", None),
        P(),
        P(),
        P(None, "dp"),
        P(),
        P(None, "dp"),
        P(),
        P(),
        P(),
        P(None, "dp"),
        P(),
        P(None, "dp"),
        P(),
    )
    return jax.shard_map(
        partial(layer, mesh.shape["ctx"]),
        mesh=mesh,
        in_specs=placed,
        out_specs=(
            P("dp", "ctx", None),
            P("dp", "ctx", None),
            P(),
            P(),
            P("dp", "ctx"),
            P(),
            P("ctx", "dp"),
            P(),
            P(),
            P(),
            P("dp", "ctx"),
            P(),
            P("ctx", "dp"),
            P(),
        ),
        check_vma=False,
    )
```

time: 803 us -> 563 us (0.70)
  the two profiles are of different devices: /device:TPU:25 before, /device:TPU:29 now
where the time goes in v2:
time: 563 us; the launch traced here: 554 us
  waiting for transfers between devices  248 us (44%)
  starting transfers between devices  90.1 us (16%)
  matrix products  69.6 us (12%)
  local copies, waits for them, and re-layouts  51.6 us (9%)
  Pallas kernels  47.2 us (8%)
  other arithmetic  31.7 us (6%)
  between operations  15.7 us (3%)
    ppermute x14, waiting for transfers between devices, across(): return lax.ppermute(x, 'dp', [(0, 1), (1, 0)])  104 us
    dot_general x20, matrix products, dot32(): return jnp.einsum(spec, a, b, preferred_element_type=F32)  69.6 us
    all_to_all x4, waiting for transfers between devices, exchange(): return lax.all_to_all(x, 'ctx', 0, 0, tiled=True)  52.8 us
    ppermute x5, waiting for transfers between devices, shards(): lax.ppermute(pieces[number], 'ctx', [edge[:2] for edge in edges_now])  32.5 us
    all_to_all x3, starting transfers between devices, everywhere(): return lax.all_to_all(packed, ('dp', 'ctx'), 0, 0, tiled=True)  29.8 us
    ppermute x6, waiting for transfers between devices, to_side(): return lax.ppermute(x, 'ctx', side_swap)  28.3 us
    all_to_all x4, starting transfers between devices, exchange(): return lax.all_to_all(x, 'ctx', 0, 0, tiled=True)  28.2 us
    ppermute x1, waiting for transfers between devices, shards(): lax.ppermute(after(down_sums, proj_slots), ('dp', 'ctx'), owner).astype(F32)  25.6 us
  transfers between devices with their start and end apart: 45, of which 18 were waited for; matrix products, arithmetic and copies ran while one was open for 23% of the time, Pallas kernels for 9%

profile of v2, /device:TPU:29, one launch (start us, length us, event | category | flops | bytes accessed | tf_op | source)
XLA Modules:
  0.0 553.8 jit_solution(15242585587518084905)
XLA Ops:
  11.4 7.7 %collective-permute-done = bf16[1600,128]{1,0:T(8,128)(2,1)S(1)} collective-permute-done((bf16[1600,128]{1,0:T(8,128)(2,1)S(1)}, bf16[1600,128]{1,0:T(8,128)(2,1)S(1)}, u32[]{:S(2)}, u32[]{:S(2)}) %collective-permute-start) | collective-permute-done | bytes 409632 | tf_op jit(solution)/shard_map/ppermute | solution.py:395
  19.5 7.7 %fusion.9 = bf16[2400,128]{1,0:T(8,128)(2,1)} fusion(bf16[1600,2400]{1,0:T(8,128)(2,1)} %param.22, f32[2400]{0:T(1024)S(1)} %dynamic_slice.98, bf16[1600,128]{1,0:T(8,128)(2,1)S(1)} %collective-permute-done, f32[128]{0:T(128)S(1)} %add_rsqrt_fusion.1, f32[128]{0:T(128)S(1)} %broadcast_multiply_fusion.5, f32[1600]{0:T(1024)S(1)} %copy-done.48, ...), kind=kOutput, calls=%fused_computation.16 | convolution fusion | flops 984883200 | bytes 8727424 | tf_op jit(solution)/shard_map/de,dt->et/dot_general | solution.py:424
  28.4 6.8 %fusion.10 = bf16[2400,128]{1,0:T(8,128)(2,1)S(1)} fusion(bf16[1600,2400]{1,0:T(8,128)(2,1)} %param.22, f32[2400]{0:T(1024)S(1)} %dynamic_slice.98, f32[1600]{0:T(1024)S(1)} %copy-done.48, f32[1600]{0:T(1024)S(1)} %copy-done.44, f32[128]{0:T(128)S(1)} %add_rsqrt_fusion.2, f32[128]{0:T(128)S(1)} %broadcast_multiply_fusion.6, bf16[128,1600]{0,1:T(8,128)(2,1)S(1)} %copy.115), kind=kOutput, calls=%fused_computation.17 | convolution fusion | flops 984883200 | bytes 8727424 | tf_op jit(solution)/shard_map/de,dt->et/dot_general | solution.py:424
  35.3 6.1 %collective-permute-done.1 = bf16[2400,128]{1,0:T(8,128)(2,1)} collective-permute-done((bf16[2400,128]{1,0:T(8,128)(2,1)}, bf16[2400,128]{1,0:T(8,128)(2,1)}, u32[]{:S(2)}, u32[]{:S(2)}) %collective-permute-start.1) | collective-permute-done | bytes 614432 | tf_op jit(solution)/shard_map/ppermute | solution.py:395
  44.4 8.1 %all-to-all-start = ((bf16[16,3,128,128]{3,2,1,0:T(8,128)(2,1)}), bf16[16,3,128,128]{3,2,1,0:T(8,128)(2,1)}, u32[]{:S(2)}, u32[]{:S(2)}) async-start(bf16[16,3,128,128]{3,2,1,0:T(8,128)(2,1)} %pad_maximum_fusion.2), calls=%async_computation | async-start | bytes 3145728 | tf_op jit(solution)/shard_map/all_to_all | solution.py:404
  53.9 33.9 %all-to-all-done.qkv = bf16[16,3,128,128]{3,2,1,0:T(8,128)(2,1)} async-done(((bf16[16,3,128,128]{3,2,1,0:T(8,128)(2,1)}), bf16[16,3,128,128]{3,2,1,0:T(8,128)(2,1)}, u32[]{:S(2)}, u32[]{:S(2)}) %all-to-all-start) | async-done | bytes 1572896 | tf_op jit(solution)/shard_map/all_to_all | solution.py:404
  87.9 4.6 dynamic_slice.105
  95.7 13.5 %attf.1 = (bf16[16,128,128]{2,1,0:T(8,128)(2,1)}, bf16[3,2,1024,128]{3,2,1,0:T(8,128)(2,1)}, bf16[2,1024,128]{2,1,0:T(8,128)(2,1)}, f32[2,1024,128]{2,1,0:T(8,128)}) custom-call(s32[2,32]{1,0:T(2,128)} %order.3, bf16[16,3,128,128]{3,2,1,0:T(8,128)(2,1)} %all-to-all-done.qkv), custom_call_target="tpu_custom_call" | custom-call | tf_op jit(solution)/shard_map/attf/pallas_call | solution.py:252
  109.3 6.3 %all-to-all-start.1 = ((bf16[16,128,128]{2,1,0:T(8,128)(2,1)}), bf16[16,128,128]{2,1,0:T(8,128)(2,1)}, u32[]{:S(2)}, u32[]{:S(2)}) async-start(bf16[16,128,128]{2,1,0:T(8,128)(2,1)} %get-tuple-element.59), calls=%async_computation.1 | async-start | bytes 1048576 | tf_op jit(solution)/shard_map/all_to_all | solution.py:404
  115.6 64.9 %collective-permute-done.2 = bf16[800,800]{0,1:T(8,128)(2,1)} collective-permute-done((bf16[800,800]{0,1:T(8,128)(2,1)}, bf16[800,800]{0,1:T(8,128)(2,1)}, u32[]{:S(2)}, u32[]{:S(2)}) %collective-permute-start.2) | collective-permute-done | bytes 1280032 | tf_op jit(solution)/shard_map/ppermute | solution.py:395
  184.7 9.2 %collective-permute-done.5 = bf16[1600,128]{1,0:T(8,128)(2,1)S(1)} collective-permute-done((bf16[1600,128]{1,0:T(8,128)(2,1)S(1)}, bf16[1600,128]{1,0:T(8,128)(2,1)S(1)}, u32[]{:S(2)}, u32[]{:S(2)}) %collective-permute-start.5) | collective-permute-done | bytes 409632 | tf_op jit(solution)/shard_map/ppermute | solution.py:395
  198.0 2.1 convolution_bitcast_fusion.4
  206.6 4.4 fusion.5
  211.0 2.9 convolution_add_fusion.1
  213.9 2.4 collective-permute-done.4
  216.3 8.5 %multiply_convert_fusion = (bf16[3200,256]{1,0:T(8,128)(2,1)S(1)}, f32[3200,256]{1,0:T(8,128)S(1)}) fusion(f32[3200]{0:T(1024)S(1)} %dynamic_slice.103, bf16[1600,3200]{1,0:T(8,128)(2,1)} %param.28, bf16[1600,128]{1,0:T(8,128)(2,1)S(1)} %collective-permute-done.4, bf16[1600,128]{1,0:T(8,128)(2,1)S(1)} %add_convert_fusion.2), kind=kOutput, calls=%fused_computation.24 | convolution fusion | flops 2631270400 | bytes 15987200 | tf_op jit(solution)/shard_map/df,dt->ft/dot_general | solution.py:424
  228.4 3.5 convert_reduce_fusion
  232.4 3.1 convolution_bitcast_fusion.1
  242.5 4.4 collective-permute-done.30.side
  251.7 12.7 %collective-permute-done.10 = bf16[2,1,1,400,512]{4,3,0,2,1:T(8,128)(2,1)S(1)} collective-permute-done((bf16[2,1,1,400,512]{4,3,0,2,1:T(8,128)(2,1)S(1)}, bf16[2,1,1,400,512]{4,3,0,2,1:T(8,128)(2,1)S(1)}, u32[]{:S(2)}, u32[]{:S(2)}) %collective-permute-start.10) | collective-permute-done | bytes 819232 | tf_op jit(solution)/shard_map/ppermute | solution.py:401
  266.0 8.0 %prod.2 = bf16[2,800,896]{2,1,0:T(8,128)(2,1)} custom-call(bf16[800,512]{1,0:T(8,128)(2,1)} %bitcast.150, bf16[800,512]{1,0:T(8,128)(2,1)} %bitcast.161, bf16[1600,256]{1,0:T(8,128)(2,1)} %copy-done.18, bf16[1600,256]{1,0:T(8,128)(2,1)} %copy-done.19, bf16[1600,512]{1,0:T(8,128)(2,1)} %copy-done.30), custom_call_target="tpu_custom_call" | custom-call | tf_op jit(solution)/shard_map/prod/pallas_call | solution.py:316
  275.9 2.1 fusion.89
  282.1 6.6 %all-to-all-start.2 = ((bf16[16,128,128]{2,1,0:T(8,128)(2,1)}), bf16[16,128,128]{2,1,0:T(8,128)(2,1)}, u32[]{:S(2)}, u32[]{:S(2)}) async-start(bf16[16,128,128]{2,1,0:T(8,128)(2,1)} %bitcast.14), calls=%async_computation.2 | async-start | bytes 1048576 | tf_op jit(solution)/shard_map/all_to_all | solution.py:404
  293.9 4.2 collective-permute-done.25
  298.1 17.1 %all-to-all-done.2.grad_slots = bf16[16,128,128]{2,1,0:T(8,128)(2,1)} async-done(((bf16[16,128,128]{2,1,0:T(8,128)(2,1)}), bf16[16,128,128]{2,1,0:T(8,128)(2,1)}, u32[]{:S(2)}, u32[]{:S(2)}) %all-to-all-start.2) | async-done | bytes 524320 | tf_op jit(solution)/shard_map/all_to_all | solution.py:404
  315.9 6.7 %all-to-all-start.5 = ((f32[32,4,128]{2,1,0:T(4,128)}), f32[32,4,128]{2,1,0:T(4,128)S(1)}, u32[]{:S(2)}, u32[]{:S(2)}) async-start(f32[32,4,128]{2,1,0:T(4,128)} %bitcast.41), calls=%async_computation.5 | async-start | bytes 131072 | tf_op jit(solution)/shard_map/all_to_all | solution.py:670
  324.4 4.0 all-to-all-done.5
  329.4 7.9 %prod.3 = bf16[2,800,896]{2,1,0:T(8,128)(2,1)} custom-call(bf16[800,512]{1,0:T(8,128)(2,1)} %bitcast.149, bf16[800,512]{1,0:T(8,128)(2,1)} %bitcast.160, bf16[1600,256]{1,0:T(8,128)(2,1)} %copy-done.16, bf16[1600,256]{1,0:T(8,128)(2,1)} %copy-done.17, bf16[1600,512]{1,0:T(8,128)(2,1)} %collective-permute-done.31.core), custom_call_target="tpu_custom_call" | custom-call | tf_op jit(solution)/shard_map/prod/pallas_call | solution.py:316
  337.2 3.6 dynamic-slice_bitcast_fusion.1
  341.5 17.7 %attb.1 = bf16[16,3,128,128]{3,2,1,0:T(8,128)(2,1)} custom-call(s32[2,32]{1,0:T(2,128)} %order.3, bf16[3,2,1024,128]{3,2,1,0:T(8,128)(2,1)} %get-tuple-element.62.natural, bf16[2,1024,128]{2,1,0:T(8,128)(2,1)} %get-tuple-element.63.out_rows, f32[2,1024,128]{2,1,0:T(8,128)} %get-tuple-element.64.log_rows, bf16[16,128,128]{2,1,0:T(8,128)(2,1)} %all-to-all-done.2.grad_slots), custom_call_target="tpu_custom_call" | custom-call | tf_op jit(solution)/shard_map/attb/pallas_call | solution.py:270
  359.2 7.2 %all-to-all-start.3 = ((bf16[16,3,128,128]{3,2,1,0:T(8,128)(2,1)}), bf16[16,3,128,128]{3,2,1,0:T(8,128)(2,1)}, u32[]{:S(2)}, u32[]{:S(2)}) async-start(bf16[16,3,128,128]{3,2,1,0:T(8,128)(2,1)} %attb.1), calls=%async_computation.3 | async-start | bytes 3145728 | tf_op jit(solution)/shard_map/all_to_all | solution.py:404
  369.0 6.5 %convolution_bitcast_fusion = f32[3,128,1600]{1,2,0:T(8,128)S(1)} fusion(bf16[16,3,128,128]{3,2,1,0:T(8,128)(2,1)S(1)} %copy-done.5, bf16[16,128,1600,1]{2,1,3,0:T(8,128)(2,1)} %bitcast.179), kind=kOutput, calls=%fused_computation.26 | convolution fusion | flops 2516582400 | bytes 10584064 | tf_op jit(solution)/shard_map/sklt,std->kld/dot_general | solution.py:424
  377.9 4.5 maximum_select_fusion
  385.0 11.1 %collective-permute-done.24 = bf16[4,1,1,100,512]{4,3,2,1,0:T(8,128)(2,1)S(1)} collective-permute-done((bf16[4,1,1,100,512]{4,3,2,1,0:T(8,128)(2,1)S(1)}, bf16[4,1,1,100,512]{4,3,2,1,0:T(8,128)(2,1)S(1)}, u32[]{:S(2)}, u32[]{:S(2)}) %collective-permute-start.24) | collective-permute-done | bytes 409632 | tf_op jit(solution)/shard_map/ppermute | solution.py:401
  396.4 2.5 convolution_convert_fusion
  405.8 7.4 %all-to-all-start.6 = ((f32[32,6,128]{2,1,0:T(8,128)}), f32[32,6,128]{2,1,0:T(8,128)S(1)}, u32[]{:S(2)}, u32[]{:S(2)}) async-start(f32[32,6,128]{2,1,0:T(8,128)} %broadcast_in_dim.117), calls=%async_computation.6 | async-start | bytes 262144 | tf_op jit(solution)/shard_map/all_to_all | solution.py:670
  416.1 4.9 collective-permute-done.13
  421.0 5.8 %convolution_bitcast_fusion.2 = f32[1600,256]{1,0:T(8,128)S(1)} fusion(bf16[1600,2400]{1,0:T(8,128)(2,1)} %param.22, bf16[2400,128]{1,0:T(8,128)(2,1)} %collective-permute-done.13, bf16[2400,128]{1,0:T(8,128)(2,1)S(1)} %get-tuple-element.150), kind=kOutput, calls=%fused_computation.29 | convolution fusion | flops 1968537600 | bytes 10547200 | tf_op jit(solution)/shard_map/de,et->dt/dot_general | solution.py:424
  432.3 4.5 collective-permute-done.14
  439.5 2.6 fusion.90
  447.3 10.3 %collective-permute-done.20 = bf16[128,800]{1,0:T(8,128)(2,1)S(1)} collective-permute-done((bf16[128,800]{1,0:T(8,128)(2,1)S(1)}, bf16[128,800]{1,0:T(8,128)(2,1)S(1)}, u32[]{:S(2)}, u32[]{:S(2)}) %collective-permute-start.20) | collective-permute-done | bytes 204832 | tf_op jit(solution)/shard_map/ppermute | solution.py:644
  457.7 22.2 %collective-permute-done.21 = bf16[128,800]{1,0:T(8,128)(2,1)S(1)} collective-permute-done((bf16[128,800]{1,0:T(8,128)(2,1)S(1)}, bf16[128,800]{1,0:T(8,128)(2,1)S(1)}, u32[]{:S(2)}, u32[]{:S(2)}) %collective-permute-start.21) | collective-permute-done | bytes 204832 | tf_op jit(solution)/shard_map/ppermute | solution.py:644
  481.5 15.6 %all-to-all-start.4 = ((f32[32,25,128]{2,1,0:T(8,128)}), f32[32,25,128]{2,1,0:T(8,128)S(1)}, u32[]{:S(2)}, u32[]{:S(2)}) async-start(f32[32,25,128]{2,1,0:T(8,128)} %broadcast_in_dim.105), calls=%async_computation.4 | async-start | bytes 1048576 | tf_op jit(solution)/shard_map/all_to_all | solution.py:670
  503.9 3.0 collective-permute-start.33
  507.0 3.1 fusion.54
  516.5 2.4 convert_bitcast_fusion
  519.0 25.6 %collective-permute-done.33 = bf16[400,800]{1,0:T(8,128)(2,1)} collective-permute-done((bf16[400,800]{1,0:T(8,128)(2,1)}, bf16[400,800]{1,0:T(8,128)(2,1)}, u32[]{:S(2)}, u32[]{:S(2)}) %collective-permute-start.33) | collective-permute-done | bytes 640032 | tf_op jit(solution)/shard_map/ppermute | solution.py:582
  544.5 2.3 convert_element_type.131
  (344 shorter events, 105.6 us)
Async XLA Ops:
  7.2 86.6 %copy-start = (bf16[1600,800]{0,1:T(8,128)(2,1)S(1)}, bf16[1600,800]{0,1:T(8,128)(2,1)}, u32[]{:S(2)}) copy-start(bf16[1600,800]{0,1:T(8,128)(2,1)} %param.24) | copy-start | bytes 7680004
  8.6 10.4 %collective-permute-start = (bf16[1600,128]{1,0:T(8,128)(2,1)S(1)}, bf16[1600,128]{1,0:T(8,128)(2,1)S(1)}, u32[]{:S(2)}, u32[]{:S(2)}) collective-permute-start(bf16[1600,128]{1,0:T(8,128)(2,1)S(1)} %bitcast.143), channel_id=1, source_target_pairs={{0,16},{16,0},{1,17},{17,1},{2,18},{18,2},{3,19},{19,3},{4,20},{20... | collective-permute-start | bytes 1228808 | tf_op jit(solution)/shard_map/ppermute | solution.py:395
  27.2 14.2 %collective-permute-start.1 = (bf16[2400,128]{1,0:T(8,128)(2,1)}, bf16[2400,128]{1,0:T(8,128)(2,1)}, u32[]{:S(2)}, u32[]{:S(2)}) collective-permute-start(bf16[2400,128]{1,0:T(8,128)(2,1)} %fusion.9), channel_id=1, source_target_pairs={{0,16},{16,0},{1,17},{17,1},{2,18},{18,2},{3,19},{19,3},{4,20},{20... | collective-permute-start | bytes 1843208 | tf_op jit(solution)/shard_map/ppermute | solution.py:395
  44.4 43.5 %all-to-all-start = ((bf16[16,3,128,128]{3,2,1,0:T(8,128)(2,1)}), bf16[16,3,128,128]{3,2,1,0:T(8,128)(2,1)}, u32[]{:S(2)}, u32[]{:S(2)}) async-start(bf16[16,3,128,128]{3,2,1,0:T(8,128)(2,1)} %pad_maximum_fusion.2), calls=%async_computation | async-start | bytes 3145728 | tf_op jit(solution)/shard_map/all_to_all | solution.py:404
  52.6 221.5 %all-gather.2.cloned.1.call-start = ((), (), s32[]{:S(2)}) async-start(), calls=%async_computation.10 | async-start | bytes 7241728 | tf_op jit(solution)/shard_map/all_gather | solution.py:457
  92.5 103.1 %collective-permute-start.6 = (bf16[3200,400]{0,1:T(8,128)(2,1)}, bf16[3200,400]{0,1:T(8,128)(2,1)}, u32[]{:S(2)}, u32[]{:S(2)}) collective-permute-start(bf16[3200,400]{0,1:T(8,128)(2,1)} %dynamic_slice.105), channel_id=1, source_target_pairs={{0,16},{16,0},{1,17},{17,1},{2,18},{18,2},{3,19},{19,3},{4,20},{20... | collective-permute-start | bytes 7680008 | tf_op jit(solution)/shard_map/ppermute | solution.py:395
  95.5 88.6 %copy-start.47 = (f32[6400]{0:T(1024)S(1)}, f32[6400]{0:T(1024)}, u32[]{:S(2)}) copy-start(f32[6400]{0:T(1024)} %param.29) | copy-start | bytes 76804
  95.5 85.0 %collective-permute-start.2 = (bf16[800,800]{0,1:T(8,128)(2,1)}, bf16[800,800]{0,1:T(8,128)(2,1)}, u32[]{:S(2)}, u32[]{:S(2)}) collective-permute-start(bf16[800,800]{0,1:T(8,128)(2,1)} %constant_dynamic-slice_fusion.14), channel_id=1, source_target_pairs={{0,16},{16,0},{1,17},{17,1},{2,18},{18,2},{3,19},{19,3},{4,20},{20... | collective-permute-start | bytes 3840008 | tf_op jit(solution)/shard_map/ppermute | solution.py:395
  109.3 84.6 %all-to-all-start.1 = ((bf16[16,128,128]{2,1,0:T(8,128)(2,1)}), bf16[16,128,128]{2,1,0:T(8,128)(2,1)}, u32[]{:S(2)}, u32[]{:S(2)}) async-start(bf16[16,128,128]{2,1,0:T(8,128)(2,1)} %get-tuple-element.59), calls=%async_computation.1 | async-start | bytes 1048576 | tf_op jit(solution)/shard_map/all_to_all | solution.py:404
  115.6 388.3 %reduce-scatter.8.cloned.1.call-start = ((), (), s32[]{:S(2)}) async-start(), calls=%async_computation.12 | async-start | bytes 3584000 | tf_op jit(solution)/shard_map/reduce_scatter | solution.py:543
  180.5 19.6 %collective-permute-start.3 = (bf16[800,800]{0,1:T(8,128)(2,1)}, bf16[800,800]{0,1:T(8,128)(2,1)}, u32[]{:S(2)}, u32[]{:S(2)}) collective-permute-start(bf16[800,800]{0,1:T(8,128)(2,1)} %collective-permute-done.2), channel_id=1, source_target_pairs={{0,1},{1,0},{2,3},{3,2},{4,5},{5,4},{6,7},{7,6},{8,9},{9,8},{10,11... | collective-permute-start | bytes 3840008 | tf_op jit(solution)/shard_map/ppermute | solution.py:398
  182.8 11.1 %collective-permute-start.5 = (bf16[1600,128]{1,0:T(8,128)(2,1)S(1)}, bf16[1600,128]{1,0:T(8,128)(2,1)S(1)}, u32[]{:S(2)}, u32[]{:S(2)}) collective-permute-start(bf16[1600,128]{1,0:T(8,128)(2,1)S(1)} %bitcast.146), channel_id=1, source_target_pairs={{0,16},{16,0},{1,17},{17,1},{2,18},{18,2},{3,19},{19,3},{4,20},{20... | collective-permute-start | bytes 1228808 | tf_op jit(solution)/shard_map/ppermute | solution.py:395
  195.7 32.7 %collective-permute-start.7 = (bf16[3200,400]{0,1:T(8,128)(2,1)}, bf16[3200,400]{0,1:T(8,128)(2,1)S(1)}, u32[]{:S(2)}, u32[]{:S(2)}) collective-permute-start(bf16[3200,400]{0,1:T(8,128)(2,1)} %collective-permute-done.6), channel_id=1, source_target_pairs={{0,1},{1,0},{2,3},{3,2},{4,5},{5,4},{6,7},{7,6},{8,9},{9,8},{10,11... | collective-permute-start | bytes 7680008 | tf_op jit(solution)/shard_map/ppermute | solution.py:398
  197.9 37.6 %collective-permute-start.11 = (bf16[1600,256]{1,0:T(8,128)(2,1)S(1)}, bf16[1600,256]{1,0:T(8,128)(2,1)S(1)}, u32[]{:S(2)}, u32[]{:S(2)}) collective-permute-start(bf16[1600,256]{1,0:T(8,128)(2,1)S(1)} %get-tuple-element.168.own), channel_id=1, source_target_pairs={{0,2},{1,3},{2,0},{3,1},{4,6},{5,7},{6,4},{7,5},{8,10},{9,11},{10,... | collective-permute-start | bytes 2457608 | tf_op jit(solution)/shard_map/ppermute | solution.py:401
  204.8 45.8 %copy-start.52 = (f32[128]{0:T(128)}, f32[128]{0:T(128)S(1)}, u32[]{:S(2)}) copy-start(f32[128]{0:T(128)S(1)} %add_rsqrt_fusion) | copy-start | bytes 1540
  205.3 11.0 %collective-permute-start.4 = (bf16[1600,128]{1,0:T(8,128)(2,1)S(1)}, bf16[1600,128]{1,0:T(8,128)(2,1)S(1)}, u32[]{:S(2)}, u32[]{:S(2)}) collective-permute-start(bf16[1600,128]{1,0:T(8,128)(2,1)S(1)} %add_convert_fusion.2), channel_id=1, source_target_pairs={{0,16},{16,0},{1,17},{17,1},{2,18},{18,2},{3,19},{19,3},{4,20},{20... | collective-permute-start | bytes 1228808 | tf_op jit(solution)/shard_map/ppermute | solution.py:395
  226.0 11.9 %collective-permute-start.9 = (bf16[2,2,1,400,256]{4,3,0,2,1:T(8,128)(2,1)S(1)}, bf16[2,2,1,400,256]{4,3,0,2,1:T(8,128)(2,1)S(1)}, u32[]{:S(2)}, u32[]{:S(2)}) collective-permute-start(bf16[2,2,1,400,256]{4,3,0,2,1:T(8,128)(2,1)S(1)} %copy.140), channel_id=1, source_target_pairs={{0,1},{1,0},{2,3},{3,2},{4,5},{5,4},{6,7},{7,6},{8,9},{9,8},{10,11... | collective-permute-start | bytes 2457608 | tf_op jit(solution)/shard_map/ppermute | solution.py:398
  227.1 19.8 %collective-permute-start.30 = (bf16[1600,256]{1,0:T(8,128)(2,1)S(1)}, bf16[1600,256]{1,0:T(8,128)(2,1)S(1)}, u32[]{:S(2)}, u32[]{:S(2)}) collective-permute-start(bf16[1600,256]{1,0:T(8,128)(2,1)S(1)} %pad_maximum_fusion.7.own), channel_id=1, source_target_pairs={{0,2},{1,3},{2,0},{3,1},{4,6},{5,7},{6,4},{7,5},{8,10},{9,11},{10,... | collective-permute-start | bytes 2457608 | tf_op jit(solution)/shard_map/ppermute | solution.py:401
  235.7 28.8 %collective-permute-start.12 = (bf16[1600,512]{1,0:T(8,128)(2,1)S(1)}, bf16[1600,512]{1,0:T(8,128)(2,1)S(1)}, u32[]{:S(2)}, u32[]{:S(2)}) collective-permute-start(bf16[1600,512]{1,0:T(8,128)(2,1)S(1)} %pad_maximum_fusion), channel_id=1, source_target_pairs={{0,1},{1,0},{2,3},{3,2},{4,5},{5,4},{6,7},{7,6},{8,9},{9,8},{10,11... | collective-permute-start | bytes 4915208 | tf_op jit(solution)/shard_map/ppermute | solution.py:398
  236.5 13.2 %collective-permute-start.8 = (bf16[1600,128]{1,0:T(8,128)(2,1)S(1)}, bf16[1600,128]{1,0:T(8,128)(2,1)S(1)}, u32[]{:S(2)}, u32[]{:S(2)}) collective-permute-start(bf16[1600,128]{1,0:T(8,128)(2,1)S(1)} %slice.259), channel_id=1, source_target_pairs={{0,16},{16,0},{1,17},{17,1},{2,18},{18,2},{3,19},{19,3},{4,20},{20... | collective-permute-start | bytes 1228808 | tf_op jit(solution)/shard_map/ppermute | solution.py:395
  238.9 25.5 %collective-permute-start.10 = (bf16[2,1,1,400,512]{4,3,0,2,1:T(8,128)(2,1)S(1)}, bf16[2,1,1,400,512]{4,3,0,2,1:T(8,128)(2,1)S(1)}, u32[]{:S(2)}, u32[]{:S(2)}) collective-permute-start(bf16[2,1,1,400,512]{4,3,0,2,1:T(8,128)(2,1)S(1)} %get-tuple-element.143), channel_id=1, source_target_pairs={{0,2},{1,3},{2,0},{3,1},{4,6},{5,7},{6,4},{7,5},{8,10},{9,11},{10,... | collective-permute-start | bytes 2457608 | tf_op jit(solution)/shard_map/ppermute | solution.py:401
  241.9 46.9 %collective-permute-start.28 = (bf16[2,2,1,400,256]{4,3,0,2,1:T(8,128)(2,1)}, bf16[2,2,1,400,256]{4,3,0,2,1:T(8,128)(2,1)}, u32[]{:S(2)}, u32[]{:S(2)}) collective-permute-start(bf16[2,2,1,400,256]{4,3,0,2,1:T(8,128)(2,1)} %copy.142), channel_id=1, source_target_pairs={{0,1},{1,0},{2,3},{3,2},{4,5},{5,4},{6,7},{7,6},{8,9},{9,8},{10,11... | collective-permute-start | bytes 2457608 | tf_op jit(solution)/shard_map/ppermute | solution.py:398
  248.3 80.1 %collective-permute-start.31 = (bf16[1600,512]{1,0:T(8,128)(2,1)}, bf16[1600,512]{1,0:T(8,128)(2,1)}, u32[]{:S(2)}, u32[]{:S(2)}) collective-permute-start(bf16[1600,512]{1,0:T(8,128)(2,1)} %pad_maximum_fusion.1), channel_id=1, source_target_pairs={{0,1},{1,0},{2,3},{3,2},{4,5},{5,4},{6,7},{7,6},{8,9},{9,8},{10,11... | collective-permute-start | bytes 4915208 | tf_op jit(solution)/shard_map/ppermute | solution.py:398
  282.1 33.1 %all-to-all-start.2 = ((bf16[16,128,128]{2,1,0:T(8,128)(2,1)}), bf16[16,128,128]{2,1,0:T(8,128)(2,1)}, u32[]{:S(2)}, u32[]{:S(2)}) async-start(bf16[16,128,128]{2,1,0:T(8,128)(2,1)} %bitcast.14), calls=%async_computation.2 | async-start | bytes 1048576 | tf_op jit(solution)/shard_map/all_to_all | solution.py:404
  291.3 37.1 %collective-permute-start.29 = (bf16[2,1,1,400,512]{4,3,0,2,1:T(8,128)(2,1)}, bf16[2,1,1,400,512]{4,3,0,2,1:T(8,128)(2,1)S(1)}, u32[]{:S(2)}, u32[]{:S(2)}) collective-permute-start(bf16[2,1,1,400,512]{4,3,0,2,1:T(8,128)(2,1)} %get-tuple-element.139), channel_id=1, source_target_pairs={{0,2},{1,3},{2,0},{3,1},{4,6},{5,7},{6,4},{7,5},{8,10},{9,11},{10,... | collective-permute-start | bytes 2457608 | tf_op jit(solution)/shard_map/ppermute | solution.py:401
  291.8 6.3 %collective-permute-start.25 = (bf16[800,128]{1,0:T(8,128)(2,1)}, bf16[800,128]{1,0:T(8,128)(2,1)S(1)}, u32[]{:S(2)}, u32[]{:S(2)}) collective-permute-start(bf16[800,128]{1,0:T(8,128)(2,1)} %get-tuple-element.171), channel_id=1, source_target_pairs={{0,16},{16,0},{1,17},{17,1},{2,18},{18,2},{3,19},{19,3},{4,20},{20... | collective-permute-start | bytes 614408 | tf_op jit(solution)/shard_map/ppermute | solution.py:395
  293.6 73.1 %collective-permute-start.22 = (bf16[1600,128]{1,0:T(8,128)(2,1)S(1)}, bf16[1600,128]{1,0:T(8,128)(2,1)S(1)}, u32[]{:S(2)}, u32[]{:S(2)}) collective-permute-start(bf16[1600,128]{1,0:T(8,128)(2,1)S(1)} %copy-done.14), channel_id=1, source_target_pairs={{0,16},{16,0},{1,17},{17,1},{2,18},{18,2},{3,19},{19,3},{4,20},{20... | collective-permute-start | bytes 1228808 | tf_op jit(solution)/shard_map/ppermute | solution.py:395
  315.9 12.6 %all-to-all-start.5 = ((f32[32,4,128]{2,1,0:T(4,128)}), f32[32,4,128]{2,1,0:T(4,128)S(1)}, u32[]{:S(2)}, u32[]{:S(2)}) async-start(f32[32,4,128]{2,1,0:T(4,128)} %bitcast.41), calls=%async_computation.5 | async-start | bytes 131072 | tf_op jit(solution)/shard_map/all_to_all | solution.py:670
  323.4 44.1 %collective-permute-start.26 = (bf16[800,256]{1,0:T(8,128)(2,1)}, bf16[800,256]{1,0:T(8,128)(2,1)}, u32[]{:S(2)}, u32[]{:S(2)}) collective-permute-start(bf16[800,256]{1,0:T(8,128)(2,1)} %pad_maximum_fusion.10), channel_id=1, source_target_pairs={{0,2},{1,3},{2,0},{3,1},{4,6},{5,7},{6,4},{7,5},{8,10},{9,11},{10,... | collective-permute-start | bytes 1228808 | tf_op jit(solution)/shard_map/ppermute | solution.py:401
  340.8 36.7 %collective-permute-start.32 = (bf16[800,896]{1,0:T(8,128)(2,1)}, bf16[800,896]{1,0:T(8,128)(2,1)}, u32[]{:S(2)}, u32[]{:S(2)}) collective-permute-start(bf16[800,896]{1,0:T(8,128)(2,1)} %get-tuple-element.138), channel_id=1, source_target_pairs={{0,16},{16,0},{1,17},{17,1},{2,18},{18,2},{3,19},{19,3},{4,20},{20... | collective-permute-start | bytes 4300808 | tf_op jit(solution)/shard_map/ppermute | solution.py:395
  359.2 42.5 %all-to-all-start.3 = ((bf16[16,3,128,128]{3,2,1,0:T(8,128)(2,1)}), bf16[16,3,128,128]{3,2,1,0:T(8,128)(2,1)}, u32[]{:S(2)}, u32[]{:S(2)}) async-start(bf16[16,3,128,128]{3,2,1,0:T(8,128)(2,1)} %attb.1), calls=%async_computation.3 | async-start | bytes 3145728 | tf_op jit(solution)/shard_map/all_to_all | solution.py:404
  366.5 147.7 %reduce-scatter.10.cloned.1.call-start = ((), (), s32[]{:S(2)}) async-start(), calls=%async_computation.13 | async-start | bytes 931840
  367.1 15.4 %collective-permute-start.23 = (bf16[4,2,1,100,256]{4,3,2,1,0:T(8,128)(2,1)S(1)}, bf16[4,2,1,100,256]{4,3,2,1,0:T(8,128)(2,1)S(1)}, u32[]{:S(2)}, u32[]{:S(2)}) collective-permute-start(bf16[4,2,1,100,256]{4,3,2,1,0:T(8,128)(2,1)S(1)} %get-tuple-element.161), channel_id=1, source_target_pairs={{0,1},{1,0},{2,3},{3,2},{4,5},{5,4},{6,7},{7,6},{8,9},{9,8},{10,11... | collective-permute-start | bytes 1228808 | tf_op jit(solution)/shard_map/ppermute | solution.py:398
  368.6 14.2 %collective-permute-start.27 = (bf16[800,512]{1,0:T(8,128)(2,1)S(1)}, bf16[800,512]{1,0:T(8,128)(2,1)S(1)}, u32[]{:S(2)}, u32[]{:S(2)}) collective-permute-start(bf16[800,512]{1,0:T(8,128)(2,1)S(1)} %pad_maximum_fusion.9), channel_id=1, source_target_pairs={{0,1},{1,0},{2,3},{3,2},{4,5},{5,4},{6,7},{7,6},{8,9},{9,8},{10,11... | collective-permute-start | bytes 2457608 | tf_op jit(solution)/shard_map/ppermute | solution.py:398
  376.8 37.1 %collective-permute-start.16 = (bf16[3,128,800]{1,2,0:T(8,128)(2,1)}, bf16[3,128,800]{1,2,0:T(8,128)(2,1)}, u32[]{:S(2)}, u32[]{:S(2)}) collective-permute-start(bf16[3,128,800]{1,2,0:T(8,128)(2,1)} %dynamic-slice_convert_fusion), channel_id=1, source_target_pairs={{0,16},{16,0},{1,17},{17,1},{2,18},{18,2},{3,19},{19,3},{4,20},{20... | collective-permute-start | bytes 1843208 | tf_op jit(solution)/shard_map/ppermute | solution.py:395
  382.5 13.6 %collective-permute-start.24 = (bf16[4,1,1,100,512]{4,3,2,1,0:T(8,128)(2,1)S(1)}, bf16[4,1,1,100,512]{4,3,2,1,0:T(8,128)(2,1)S(1)}, u32[]{:S(2)}, u32[]{:S(2)}) collective-permute-start(bf16[4,1,1,100,512]{4,3,2,1,0:T(8,128)(2,1)S(1)} %get-tuple-element.160), channel_id=1, source_target_pairs={{0,2},{1,3},{2,0},{3,1},{4,6},{5,7},{6,4},{7,5},{8,10},{9,11},{10,... | collective-permute-start | bytes 1228808 | tf_op jit(solution)/shard_map/ppermute | solution.py:401
  404.3 16.6 %collective-permute-start.13 = (bf16[2400,128]{1,0:T(8,128)(2,1)}, bf16[2400,128]{1,0:T(8,128)(2,1)}, u32[]{:S(2)}, u32[]{:S(2)}) collective-permute-start(bf16[2400,128]{1,0:T(8,128)(2,1)} %get-tuple-element.151), channel_id=1, source_target_pairs={{0,16},{16,0},{1,17},{17,1},{2,18},{18,2},{3,19},{19,3},{4,20},{20... | collective-permute-start | bytes 1843208 | tf_op jit(solution)/shard_map/ppermute | solution.py:395
  405.8 74.8 %all-to-all-start.6 = ((f32[32,6,128]{2,1,0:T(8,128)}), f32[32,6,128]{2,1,0:T(8,128)S(1)}, u32[]{:S(2)}, u32[]{:S(2)}) async-start(f32[32,6,128]{2,1,0:T(8,128)} %broadcast_in_dim.117), calls=%async_computation.6 | async-start | bytes 262144 | tf_op jit(solution)/shard_map/all_to_all | solution.py:670
  413.3 103.2 %reduce-scatter.6.cloned.1.call-start = ((), (), s32[]{:S(2)}) async-start(), calls=%async_computation.11 | async-start | bytes 3584000 | tf_op jit(solution)/shard_map/reduce_scatter | solution.py:543
  426.9 9.9 %collective-permute-start.14 = (bf16[1600,128]{1,0:T(8,128)(2,1)S(1)}, bf16[1600,128]{1,0:T(8,128)(2,1)S(1)}, u32[]{:S(2)}, u32[]{:S(2)}) collective-permute-start(bf16[1600,128]{1,0:T(8,128)(2,1)S(1)} %slice.258), channel_id=1, source_target_pairs={{0,16},{16,0},{1,17},{17,1},{2,18},{18,2},{3,19},{19,3},{4,20},{20... | collective-permute-start | bytes 1228808 | tf_op jit(solution)/shard_map/ppermute | solution.py:395
  428.2 18.2 %collective-permute-start.17 = (bf16[128,800]{1,0:T(8,128)(2,1)S(1)}, bf16[128,800]{1,0:T(8,128)(2,1)S(1)}, u32[]{:S(2)}, u32[]{:S(2)}) collective-permute-start(bf16[128,800]{1,0:T(8,128)(2,1)S(1)} %get-tuple-element.158), channel_id=1, source_target_pairs={{0,11},{1,6},{2,0},{3,7},{4,1},{5,12},{6,8},{7,2},{8,3},{9,9},{10,... | collective-permute-start | bytes 614408 | tf_op jit(solution)/shard_map/ppermute | solution.py:644
  429.0 18.3 %collective-permute-start.18 = (bf16[128,800]{1,0:T(8,128)(2,1)S(1)}, bf16[128,800]{1,0:T(8,128)(2,1)S(1)}, u32[]{:S(2)}, u32[]{:S(2)}) collective-permute-start(bf16[128,800]{1,0:T(8,128)(2,1)S(1)} %get-tuple-element.157), channel_id=1, source_target_pairs={{0,0},{1,11},{2,1},{3,6},{4,2},{5,13},{6,7},{7,3},{8,8},{9,14},{10... | collective-permute-start | bytes 614408 | tf_op jit(solution)/shard_map/ppermute | solution.py:644
  429.7 17.6 %collective-permute-start.19 = (bf16[128,800]{1,0:T(8,128)(2,1)S(1)}, bf16[128,800]{1,0:T(8,128)(2,1)S(1)}, u32[]{:S(2)}, u32[]{:S(2)}) collective-permute-start(bf16[128,800]{1,0:T(8,128)(2,1)S(1)} %get-tuple-element.156), channel_id=1, source_target_pairs={{0,5},{1,0},{2,11},{3,1},{4,7},{5,2},{6,13},{7,8},{8,14},{9,3},{10... | collective-permute-start | bytes 614408 | tf_op jit(solution)/shard_map/ppermute | solution.py:644
  431.0 26.6 %collective-permute-start.20 = (bf16[128,800]{1,0:T(8,128)(2,1)S(1)}, bf16[128,800]{1,0:T(8,128)(2,1)S(1)}, u32[]{:S(2)}, u32[]{:S(2)}) collective-permute-start(bf16[128,800]{1,0:T(8,128)(2,1)S(1)} %get-tuple-element.155), channel_id=1, source_target_pairs={{0,10},{1,5},{2,6},{3,11},{4,12},{5,7},{6,2},{7,13},{8,9},{9,4},{1... | collective-permute-start | bytes 614408 | tf_op jit(solution)/shard_map/ppermute | solution.py:644
  436.8 43.0 %collective-permute-start.21 = (bf16[128,800]{1,0:T(8,128)(2,1)S(1)}, bf16[128,800]{1,0:T(8,128)(2,1)S(1)}, u32[]{:S(2)}, u32[]{:S(2)}) collective-permute-start(bf16[128,800]{1,0:T(8,128)(2,1)S(1)} %get-tuple-element.154), channel_id=1, source_target_pairs={{3,12},{7,14},{10,15},{19,28},{23,30},{26,31}} | collective-permute-start | bytes 614408 | tf_op jit(solution)/shard_map/ppermute | solution.py:644
  446.4 60.5 %collective-permute-start.15 = (bf16[1600,128]{1,0:T(8,128)(2,1)}, bf16[1600,128]{1,0:T(8,128)(2,1)}, u32[]{:S(2)}, u32[]{:S(2)}) collective-permute-start(bf16[1600,128]{1,0:T(8,128)(2,1)} %slice.257), channel_id=1, source_target_pairs={{0,16},{16,0},{1,17},{17,1},{2,18},{18,2},{3,19},{19,3},{4,20},{20... | collective-permute-start | bytes 1228808 | tf_op jit(solution)/shard_map/ppermute | solution.py:395
  481.5 32.6 %all-to-all-start.4 = ((f32[32,25,128]{2,1,0:T(8,128)}), f32[32,25,128]{2,1,0:T(8,128)S(1)}, u32[]{:S(2)}, u32[]{:S(2)}) async-start(f32[32,25,128]{2,1,0:T(8,128)} %broadcast_in_dim.105), calls=%async_computation.4 | async-start | bytes 1048576 | tf_op jit(solution)/shard_map/all_to_all | solution.py:670
  503.9 40.6 %collective-permute-start.33 = (bf16[400,800]{1,0:T(8,128)(2,1)}, bf16[400,800]{1,0:T(8,128)(2,1)}, u32[]{:S(2)}, u32[]{:S(2)}) collective-permute-start(bf16[400,800]{1,0:T(8,128)(2,1)} %bitcast.180), channel_id=1, source_target_pairs={{0,0},{1,1},{2,2},{3,3},{4,4},{5,5},{6,6},{7,7},{8,16},{9,17},{10,... | collective-permute-start | bytes 1920008 | tf_op jit(solution)/shard_map/ppermute | solution.py:582
  (71 other events, 608.6 us)
Sparse Core Ops, SparseCore 0:
  88.0 69.8 all-gather.1
  274.2 65.4 reduce-scatter.7
  400.1 26.4 reduce-scatter.9
  428.7 79.8 reduce-scatter.5

commit v3 on v2

--- a/solution.py
+++ b/solution.py
@@ -280,7 +280,7 @@
     )(order, natural, out_rows, log_rows, grad_slots)
 
 
-def product_kernel(kept, got, own, side, core, parts):
+def product_kernel(flip, kept, got, own, side, core, parts):
     units, tokens = kept.shape[0], own.shape[1]
     halves, _, width = parts.shape
     block = own.shape[0] // halves
@@ -297,7 +297,7 @@
             total = jnp.zeros((step, block), F32)
             for left, left_at, right, right_at in pairs:
                 a = left[first : first + step, left_at : left_at + tokens]
-                rows = pl.ds(pl.multiple_of(half * block, 16), block)
+                rows = pl.ds(pl.multiple_of((half ^ flip[0]) * block, 16), block)
                 b = right[rows, right_at : right_at + tokens]
                 total = total + dot(a, b, ((1,), (1,)))
             parts[half, first : first + step, :block] = total.astype(BF16)
@@ -309,17 +309,17 @@
     lax.fori_loop(0, halves, one_half, 0)
 
 
-def tokens_product(units, rows):
+def tokens_product(units, rows, flip):
     kept, got = units
     own, side, core = rows
     width = own.shape[0] // 2
     return pl.pallas_call(
         product_kernel,
-        in_specs=in_vmem(5),
+        in_specs=[pl.BlockSpec(memory_space=pltpu.SMEM)] + in_vmem(5),
         out_specs=in_vmem(1)[0],
         out_shape=jax.ShapeDtypeStruct((2, kept.shape[0], width + -width % 128), BF16),
         name="prod",
-    )(kept, got, own, side, core)
+    )(jnp.full((1,), flip, jnp.int32), kept, got, own, side, core)
 
 
 def rounds_of(edges):
@@ -521,10 +521,6 @@
         side = after(to_side(data), *later)
         return data, side, to_core(jnp.concatenate([data, side], axis=-1))
 
-    def all_rows(own, side, core):
-        size = own.shape[-1]
-        return jnp.concatenate([own, core[..., :size], side, core[..., size:]], axis=-1)
-
     def plane_units(units, later):
         size = units.shape[0] // (planes // 2 * 4)
         grid = units.reshape(planes // 2, 2, 2, size, units.shape[1])
@@ -533,9 +529,6 @@
         kept, sent = split(both, my_side, 1)
         return kept, to_side(sent)
 
-    def all_units(kept, got):
-        return jnp.concatenate([kept, got], axis=-1).reshape(-1, 2 * kept.shape[-1])
-
     def flat(units):
         return units.reshape(-1, units.shape[-1])
 
@@ -549,11 +542,12 @@
     out_grad_early = jnp.concatenate([own_out_grad, after(other_out_grad, qkv_heads)], axis=1)
     out_grad_all = plane_rows(out_grad_early, (two_send,))
 
-    down_parts = tokens_product((flat(active_kept), flat(after(active_got, two_send))), out_grad_all)
+    units = (flat(active_kept), flat(after(active_got, two_send)))
+    down_parts = tokens_product(units, out_grad_all, 0)
     down_parts = down_parts.reshape(planes, -1, down_parts.shape[2])
     hidden_two_all = plane_rows(hidden_two_pair, (two_send,))
-    up_parts = tokens_product((flat(pre_kept), flat(after(pre_got, down_parts))), hidden_two_all)
-    up_kept, up_sent = [x[0] for x in split(up_parts, my_dp, 0)]
+    units = (flat(pre_kept), flat(after(pre_got, down_parts)))
+    up_kept, up_sent = tokens_product(units, hidden_two_all, my_dp)
     up_got = across(up_sent)
 
     line_ready = after(down_parts, hidden_one_all)
@@ -579,27 +573,12 @@
     grad_proj = jnp.concatenate(
         [from_heads(proj_back[:, kind], width) for kind in range(3)], axis=0
     )
-    down_grad = lax.ppermute(after(down_sums, proj_slots), ("dp", "ctx"), owner).astype(F32)
-
-    attended_late = after(attended, hidden_two)
-    attended_got = after(across(attended_late), proj_slots)
-    attended_pair = jnp.concatenate([attended_late, attended_got], axis=1)
-    size = width // ctx
-    grid = attended_pair.reshape(planes, 2, 2, size, 2 * tokens)
-    kept, sent = split(grid, my_core, 2)
-    both = jnp.concatenate([kept, to_core(sent)], axis=-1)
-    kept, sent = split(both, my_side, 1)
-    out_units = (kept, after(to_side(sent), proj_slots))
-    mixed_pair = jnp.concatenate([mixed_own, after(across(mixed_other), grad_send)], axis=1)
-    mixed_all = all_rows(*plane_rows(mixed_pair, (proj_slots,)))
-    out_part = dot32(all_units(*out_units), mixed_all, "ct,dt->cd").astype(BF16)
-    out_part = out_part.reshape(planes, size, half_cols)
+    down_grad = lax.ppermute(after(down_sums, proj_slots), ("dp", "ctx"), owner)
+
     unit_block = 2 * half_units // ctx
     up_parts = joined(my_dp, up_kept, after(up_got, proj_slots))
     up_parts = up_parts.reshape(planes, unit_block, -1)
     up_sums = line_sum(up_parts)
-    out_sums = line_sum(after(out_part, up_parts))
-
     proj_mine, proj_rest = split(grad_proj, my_dp, 0)
     proj_pair = jnp.concatenate([proj_mine, across(proj_rest)], axis=1)
     grad_one = dot32(w_qkv, proj_pair, "de,et->dt")
@@ -608,6 +587,29 @@
     grad_hidden_one = grad_one[:, :tokens] + grad_one_got.astype(F32)
     input_grad = grad_residual + norm_back(grad_hidden_one * gain_one, normed_one, inverse_one)
     input_grad = input_grad.astype(BF16).T
+
+    attended_late = after(attended, hidden_two)
+    attended_got = after(across(attended_late), proj_back)
+    attended_pair = jnp.concatenate([attended_late, attended_got], axis=1)
+    size = width // ctx
+    grid = attended_pair.reshape(planes, 2, 2, size, 2 * tokens)
+    kept, sent = split(grid, my_core, 2)
+    both = jnp.concatenate([kept, to_core(sent)], axis=-1)
+    kept, sent = split(both, my_side, 1)
+    out_units = (kept, after(to_side(sent), proj_slots))
+    mixed_pair = jnp.concatenate([mixed_own, after(across(mixed_other), proj_back)], axis=1)
+    mixed_all = plane_rows(mixed_pair, (one_send,))
+    out_part = 0.0
+    step = 2 * tokens
+    kept, got = [flat(units) for units in out_units]
+    for units, at, rows in ((kept, 0, 0), (kept, 1, 2), (got, 0, 1), (got, 1, 2)):
+        begin = step if rows == 2 and units is got else 0
+        rows = mixed_all[rows][:, begin : begin + step]
+        out_part += dot32(units[:, at * step : (at + 1) * step], rows, "ct,dt->cd")
+    out_part = out_part.astype(BF16)
+    out_part = out_part.reshape(planes, size, half_cols)
+    out_part = jnp.pad(out_part, ((0, 0), (0, -size % 8), (0, -half_cols % 128)))
+    out_sums = line_sum(after(out_part, up_parts))[:size, :half_cols]
 
     qkv_part = dot32(
         proj_slots, hidden_one_all.reshape(ctx, tokens, width), "sklt,std->kld"
@@ -642,9 +644,7 @@
     received = []
     for number, edges_now in enumerate(rounds):
         piece = lax.ppermute(pieces[number], "ctx", [edge[:2] for edge in edges_now])
-        received.append(after(piece, grad_one_got))
-    received = jnp.concatenate(received, axis=0)
-    qkv_grad = dot32(chosen, received, "cr,rd->cd").T
+        received.append(piece)
 
     activated_late = after(activated, grad_one_got)
     down_sum = joined(
@@ -676,25 +676,28 @@
             first += item.shape[0]
 
     early = middle_sums[:4] + [at_dp(middle_sums[4])]
-    packed = after(jnp.concatenate(early), grad_slots)
+    packed = after(jnp.concatenate(early), proj_back)
     size = -(-packed.shape[0] // (devices * 128)) * 128
     packed = jnp.pad(packed, (0, devices * size - packed.shape[0]))
     mine = everywhere(packed.reshape(devices, size // 128, 128))
-    mine = jnp.sum(mine, axis=0).reshape(-1)
+    mine = jnp.sum(after(mine, grad_one_got), axis=0).reshape(-1)
     head_sums = jnp.sum(proj_slots.astype(F32), axis=(0, 3))
-    packed = jnp.concatenate([mine, head_sums[0], head_sums[2]])
+    late = [jnp.sum(grad_hidden_one * normed_one, axis=1), jnp.sum(grad_hidden_one, axis=1)]
+    packed = jnp.concatenate([mine, head_sums[0], head_sums[2]] + late)
     packed = jnp.pad(packed, (0, -packed.shape[0] % 128)).reshape(1, -1, 128)
     packed = jnp.broadcast_to(packed, (devices,) + packed.shape[1:])
-    totals = after(everywhere(packed), grad_one_got).reshape(devices, -1)
+    totals = everywhere(packed).reshape(devices, -1)
+    pieces_in = [after(piece, packed) for piece in received]
+    qkv_grad = sum(
+        dot32(chosen[:, i * lanes : (i + 1) * lanes], piece, "cr,rd->cd")
+        for i, piece in enumerate(pieces_in)
+    ).T
     pieces = list(pieces_of(totals[:, :size].reshape(-1), early))
     head_sums = totals[:, size : size + 2 * lanes].reshape(2, ctx, 2, lanes)
     head_sums = jnp.transpose(jnp.sum(head_sums, axis=0), (1, 0, 2)).reshape(2, -1)[:, :width]
-    late = [jnp.sum(grad_hidden_one * normed_one, axis=1), jnp.sum(grad_hidden_one, axis=1)]
-    packed = jnp.concatenate(late).reshape(1, -1, 128)
-    packed = jnp.broadcast_to(packed, (devices,) + packed.shape[1:])
-    totals = jnp.sum(everywhere(packed), axis=0)
-    ln1 = list(pieces_of(totals.reshape(-1), late))
+    ln1 = list(pieces_of(jnp.sum(totals[:, size + 2 * lanes :], axis=0), late))
     up_grad = after(up_sums, totals)[:, :half_cols].astype(F32).T
+    down_grad = after(down_grad, totals).astype(F32)
     out_weight_grad = after(out_sums, totals).astype(F32)
 
     return (

time: 563 us -> 589 us (1.046)
  the two profiles are of different devices: /device:TPU:29 before, /device:TPU:0 now
where the time goes in v3:
time: 589 us; the launch traced here: 580 us
  waiting for transfers between devices  248 us (42%)
  starting transfers between devices  90.3 us (15%)
  matrix products  82.9 us (14%)
  local copies, waits for them, and re-layouts  52.9 us (9%)
  Pallas kernels  47.3 us (8%)
  other arithmetic  42.8 us (7%)
  between operations  15.6 us (3%)
    ppermute x14, waiting for transfers between devices, across(): return lax.ppermute(x, 'dp', [(0, 1), (1, 0)])  137 us
    dot_general x27, matrix products, dot32(): return jnp.einsum(spec, a, b, preferred_element_type=F32)  82.9 us
    all_to_all x4, waiting for transfers between devices, exchange(): return lax.all_to_all(x, 'ctx', 0, 0, tiled=True)  49.2 us
    unnamed x5, waiting for transfers between devices  39 us
    all_to_all x4, starting transfers between devices, exchange(): return lax.all_to_all(x, 'ctx', 0, 0, tiled=True)  32.5 us
    ppermute x6, waiting for transfers between devices, to_side(): return lax.ppermute(x, 'ctx', side_swap)  22.5 us
    ppermute x14, starting transfers between devices, across(): return lax.ppermute(x, 'dp', [(0, 1), (1, 0)])  20.5 us
    ppermute x5, starting transfers between devices, shards(): lax.ppermute(pieces[number], 'ctx', [edge[:2] for edge in edges_now])  18.8 us
  transfers between devices with their start and end apart: 44, of which 14 were waited for; matrix products, arithmetic and copies ran while one was open for 28% of the time, Pallas kernels for 8%

profile of v3, /device:TPU:0, one launch (start us, length us, event | category | flops | bytes accessed | tf_op | source)
XLA Modules:
  0.0 580.0 jit_solution(17948953552982674196)
XLA Ops:
  8.6 3.0 collective-permute-start
  13.1 8.0 %collective-permute-done = bf16[1600,128]{1,0:T(8,128)(2,1)S(1)} collective-permute-done((bf16[1600,128]{1,0:T(8,128)(2,1)S(1)}, bf16[1600,128]{1,0:T(8,128)(2,1)S(1)}, u32[]{:S(2)}, u32[]{:S(2)}) %collective-permute-start) | collective-permute-done | bytes 409632 | tf_op jit(solution)/shard_map/ppermute | solution.py:395
  21.6 7.7 %fusion.9 = bf16[2400,128]{1,0:T(8,128)(2,1)} fusion(bf16[1600,2400]{1,0:T(8,128)(2,1)} %param.22, f32[2400]{0:T(1024)S(1)} %dynamic_slice.92, bf16[1600,128]{1,0:T(8,128)(2,1)S(1)} %collective-permute-done, f32[128]{0:T(128)S(1)} %add_rsqrt_fusion.1, f32[128]{0:T(128)S(1)} %broadcast_multiply_fusion.5, f32[1600]{0:T(1024)S(1)} %copy-done.54, ...), kind=kOutput, calls=%fused_computation.16 | convolution fusion | flops 984883200 | bytes 8727424 | tf_op jit(solution)/shard_map/de,dt->et/dot_general | solution.py:424
  31.0 6.8 %fusion.10 = bf16[2400,128]{1,0:T(8,128)(2,1)S(1)} fusion(bf16[1600,2400]{1,0:T(8,128)(2,1)} %param.22, f32[2400]{0:T(1024)S(1)} %dynamic_slice.92, f32[1600]{0:T(1024)S(1)} %copy-done.54, f32[1600]{0:T(1024)S(1)} %copy-done.46, f32[128]{0:T(128)S(1)} %add_rsqrt_fusion.2, f32[128]{0:T(128)S(1)} %broadcast_multiply_fusion.6, bf16[128,1600]{0,1:T(8,128)(2,1)S(1)} %copy.86), kind=kOutput, calls=%fused_computation.17 | convolution fusion | flops 984883200 | bytes 8727424 | tf_op jit(solution)/shard_map/de,dt->et/dot_general | solution.py:424
  37.9 6.7 %collective-permute-done.1 = bf16[2400,128]{1,0:T(8,128)(2,1)} collective-permute-done((bf16[2400,128]{1,0:T(8,128)(2,1)}, bf16[2400,128]{1,0:T(8,128)(2,1)}, u32[]{:S(2)}, u32[]{:S(2)}) %collective-permute-start.1) | collective-permute-done | bytes 614432 | tf_op jit(solution)/shard_map/ppermute | solution.py:395
  47.6 6.1 %all-to-all-start = ((bf16[16,3,128,128]{3,2,1,0:T(8,128)(2,1)}), bf16[16,3,128,128]{3,2,1,0:T(8,128)(2,1)}, u32[]{:S(2)}, u32[]{:S(2)}) async-start(bf16[16,3,128,128]{3,2,1,0:T(8,128)(2,1)} %pad_maximum_fusion.2), calls=%async_computation | async-start | bytes 3145728 | tf_op jit(solution)/shard_map/all_to_all | solution.py:404
  55.1 30.5 %all-to-all-done.qkv = bf16[16,3,128,128]{3,2,1,0:T(8,128)(2,1)} async-done(((bf16[16,3,128,128]{3,2,1,0:T(8,128)(2,1)}), bf16[16,3,128,128]{3,2,1,0:T(8,128)(2,1)}, u32[]{:S(2)}, u32[]{:S(2)}) %all-to-all-start) | async-done | bytes 1572896 | tf_op jit(solution)/shard_map/all_to_all | solution.py:404
  85.7 4.6 dynamic_slice.99
  94.0 13.4 %attf.1 = (bf16[16,128,128]{2,1,0:T(8,128)(2,1)}, bf16[3,2,1024,128]{3,2,1,0:T(8,128)(2,1)}, bf16[2,1024,128]{2,1,0:T(8,128)(2,1)}, f32[2,1024,128]{2,1,0:T(8,128)}) custom-call(s32[2,32]{1,0:T(2,128)} %order.3, bf16[16,3,128,128]{3,2,1,0:T(8,128)(2,1)} %all-to-all-done.qkv), custom_call_target="tpu_custom_call" | custom-call | tf_op jit(solution)/shard_map/attf/pallas_call | solution.py:252
  107.5 9.3 %all-to-all-start.1 = ((bf16[16,128,128]{2,1,0:T(8,128)(2,1)}), bf16[16,128,128]{2,1,0:T(8,128)(2,1)}, u32[]{:S(2)}, u32[]{:S(2)}) async-start(bf16[16,128,128]{2,1,0:T(8,128)(2,1)} %get-tuple-element.60), calls=%async_computation.1 | async-start | bytes 1048576 | tf_op jit(solution)/shard_map/all_to_all | solution.py:404
  116.8 62.9 %collective-permute-done.2 = bf16[800,800]{0,1:T(8,128)(2,1)} collective-permute-done((bf16[800,800]{0,1:T(8,128)(2,1)}, bf16[800,800]{0,1:T(8,128)(2,1)}, u32[]{:S(2)}, u32[]{:S(2)}) %collective-permute-start.2) | collective-permute-done | bytes 1280032 | tf_op jit(solution)/shard_map/ppermute | solution.py:395
  182.8 10.2 %collective-permute-done.5 = bf16[1600,128]{1,0:T(8,128)(2,1)S(1)} collective-permute-done((bf16[1600,128]{1,0:T(8,128)(2,1)S(1)}, bf16[1600,128]{1,0:T(8,128)(2,1)S(1)}, u32[]{:S(2)}, u32[]{:S(2)}) %collective-permute-start.5) | collective-permute-done | bytes 409632 | tf_op jit(solution)/shard_map/ppermute | solution.py:395
  196.3 2.7 collective-permute-start.11
  207.6 4.4 fusion.5
  212.0 2.9 convolution_add_fusion.1
  214.9 2.7 collective-permute-done.4
  217.7 8.3 %multiply_convert_fusion = (bf16[3200,256]{1,0:T(8,128)(2,1)S(1)}, f32[3200,256]{1,0:T(8,128)S(1)}) fusion(f32[3200]{0:T(1024)S(1)} %dynamic_slice.97, bf16[1600,3200]{1,0:T(8,128)(2,1)} %param.28, bf16[1600,128]{1,0:T(8,128)(2,1)S(1)} %collective-permute-done.4, bf16[1600,128]{1,0:T(8,128)(2,1)S(1)} %add_convert_fusion.2), kind=kOutput, calls=%fused_computation.24 | convolution fusion | flops 2631270400 | bytes 15987200 | tf_op jit(solution)/shard_map/df,dt->ft/dot_general | solution.py:424
  228.5 3.5 convert_reduce_fusion
  232.7 3.1 convolution_bitcast_fusion.1
  246.5 16.9 %collective-permute-done.10 = bf16[2,1,1,400,512]{4,3,0,2,1:T(8,128)(2,1)} collective-permute-done((bf16[2,1,1,400,512]{4,3,0,2,1:T(8,128)(2,1)}, bf16[2,1,1,400,512]{4,3,0,2,1:T(8,128)(2,1)}, u32[]{:S(2)}, u32[]{:S(2)}) %collective-permute-start.10) | collective-permute-done | bytes 819232 | tf_op jit(solution)/shard_map/ppermute | solution.py:401
  263.4 8.0 %prod.2 = bf16[2,800,896]{2,1,0:T(8,128)(2,1)} custom-call(s32[1]{0:T(128)} %constant.122.clone.1.flip, bf16[800,512]{1,0:T(8,128)(2,1)} %bitcast.151, bf16[800,512]{1,0:T(8,128)(2,1)} %bitcast.17.got, bf16[1600,256]{1,0:T(8,128)(2,1)} %copy-done.23, bf16[1600,256]{1,0:T(8,128)(2,1)} %copy-done.24, bf16[1600,512]{1,0:T(8,128)(2,1)} %collective-permute-done.12.core), custom_call_target="tpu_custom_call" | custom-call | tf_op jit(solution)/shard_map/prod/pallas_call | solution.py:316
  274.8 5.6 collective-permute-done.30.side
  280.4 2.5 pad_maximum_fusion.1
  293.7 6.5 %all-to-all-start.2 = ((bf16[16,128,128]{2,1,0:T(8,128)(2,1)}), bf16[16,128,128]{2,1,0:T(8,128)(2,1)}, u32[]{:S(2)}, u32[]{:S(2)}) async-start(bf16[16,128,128]{2,1,0:T(8,128)(2,1)} %bitcast.14), calls=%async_computation.2 | async-start | bytes 1048576 | tf_op jit(solution)/shard_map/all_to_all | solution.py:404
  304.7 18.7 %all-to-all-done.2.grad_slots = bf16[16,128,128]{2,1,0:T(8,128)(2,1)} async-done(((bf16[16,128,128]{2,1,0:T(8,128)(2,1)}), bf16[16,128,128]{2,1,0:T(8,128)(2,1)}, u32[]{:S(2)}, u32[]{:S(2)}) %all-to-all-start.2) | async-done | bytes 524320 | tf_op jit(solution)/shard_map/all_to_all | solution.py:404
  323.4 17.8 %attb.1 = bf16[16,3,128,128]{3,2,1,0:T(8,128)(2,1)} custom-call(s32[2,32]{1,0:T(2,128)} %order.3, bf16[3,2,1024,128]{3,2,1,0:T(8,128)(2,1)} %get-tuple-element.63.natural, bf16[2,1024,128]{2,1,0:T(8,128)(2,1)} %get-tuple-element.64.out_rows, f32[2,1024,128]{2,1,0:T(8,128)} %get-tuple-element.65.log_rows, bf16[16,128,128]{2,1,0:T(8,128)(2,1)} %all-to-all-done.2.grad_slots), custom_call_target="tpu_custom_call" | custom-call | tf_op jit(solution)/shard_map/attb/pallas_call | solution.py:270
  341.2 10.6 %all-to-all-start.3 = ((bf16[16,3,128,128]{3,2,1,0:T(8,128)(2,1)}), bf16[16,3,128,128]{3,2,1,0:T(8,128)(2,1)}, u32[]{:S(2)}, u32[]{:S(2)}) async-start(bf16[16,3,128,128]{3,2,1,0:T(8,128)(2,1)} %attb.1), calls=%async_computation.3 | async-start | bytes 3145728 | tf_op jit(solution)/shard_map/all_to_all | solution.py:404
  352.9 8.1 %prod.3 = bf16[2,800,896]{2,1,0:T(8,128)(2,1)} custom-call(s32[1]{0:T(128)} %bitcast.46.flip, bf16[800,512]{1,0:T(8,128)(2,1)} %bitcast.150, bf16[800,512]{1,0:T(8,128)(2,1)} %bitcast.164, bf16[1600,256]{1,0:T(8,128)(2,1)} %pad_maximum_fusion.6.own, bf16[1600,256]{1,0:T(8,128)(2,1)} %collective-permute-done.30.side, ...), custom_call_target="tpu_custom_call" | custom-call | tf_op jit(solution)/shard_map/prod/pallas_call | solution.py:316
  361.0 3.7 slice_bitcast_fusion.1
  369.9 6.6 %convolution_bitcast_fusion = f32[3,128,1600]{1,2,0:T(8,128)S(1)} fusion(bf16[16,3,128,128]{3,2,1,0:T(8,128)(2,1)S(1)} %copy-done.5, bf16[16,128,1600,1]{2,1,3,0:T(8,128)(2,1)} %bitcast.177), kind=kOutput, calls=%fused_computation.26 | convolution fusion | flops 2516582400 | bytes 10584064 | tf_op jit(solution)/shard_map/sklt,std->kld/dot_general | solution.py:424
  377.1 22.2 %collective-permute-done.32 = bf16[800,896]{1,0:T(8,128)(2,1)} collective-permute-done((bf16[800,896]{1,0:T(8,128)(2,1)}, bf16[800,896]{1,0:T(8,128)(2,1)}, u32[]{:S(2)}, u32[]{:S(2)}) %collective-permute-start.32) | collective-permute-done | bytes 1433632 | tf_op jit(solution)/shard_map/ppermute | solution.py:395
  399.3 4.4 maximum_select_fusion
  404.5 20.5 %collective-permute-done.16 = bf16[3,128,800]{1,2,0:T(8,128)(2,1)} collective-permute-done((bf16[3,128,800]{1,2,0:T(8,128)(2,1)S(1)}, bf16[3,128,800]{1,2,0:T(8,128)(2,1)}, u32[]{:S(2)}, u32[]{:S(2)}) %collective-permute-start.16) | collective-permute-done | bytes 614432 | tf_op jit(solution)/shard_map/ppermute | solution.py:395
  445.0 5.7 convolution_bitcast_fusion.2
  455.7 6.4 %collective-permute-start.20 = (bf16[128,800]{1,0:T(8,128)(2,1)}, bf16[128,800]{1,0:T(8,128)(2,1)}, u32[]{:S(2)}, u32[]{:S(2)}) collective-permute-start(bf16[128,800]{1,0:T(8,128)(2,1)} %get-tuple-element.156), channel_id=1, source_target_pairs={{0,10},{1,5},{2,6},{3,11},{4,12},{5,7},{6,2},{7,13},{8,9},{9,4},{1... | collective-permute-start | bytes 614408 | tf_op jit(solution)/shard_map/ppermute | solution.py:646
  462.7 2.6 all-to-all-start.4
  465.3 2.6 fusion.75
  467.9 3.6 collective-permute-start.19
  473.5 3.5 collective-permute-start.18
  478.9 4.0 collective-permute-start.17
  482.8 3.1 fusion.111
  485.9 2.6 fusion.110
  488.6 4.0 fusion.3
  496.5 4.6 all-to-all-start.5
  508.1 2.5 fusion.19
  518.4 2.5 fusion.58
  528.7 2.5 convert_bitcast_fusion
  531.2 38.9 %reduce-scatter.10.cloned.1.call-done = bf16[1,104,896]{2,1,0:T(8,128)(2,1)} async-done(((bf16[4,104,896]{2,1,0:T(8,128)(2,1)}), bf16[1,104,896]{2,1,0:T(8,128)(2,1)}) %reduce-scatter.10.cloned.1.call-update) | async-done | bytes 186384
  (341 shorter events, 126.3 us)
Async XLA Ops:
  7.2 84.6 %copy-start = (bf16[1600,800]{0,1:T(8,128)(2,1)S(1)}, bf16[1600,800]{0,1:T(8,128)(2,1)}, u32[]{:S(2)}) copy-start(bf16[1600,800]{0,1:T(8,128)(2,1)} %param.24) | copy-start | bytes 7680004
  8.6 12.5 %collective-permute-start = (bf16[1600,128]{1,0:T(8,128)(2,1)S(1)}, bf16[1600,128]{1,0:T(8,128)(2,1)S(1)}, u32[]{:S(2)}, u32[]{:S(2)}) collective-permute-start(bf16[1600,128]{1,0:T(8,128)(2,1)S(1)} %bitcast.144), channel_id=1, source_target_pairs={{0,16},{16,0},{1,17},{17,1},{2,18},{18,2},{3,19},{19,3},{4,20},{20... | collective-permute-start | bytes 1228808 | tf_op jit(solution)/shard_map/ppermute | solution.py:395
  29.3 15.3 %collective-permute-start.1 = (bf16[2400,128]{1,0:T(8,128)(2,1)}, bf16[2400,128]{1,0:T(8,128)(2,1)}, u32[]{:S(2)}, u32[]{:S(2)}) collective-permute-start(bf16[2400,128]{1,0:T(8,128)(2,1)} %fusion.9), channel_id=1, source_target_pairs={{0,16},{16,0},{1,17},{17,1},{2,18},{18,2},{3,19},{19,3},{4,20},{20... | collective-permute-start | bytes 1843208 | tf_op jit(solution)/shard_map/ppermute | solution.py:395
  47.6 38.0 %all-to-all-start = ((bf16[16,3,128,128]{3,2,1,0:T(8,128)(2,1)}), bf16[16,3,128,128]{3,2,1,0:T(8,128)(2,1)}, u32[]{:S(2)}, u32[]{:S(2)}) async-start(bf16[16,3,128,128]{3,2,1,0:T(8,128)(2,1)} %pad_maximum_fusion.2), calls=%async_computation | async-start | bytes 3145728 | tf_op jit(solution)/shard_map/all_to_all | solution.py:404
  53.7 217.7 %all-gather.2.cloned.1.call-start = ((), (), s32[]{:S(2)}) async-start(), calls=%async_computation.9 | async-start | bytes 7241728 | tf_op jit(solution)/shard_map/all_gather | solution.py:457
  90.3 104.4 %collective-permute-start.6 = (bf16[3200,400]{0,1:T(8,128)(2,1)}, bf16[3200,400]{0,1:T(8,128)(2,1)}, u32[]{:S(2)}, u32[]{:S(2)}) collective-permute-start(bf16[3200,400]{0,1:T(8,128)(2,1)} %dynamic_slice.99), channel_id=1, source_target_pairs={{0,16},{16,0},{1,17},{17,1},{2,18},{18,2},{3,19},{19,3},{4,20},{20... | collective-permute-start | bytes 7680008 | tf_op jit(solution)/shard_map/ppermute | solution.py:395
  93.5 89.1 %copy-start.51 = (f32[6400]{0:T(1024)S(1)}, f32[6400]{0:T(1024)}, u32[]{:S(2)}) copy-start(f32[6400]{0:T(1024)} %param.29) | copy-start | bytes 76804
  93.5 86.2 %collective-permute-start.2 = (bf16[800,800]{0,1:T(8,128)(2,1)}, bf16[800,800]{0,1:T(8,128)(2,1)}, u32[]{:S(2)}, u32[]{:S(2)}) collective-permute-start(bf16[800,800]{0,1:T(8,128)(2,1)} %constant_dynamic-slice_fusion.14), channel_id=1, source_target_pairs={{0,16},{16,0},{1,17},{17,1},{2,18},{18,2},{3,19},{19,3},{4,20},{20... | collective-permute-start | bytes 3840008 | tf_op jit(solution)/shard_map/ppermute | solution.py:395
  107.5 85.5 %all-to-all-start.1 = ((bf16[16,128,128]{2,1,0:T(8,128)(2,1)}), bf16[16,128,128]{2,1,0:T(8,128)(2,1)}, u32[]{:S(2)}, u32[]{:S(2)}) async-start(bf16[16,128,128]{2,1,0:T(8,128)(2,1)} %get-tuple-element.60), calls=%async_computation.1 | async-start | bytes 1048576 | tf_op jit(solution)/shard_map/all_to_all | solution.py:404
  116.7 408.9 %reduce-scatter.8.cloned.1.call-start = ((), (), s32[]{:S(2)}) async-start(), calls=%async_computation.11 | async-start | bytes 3584000 | tf_op jit(solution)/shard_map/reduce_scatter | solution.py:536
  179.7 21.1 %collective-permute-start.3 = (bf16[800,800]{0,1:T(8,128)(2,1)}, bf16[800,800]{0,1:T(8,128)(2,1)}, u32[]{:S(2)}, u32[]{:S(2)}) collective-permute-start(bf16[800,800]{0,1:T(8,128)(2,1)} %collective-permute-done.2), channel_id=1, source_target_pairs={{0,1},{1,0},{2,3},{3,2},{4,5},{5,4},{6,7},{7,6},{8,9},{9,8},{10,11... | collective-permute-start | bytes 3840008 | tf_op jit(solution)/shard_map/ppermute | solution.py:398
  181.1 11.9 %collective-permute-start.5 = (bf16[1600,128]{1,0:T(8,128)(2,1)S(1)}, bf16[1600,128]{1,0:T(8,128)(2,1)S(1)}, u32[]{:S(2)}, u32[]{:S(2)}) collective-permute-start(bf16[1600,128]{1,0:T(8,128)(2,1)S(1)} %bitcast.147), channel_id=1, source_target_pairs={{0,16},{16,0},{1,17},{17,1},{2,18},{18,2},{3,19},{19,3},{4,20},{20... | collective-permute-start | bytes 1228808 | tf_op jit(solution)/shard_map/ppermute | solution.py:395
  194.7 33.7 %collective-permute-start.7 = (bf16[3200,400]{0,1:T(8,128)(2,1)}, bf16[3200,400]{0,1:T(8,128)(2,1)S(1)}, u32[]{:S(2)}, u32[]{:S(2)}) collective-permute-start(bf16[3200,400]{0,1:T(8,128)(2,1)} %collective-permute-done.6), channel_id=1, source_target_pairs={{0,1},{1,0},{2,3},{3,2},{4,5},{5,4},{6,7},{7,6},{8,9},{9,8},{10,11... | collective-permute-start | bytes 7680008 | tf_op jit(solution)/shard_map/ppermute | solution.py:398
  196.3 40.4 %collective-permute-start.11 = (bf16[1600,256]{1,0:T(8,128)(2,1)S(1)}, bf16[1600,256]{1,0:T(8,128)(2,1)S(1)}, u32[]{:S(2)}, u32[]{:S(2)}) collective-permute-start(bf16[1600,256]{1,0:T(8,128)(2,1)S(1)} %get-tuple-element.168.own), channel_id=1, source_target_pairs={{0,2},{1,3},{2,0},{3,1},{4,6},{5,7},{6,4},{7,5},{8,10},{9,11},{10,... | collective-permute-start | bytes 2457608 | tf_op jit(solution)/shard_map/ppermute | solution.py:401
  205.5 79.9 %copy-start.58 = (f32[128]{0:T(128)}, f32[128]{0:T(128)S(1)}, u32[]{:S(2)}) copy-start(f32[128]{0:T(128)S(1)} %add_rsqrt_fusion) | copy-start | bytes 1540
  206.0 11.6 %collective-permute-start.4 = (bf16[1600,128]{1,0:T(8,128)(2,1)S(1)}, bf16[1600,128]{1,0:T(8,128)(2,1)S(1)}, u32[]{:S(2)}, u32[]{:S(2)}) collective-permute-start(bf16[1600,128]{1,0:T(8,128)(2,1)S(1)} %add_convert_fusion.2), channel_id=1, source_target_pairs={{0,16},{16,0},{1,17},{17,1},{2,18},{18,2},{3,19},{19,3},{4,20},{20... | collective-permute-start | bytes 1228808 | tf_op jit(solution)/shard_map/ppermute | solution.py:395
  228.4 11.0 %collective-permute-start.9 = (bf16[2,2,1,400,256]{4,3,0,2,1:T(8,128)(2,1)}, bf16[2,2,1,400,256]{4,3,0,2,1:T(8,128)(2,1)}, u32[]{:S(2)}, u32[]{:S(2)}) collective-permute-start(bf16[2,2,1,400,256]{4,3,0,2,1:T(8,128)(2,1)} %copy.107), channel_id=1, source_target_pairs={{0,1},{1,0},{2,3},{3,2},{4,5},{5,4},{6,7},{7,6},{8,9},{9,8},{10,11... | collective-permute-start | bytes 2457608 | tf_op jit(solution)/shard_map/ppermute | solution.py:398
  238.2 25.2 %collective-permute-start.12 = (bf16[1600,512]{1,0:T(8,128)(2,1)}, bf16[1600,512]{1,0:T(8,128)(2,1)}, u32[]{:S(2)}, u32[]{:S(2)}) collective-permute-start(bf16[1600,512]{1,0:T(8,128)(2,1)} %pad_maximum_fusion), channel_id=1, source_target_pairs={{0,1},{1,0},{2,3},{3,2},{4,5},{5,4},{6,7},{7,6},{8,9},{9,8},{10,11... | collective-permute-start | bytes 4915208 | tf_op jit(solution)/shard_map/ppermute | solution.py:398
  242.0 21.4 %collective-permute-start.10 = (bf16[2,1,1,400,512]{4,3,0,2,1:T(8,128)(2,1)}, bf16[2,1,1,400,512]{4,3,0,2,1:T(8,128)(2,1)}, u32[]{:S(2)}, u32[]{:S(2)}) collective-permute-start(bf16[2,1,1,400,512]{4,3,0,2,1:T(8,128)(2,1)} %get-tuple-element.143), channel_id=1, source_target_pairs={{0,2},{1,3},{2,0},{3,1},{4,6},{5,7},{6,4},{7,5},{8,10},{9,11},{10,... | collective-permute-start | bytes 2457608 | tf_op jit(solution)/shard_map/ppermute | solution.py:401
  243.5 36.9 %collective-permute-start.30 = (bf16[1600,256]{1,0:T(8,128)(2,1)}, bf16[1600,256]{1,0:T(8,128)(2,1)}, u32[]{:S(2)}, u32[]{:S(2)}) collective-permute-start(bf16[1600,256]{1,0:T(8,128)(2,1)} %pad_maximum_fusion.6.own), channel_id=1, source_target_pairs={{0,2},{1,3},{2,0},{3,1},{4,6},{5,7},{6,4},{7,5},{8,10},{9,11},{10,... | collective-permute-start | bytes 2457608 | tf_op jit(solution)/shard_map/ppermute | solution.py:401
  245.0 37.9 %collective-permute-start.8 = (bf16[1600,128]{1,0:T(8,128)(2,1)}, bf16[1600,128]{1,0:T(8,128)(2,1)}, u32[]{:S(2)}, u32[]{:S(2)}) collective-permute-start(bf16[1600,128]{1,0:T(8,128)(2,1)} %slice.335), channel_id=1, source_target_pairs={{0,16},{16,0},{1,17},{17,1},{2,18},{18,2},{3,19},{19,3},{4,20},{20... | collective-permute-start | bytes 1228808 | tf_op jit(solution)/shard_map/ppermute | solution.py:395
  274.8 25.6 %collective-permute-start.28 = (bf16[2,2,1,400,256]{4,3,0,2,1:T(8,128)(2,1)}, bf16[2,2,1,400,256]{4,3,0,2,1:T(8,128)(2,1)}, u32[]{:S(2)}, u32[]{:S(2)}) collective-permute-start(bf16[2,2,1,400,256]{4,3,0,2,1:T(8,128)(2,1)} %copy.109), channel_id=1, source_target_pairs={{0,1},{1,0},{2,3},{3,2},{4,5},{5,4},{6,7},{7,6},{8,9},{9,8},{10,11... | collective-permute-start | bytes 2457608 | tf_op jit(solution)/shard_map/ppermute | solution.py:398
  282.9 69.1 %collective-permute-start.31 = (bf16[1600,512]{1,0:T(8,128)(2,1)}, bf16[1600,512]{1,0:T(8,128)(2,1)}, u32[]{:S(2)}, u32[]{:S(2)}) collective-permute-start(bf16[1600,512]{1,0:T(8,128)(2,1)} %pad_maximum_fusion.1), channel_id=1, source_target_pairs={{0,1},{1,0},{2,3},{3,2},{4,5},{5,4},{6,7},{7,6},{8,9},{9,8},{10,11... | collective-permute-start | bytes 4915208 | tf_op jit(solution)/shard_map/ppermute | solution.py:398
  293.7 29.7 %all-to-all-start.2 = ((bf16[16,128,128]{2,1,0:T(8,128)(2,1)}), bf16[16,128,128]{2,1,0:T(8,128)(2,1)}, u32[]{:S(2)}, u32[]{:S(2)}) async-start(bf16[16,128,128]{2,1,0:T(8,128)(2,1)} %bitcast.14), calls=%async_computation.2 | async-start | bytes 1048576 | tf_op jit(solution)/shard_map/all_to_all | solution.py:404
  302.7 49.3 %collective-permute-start.29 = (bf16[2,1,1,400,512]{4,3,0,2,1:T(8,128)(2,1)S(1)}, bf16[2,1,1,400,512]{4,3,0,2,1:T(8,128)(2,1)S(1)}, u32[]{:S(2)}, u32[]{:S(2)}) collective-permute-start(bf16[2,1,1,400,512]{4,3,0,2,1:T(8,128)(2,1)S(1)} %get-tuple-element.139), channel_id=1, source_target_pairs={{0,2},{1,3},{2,0},{3,1},{4,6},{5,7},{6,4},{7,5},{8,10},{9,11},{10,... | collective-permute-start | bytes 2457608 | tf_op jit(solution)/shard_map/ppermute | solution.py:401
  341.2 85.4 %all-to-all-start.3 = ((bf16[16,3,128,128]{3,2,1,0:T(8,128)(2,1)}), bf16[16,3,128,128]{3,2,1,0:T(8,128)(2,1)}, u32[]{:S(2)}, u32[]{:S(2)}) async-start(bf16[16,3,128,128]{3,2,1,0:T(8,128)(2,1)} %attb.1), calls=%async_computation.3 | async-start | bytes 3145728 | tf_op jit(solution)/shard_map/all_to_all | solution.py:404
  351.8 176.9 %reduce-scatter.6.cloned.1.call-start = ((), (), s32[]{:S(2)}) async-start(), calls=%async_computation.10 | async-start | bytes 3584000 | tf_op jit(solution)/shard_map/reduce_scatter | solution.py:536
  364.7 34.6 %collective-permute-start.32 = (bf16[800,896]{1,0:T(8,128)(2,1)}, bf16[800,896]{1,0:T(8,128)(2,1)}, u32[]{:S(2)}, u32[]{:S(2)}) collective-permute-start(bf16[800,896]{1,0:T(8,128)(2,1)} %get-tuple-element.138), channel_id=1, source_target_pairs={{0,16},{16,0},{1,17},{17,1},{2,18},{18,2},{3,19},{19,3},{4,20},{20... | collective-permute-start | bytes 4300808 | tf_op jit(solution)/shard_map/ppermute | solution.py:395
  367.8 63.3 %collective-permute-start.22 = (bf16[1600,128]{1,0:T(8,128)(2,1)S(1)}, bf16[1600,128]{1,0:T(8,128)(2,1)}, u32[]{:S(2)}, u32[]{:S(2)}) collective-permute-start(bf16[1600,128]{1,0:T(8,128)(2,1)S(1)} %copy-done.19), channel_id=1, source_target_pairs={{0,16},{16,0},{1,17},{17,1},{2,18},{18,2},{3,19},{19,3},{4,20},{20... | collective-permute-start | bytes 1228808 | tf_op jit(solution)/shard_map/ppermute | solution.py:395
  368.1 68.8 %collective-permute-start.24 = (bf16[800,128]{1,0:T(8,128)(2,1)}, bf16[800,128]{1,0:T(8,128)(2,1)}, u32[]{:S(2)}, u32[]{:S(2)}) collective-permute-start(bf16[800,128]{1,0:T(8,128)(2,1)} %get-tuple-element.171), channel_id=1, source_target_pairs={{0,16},{16,0},{1,17},{17,1},{2,18},{18,2},{3,19},{19,3},{4,20},{20... | collective-permute-start | bytes 614408 | tf_op jit(solution)/shard_map/ppermute | solution.py:395
  376.7 48.4 %collective-permute-start.16 = (bf16[3,128,800]{1,2,0:T(8,128)(2,1)S(1)}, bf16[3,128,800]{1,2,0:T(8,128)(2,1)}, u32[]{:S(2)}, u32[]{:S(2)}) collective-permute-start(bf16[3,128,800]{1,2,0:T(8,128)(2,1)S(1)} %dynamic-slice_convert_fusion), channel_id=1, source_target_pairs={{0,16},{16,0},{1,17},{17,1},{2,18},{18,2},{3,19},{19,3},{4,20},{20... | collective-permute-start | bytes 1843208 | tf_op jit(solution)/shard_map/ppermute | solution.py:395
  429.4 15.6 %collective-permute-start.13 = (bf16[2400,128]{1,0:T(8,128)(2,1)}, bf16[2400,128]{1,0:T(8,128)(2,1)}, u32[]{:S(2)}, u32[]{:S(2)}) collective-permute-start(bf16[2400,128]{1,0:T(8,128)(2,1)} %get-tuple-element.151), channel_id=1, source_target_pairs={{0,16},{16,0},{1,17},{17,1},{2,18},{18,2},{3,19},{19,3},{4,20},{20... | collective-permute-start | bytes 1843208 | tf_op jit(solution)/shard_map/ppermute | solution.py:395
  435.3 5.0 collective-permute-start.23
  438.7 29.2 %collective-permute-start.25 = (bf16[800,256]{1,0:T(8,128)(2,1)}, bf16[800,256]{1,0:T(8,128)(2,1)}, u32[]{:S(2)}, u32[]{:S(2)}) collective-permute-start(bf16[800,256]{1,0:T(8,128)(2,1)} %pad_maximum_fusion.9), channel_id=1, source_target_pairs={{0,2},{1,3},{2,0},{3,1},{4,6},{5,7},{6,4},{7,5},{8,10},{9,11},{10,... | collective-permute-start | bytes 1228808 | tf_op jit(solution)/shard_map/ppermute | solution.py:401
  442.2 31.3 %collective-permute-start.27 = (bf16[4,1,1,100,512]{4,3,2,1,0:T(8,128)(2,1)}, bf16[4,1,1,100,512]{4,3,2,1,0:T(8,128)(2,1)}, u32[]{:S(2)}, u32[]{:S(2)}) collective-permute-start(bf16[4,1,1,100,512]{4,3,2,1,0:T(8,128)(2,1)} %get-tuple-element.160), channel_id=1, source_target_pairs={{0,2},{1,3},{2,0},{3,1},{4,6},{5,7},{6,4},{7,5},{8,10},{9,11},{10,... | collective-permute-start | bytes 1228808 | tf_op jit(solution)/shard_map/ppermute | solution.py:401
  451.6 27.2 %collective-permute-start.14 = (bf16[1600,128]{1,0:T(8,128)(2,1)}, bf16[1600,128]{1,0:T(8,128)(2,1)S(1)}, u32[]{:S(2)}, u32[]{:S(2)}) collective-permute-start(bf16[1600,128]{1,0:T(8,128)(2,1)} %slice.334), channel_id=1, source_target_pairs={{0,16},{16,0},{1,17},{17,1},{2,18},{18,2},{3,19},{19,3},{4,20},{20... | collective-permute-start | bytes 1228808 | tf_op jit(solution)/shard_map/ppermute | solution.py:395
  454.3 47.0 %collective-permute-start.21 = (bf16[128,800]{1,0:T(8,128)(2,1)}, bf16[128,800]{1,0:T(8,128)(2,1)}, u32[]{:S(2)}, u32[]{:S(2)}) collective-permute-start(bf16[128,800]{1,0:T(8,128)(2,1)} %get-tuple-element.155), channel_id=1, source_target_pairs={{3,12},{7,14},{10,15},{19,28},{23,30},{26,31}} | collective-permute-start | bytes 614408 | tf_op jit(solution)/shard_map/ppermute | solution.py:646
  455.7 45.8 %collective-permute-start.20 = (bf16[128,800]{1,0:T(8,128)(2,1)}, bf16[128,800]{1,0:T(8,128)(2,1)}, u32[]{:S(2)}, u32[]{:S(2)}) collective-permute-start(bf16[128,800]{1,0:T(8,128)(2,1)} %get-tuple-element.156), channel_id=1, source_target_pairs={{0,10},{1,5},{2,6},{3,11},{4,12},{5,7},{6,2},{7,13},{8,9},{9,4},{1... | collective-permute-start | bytes 614408 | tf_op jit(solution)/shard_map/ppermute | solution.py:646
  462.7 30.9 %all-to-all-start.4 = ((f32[32,4,128]{2,1,0:T(4,128)}), f32[32,4,128]{2,1,0:T(4,128)S(1)}, u32[]{:S(2)}, u32[]{:S(2)}) async-start(f32[32,4,128]{2,1,0:T(4,128)} %bitcast.27), calls=%async_computation.4 | async-start | bytes 131072 | tf_op jit(solution)/shard_map/all_to_all | solution.py:670
  467.9 35.2 %collective-permute-start.19 = (bf16[128,800]{1,0:T(8,128)(2,1)}, bf16[128,800]{1,0:T(8,128)(2,1)}, u32[]{:S(2)}, u32[]{:S(2)}) collective-permute-start(bf16[128,800]{1,0:T(8,128)(2,1)} %get-tuple-element.157), channel_id=1, source_target_pairs={{0,5},{1,0},{2,11},{3,1},{4,7},{5,2},{6,13},{7,8},{8,14},{9,3},{10... | collective-permute-start | bytes 614408 | tf_op jit(solution)/shard_map/ppermute | solution.py:646
  473.5 29.6 %collective-permute-start.18 = (bf16[128,800]{1,0:T(8,128)(2,1)}, bf16[128,800]{1,0:T(8,128)(2,1)}, u32[]{:S(2)}, u32[]{:S(2)}) collective-permute-start(bf16[128,800]{1,0:T(8,128)(2,1)} %get-tuple-element.158), channel_id=1, source_target_pairs={{0,0},{1,11},{2,1},{3,6},{4,2},{5,13},{6,7},{7,3},{8,8},{9,14},{10... | collective-permute-start | bytes 614408 | tf_op jit(solution)/shard_map/ppermute | solution.py:646
  478.9 24.3 %collective-permute-start.17 = (bf16[128,800]{1,0:T(8,128)(2,1)}, bf16[128,800]{1,0:T(8,128)(2,1)}, u32[]{:S(2)}, u32[]{:S(2)}) collective-permute-start(bf16[128,800]{1,0:T(8,128)(2,1)} %get-tuple-element.154), channel_id=1, source_target_pairs={{0,11},{1,6},{2,0},{3,7},{4,1},{5,12},{6,8},{7,2},{8,3},{9,9},{10,... | collective-permute-start | bytes 614408 | tf_op jit(solution)/shard_map/ppermute | solution.py:646
  496.5 26.3 %all-to-all-start.5 = ((f32[32,31,128]{2,1,0:T(8,128)}), f32[32,31,128]{2,1,0:T(8,128)}, u32[]{:S(2)}, u32[]{:S(2)}) async-start(f32[32,31,128]{2,1,0:T(8,128)} %broadcast_in_dim.101), calls=%async_computation.5 | async-start | bytes 1048576 | tf_op jit(solution)/shard_map/all_to_all | solution.py:670
  501.2 68.9 %reduce-scatter.10.cloned.1.call-start = ((), (), s32[]{:S(2)}) async-start(), calls=%async_computation.12 | async-start | bytes 931840
  501.3 9.4 %collective-permute-start.26 = (bf16[800,512]{1,0:T(8,128)(2,1)}, bf16[800,512]{1,0:T(8,128)(2,1)S(1)}, u32[]{:S(2)}, u32[]{:S(2)}) collective-permute-start(bf16[800,512]{1,0:T(8,128)(2,1)} %pad_maximum_fusion.8), channel_id=1, source_target_pairs={{0,1},{1,0},{2,3},{3,2},{4,5},{5,4},{6,7},{7,6},{8,9},{9,8},{10,11... | collective-permute-start | bytes 2457608 | tf_op jit(solution)/shard_map/ppermute | solution.py:398
  501.5 16.9 %collective-permute-start.15 = (bf16[1600,128]{1,0:T(8,128)(2,1)}, bf16[1600,128]{1,0:T(8,128)(2,1)}, u32[]{:S(2)}, u32[]{:S(2)}) collective-permute-start(bf16[1600,128]{1,0:T(8,128)(2,1)} %slice.333), channel_id=1, source_target_pairs={{0,16},{16,0},{1,17},{17,1},{2,18},{18,2},{3,19},{19,3},{4,20},{20... | collective-permute-start | bytes 1228808 | tf_op jit(solution)/shard_map/ppermute | solution.py:395
  525.6 46.2 %collective-permute-start.33 = (bf16[400,800]{1,0:T(8,128)(2,1)}, bf16[400,800]{1,0:T(8,128)(2,1)S(1)}, u32[]{:S(2)}, u32[]{:S(2)}) collective-permute-start(bf16[400,800]{1,0:T(8,128)(2,1)} %bitcast.178), channel_id=1, source_target_pairs={{0,0},{1,1},{2,2},{3,3},{4,4},{5,5},{6,6},{7,7},{8,16},{9,17},{10,... | collective-permute-start | bytes 1920008 | tf_op jit(solution)/shard_map/ppermute | solution.py:576
  528.7 44.3 %copy-start.1 = (bf16[1600,800]{0,1:T(8,128)(2,1)S(1)}, bf16[1600,800]{0,1:T(8,128)(2,1)}, u32[]{:S(2)}) copy-start(bf16[1600,800]{0,1:T(8,128)(2,1)} %param.24) | copy-start | bytes 7680004
  (71 other events, 467.4 us)
Sparse Core Ops, SparseCore 0:
  85.8 75.3 all-gather.1
  271.6 66.3 reduce-scatter.7
  403.8 57.6 reduce-scatter.5
  516.8 53.2 reduce-scatter.9

commit v4 on v3

--- a/solution.py
+++ b/solution.py
@@ -280,9 +280,10 @@
     )(order, natural, out_rows, log_rows, grad_slots)
 
 
-def product_kernel(flip, kept, got, own, side, core, parts):
+def product_kernel(flip, kept, got, own, side, core, *parts):
     units, tokens = kept.shape[0], own.shape[1]
-    halves, _, width = parts.shape
+    halves = 2
+    width = parts[0].shape[-1]
     block = own.shape[0] // halves
     pairs = (
         (kept, 0, own, 0),
@@ -300,24 +301,35 @@
                 rows = pl.ds(pl.multiple_of((half ^ flip[0]) * block, 16), block)
                 b = right[rows, right_at : right_at + tokens]
                 total = total + dot(a, b, ((1,), (1,)))
-            parts[half, first : first + step, :block] = total.astype(BF16)
+            total = total.astype(BF16)
             if width > block:
-                blank = jnp.zeros((step, width - block), BF16)
-                parts[half, first : first + step, block:] = blank
+                total = jnp.concatenate([total, jnp.zeros((step, width - block), BF16)], axis=1)
+            if len(parts) == 1:
+                parts[0][half, first : first + step] = total
+            else:
+                for index, part in enumerate(parts):
+
+                    @pl.when(half == index)
+                    def _(part=part):
+                        part[first : first + step] = total
+
         return carry
 
     lax.fori_loop(0, halves, one_half, 0)
 
 
-def tokens_product(units, rows, flip):
+def tokens_product(units, rows, flip, apart):
     kept, got = units
     own, side, core = rows
     width = own.shape[0] // 2
+    whole = (2, kept.shape[0], width + -width % 128)
     return pl.pallas_call(
         product_kernel,
         in_specs=[pl.BlockSpec(memory_space=pltpu.SMEM)] + in_vmem(5),
-        out_specs=in_vmem(1)[0],
-        out_shape=jax.ShapeDtypeStruct((2, kept.shape[0], width + -width % 128), BF16),
+        out_specs=in_vmem(2) if apart else in_vmem(1)[0],
+        out_shape=[jax.ShapeDtypeStruct(whole[1:], BF16)] * 2
+        if apart
+        else jax.ShapeDtypeStruct(whole, BF16),
         name="prod",
     )(jnp.full((1,), flip, jnp.int32), kept, got, own, side, core)
 
@@ -433,6 +445,7 @@
     gain_one, bias_one = column(ln1_gain), column(ln1_bias)
     hidden_one = (normed_one * gain_one + bias_one).astype(BF16)
     hidden_one_other = (normalize(other_in.astype(F32))[0] * gain_one + bias_one).astype(BF16)
+    hidden_one_other = lax.optimization_barrier(hidden_one_other)
     proj_bias = jnp.concatenate([qv_bias[0], jnp.zeros_like(qv_bias[0]), qv_bias[1]])
     proj_bias = column(pick(proj_bias, my_dp, 0))
     proj_other = (dot32(w_qkv, hidden_one_other, "de,dt->et") + proj_bias).astype(BF16)
@@ -543,11 +556,11 @@
     out_grad_all = plane_rows(out_grad_early, (two_send,))
 
     units = (flat(active_kept), flat(after(active_got, two_send)))
-    down_parts = tokens_product(units, out_grad_all, 0)
+    down_parts = tokens_product(units, out_grad_all, 0, False)
     down_parts = down_parts.reshape(planes, -1, down_parts.shape[2])
     hidden_two_all = plane_rows(hidden_two_pair, (two_send,))
     units = (flat(pre_kept), flat(after(pre_got, down_parts)))
-    up_kept, up_sent = tokens_product(units, hidden_two_all, my_dp)
+    up_kept, up_sent = tokens_product(units, hidden_two_all, my_dp, True)
     up_got = across(up_sent)
 
     line_ready = after(down_parts, hidden_one_all)
@@ -608,16 +621,25 @@
         out_part += dot32(units[:, at * step : (at + 1) * step], rows, "ct,dt->cd")
     out_part = out_part.astype(BF16)
     out_part = out_part.reshape(planes, size, half_cols)
-    out_part = jnp.pad(out_part, ((0, 0), (0, -size % 8), (0, -half_cols % 128)))
-    out_sums = line_sum(after(out_part, up_parts))[:size, :half_cols]
+    my_plane = my_ctx // 4
+    if planes > 4:
+        out_part = jnp.pad(out_part, ((0, 0), (0, -size % 8), (0, -half_cols % 128)))
+        out_sums = [line_sum(out_part)[:size, :half_cols]]
+    else:
+        out_sums = [lax.dynamic_index_in_dim(out_part, my_plane, 0, keepdims=False)]
+        for step in range(1, planes):
+            target = (my_plane + step) % planes
+            piece = lax.dynamic_index_in_dim(out_part, target, 0, keepdims=False)
+            pairs = [(k, (k + 4 * step) % ctx) for k in range(ctx)]
+            out_sums.append(lax.ppermute(piece, "ctx", pairs))
 
     qkv_part = dot32(
-        proj_slots, hidden_one_all.reshape(ctx, tokens, width), "sklt,std->kld"
-    )
-    qkv_kept, qkv_send = split(qkv_part, my_dp, 2)
+        proj_slots, hidden_one_all.reshape(ctx, tokens, width), "sklt,std->dkl"
+    )
+    qkv_kept, qkv_send = split(qkv_part, my_dp, 0)
     qkv_send = qkv_send.astype(BF16)
-    qkv_sums = qkv_kept + across(qkv_send).astype(F32)
-    qkv_sums = qkv_sums.astype(BF16)
+    qkv_got = across(qkv_send)
+    qkv_sums = (qkv_kept + qkv_got.astype(F32)).astype(BF16)
     block = 2 * half_proj // ctx
     edges = []
     for source in range(ctx):
@@ -635,12 +657,15 @@
             kinds[number][source] = kind
             offsets[number][target] = kind * width + source * lanes - target * block
     mine = jnp.arange(ctx, dtype=jnp.int32)[None, :] == my_ctx
-    kinds = jnp.sum(jnp.where(mine, jnp.asarray(kinds, jnp.int32), 0), axis=1)[:, None, None]
+    kinds = jnp.sum(jnp.where(mine, jnp.asarray(kinds, jnp.int32), 0), axis=1)
     offsets = jnp.sum(jnp.where(mine, jnp.asarray(offsets, jnp.int32), 0), axis=1)
-    place = offsets[:, None] + jnp.arange(lanes, dtype=jnp.int32)[None, :]
-    targets = jnp.arange(block, dtype=jnp.int32)[:, None]
-    chosen = (targets == place.reshape(1, -1)).astype(BF16)
-    pieces = jnp.where(kinds == 0, qkv_sums[:1], jnp.where(kinds == 1, qkv_sums[1:2], qkv_sums[2:]))
+    place = offsets[:, None, None] + jnp.arange(lanes, dtype=jnp.int32)[None, :, None]
+    targets = jnp.arange(block, dtype=jnp.int32)[None, None, :]
+    chosen = (targets == place).astype(BF16)
+    pieces = [
+        jnp.where(kind == 0, qkv_sums[:, 0], jnp.where(kind == 1, qkv_sums[:, 1], qkv_sums[:, 2]))
+        for kind in kinds
+    ]
     received = []
     for number, edges_now in enumerate(rounds):
         piece = lax.ppermute(pieces[number], "ctx", [edge[:2] for edge in edges_now])
@@ -676,11 +701,11 @@
             first += item.shape[0]
 
     early = middle_sums[:4] + [at_dp(middle_sums[4])]
-    packed = after(jnp.concatenate(early), proj_back)
+    packed = after(jnp.concatenate(early), grad_slots)
     size = -(-packed.shape[0] // (devices * 128)) * 128
     packed = jnp.pad(packed, (0, devices * size - packed.shape[0]))
     mine = everywhere(packed.reshape(devices, size // 128, 128))
-    mine = jnp.sum(after(mine, grad_one_got), axis=0).reshape(-1)
+    mine = jnp.sum(mine, axis=0).reshape(-1)
     head_sums = jnp.sum(proj_slots.astype(F32), axis=(0, 3))
     late = [jnp.sum(grad_hidden_one * normed_one, axis=1), jnp.sum(grad_hidden_one, axis=1)]
     packed = jnp.concatenate([mine, head_sums[0], head_sums[2]] + late)
@@ -689,16 +714,15 @@
     totals = everywhere(packed).reshape(devices, -1)
     pieces_in = [after(piece, packed) for piece in received]
     qkv_grad = sum(
-        dot32(chosen[:, i * lanes : (i + 1) * lanes], piece, "cr,rd->cd")
-        for i, piece in enumerate(pieces_in)
-    ).T
+        dot32(piece, chosen[i], "dr,rc->dc") for i, piece in enumerate(pieces_in)
+    )
     pieces = list(pieces_of(totals[:, :size].reshape(-1), early))
     head_sums = totals[:, size : size + 2 * lanes].reshape(2, ctx, 2, lanes)
     head_sums = jnp.transpose(jnp.sum(head_sums, axis=0), (1, 0, 2)).reshape(2, -1)[:, :width]
     ln1 = list(pieces_of(jnp.sum(totals[:, size + 2 * lanes :], axis=0), late))
     up_grad = after(up_sums, totals)[:, :half_cols].astype(F32).T
     down_grad = after(down_grad, totals).astype(F32)
-    out_weight_grad = after(out_sums, totals).astype(F32)
+    out_weight_grad = sum(after(piece, totals).astype(F32) for piece in out_sums)
 
     return (
         layer_out.reshape(layer_in.shape),

time: 589 us -> 567 us (0.963)
  the two profiles are of different devices: /device:TPU:0 before, /device:TPU:25 now
where the time goes in v4:
time: 567 us; the launch traced here: 557 us
  waiting for transfers between devices  218 us (38%)
  starting transfers between devices  94.5 us (17%)
  matrix products  81.2 us (14%)
  local copies, waits for them, and re-layouts  52 us (9%)
  Pallas kernels  48 us (8%)
  other arithmetic  41.1 us (7%)
  between operations  22.2 us (4%)
    ppermute x14, waiting for transfers between devices, across(): return lax.ppermute(x, 'dp', [(0, 1), (1, 0)])  117 us
    dot_general x27, matrix products, dot32(): return jnp.einsum(spec, a, b, preferred_element_type=F32)  81.2 us
    all_to_all x4, waiting for transfers between devices, exchange(): return lax.all_to_all(x, 'ctx', 0, 0, tiled=True)  51 us
    ppermute x1, waiting for transfers between devices, shards(): down_grad = lax.ppermute(after(down_sums, proj_slots), ('dp', 'ctx'), owner)  30.2 us
    all_to_all x4, starting transfers between devices, exchange(): return lax.all_to_all(x, 'ctx', 0, 0, tiled=True)  28.3 us
    all_to_all x2, starting transfers between devices, everywhere(): return lax.all_to_all(packed, ('dp', 'ctx'), 0, 0, tiled=True)  22.6 us
    ppermute x6, waiting for transfers between devices, to_side(): return lax.ppermute(x, 'ctx', side_swap)  18.8 us
    pallas_call x1, Pallas kernels, attend_backward(): pl.pallas_call(partial(backward_kernel, tokens // seqs // 2, block, head_...  17.8 us
  transfers between devices with their start and end apart: 46, of which 14 were waited for; matrix products, arithmetic and copies ran while one was open for 27% of the time, Pallas kernels for 9%

profile of v4, /device:TPU:25, one launch (start us, length us, event | category | flops | bytes accessed | tf_op | source)
XLA Modules:
  0.0 556.7 jit_solution(8193054397068569712)
XLA Ops:
  11.4 7.7 %collective-permute-done = bf16[1600,128]{1,0:T(8,128)(2,1)S(1)} collective-permute-done((bf16[1600,128]{1,0:T(8,128)(2,1)S(1)}, bf16[1600,128]{1,0:T(8,128)(2,1)S(1)}, u32[]{:S(2)}, u32[]{:S(2)}) %collective-permute-start) | collective-permute-done | bytes 409632 | tf_op jit(solution)/shard_map/ppermute | solution.py:407
  20.0 7.3 %fusion.9 = bf16[2400,128]{1,0:T(8,128)(2,1)} fusion(bf16[1600,128]{1,0:T(8,128)(2,1)S(1)} %fusion.46, bf16[1600,2400]{1,0:T(8,128)(2,1)} %param.22, f32[2400]{0:T(1024)S(1)} %dynamic_slice.105), kind=kOutput, calls=%fused_computation.16 | convolution fusion | flops 983654400 | bytes 8713600 | tf_op jit(solution)/shard_map/de,dt->et/dot_general | solution.py:436
  28.5 6.8 %fusion.10 = bf16[2400,128]{1,0:T(8,128)(2,1)S(1)} fusion(bf16[1600,2400]{1,0:T(8,128)(2,1)} %param.22, f32[2400]{0:T(1024)S(1)} %dynamic_slice.105, f32[1600]{0:T(1024)S(1)} %copy-done.53, f32[1600]{0:T(1024)S(1)} %copy-done.50, f32[128]{0:T(128)S(1)} %add_rsqrt_fusion.2, f32[128]{0:T(128)S(1)} %broadcast_multiply_fusion.6, bf16[128,1600]{0,1:T(8,128)(2,1)S(1)} %copy.88), kind=kOutput, calls=%fused_computation.17 | convolution fusion | flops 984883200 | bytes 8727424 | tf_op jit(solution)/shard_map/de,dt->et/dot_general | solution.py:436
  35.4 6.1 %collective-permute-done.1 = bf16[2400,128]{1,0:T(8,128)(2,1)} collective-permute-done((bf16[2400,128]{1,0:T(8,128)(2,1)}, bf16[2400,128]{1,0:T(8,128)(2,1)}, u32[]{:S(2)}, u32[]{:S(2)}) %collective-permute-start.1) | collective-permute-done | bytes 614432 | tf_op jit(solution)/shard_map/ppermute | solution.py:407
  44.5 8.2 %all-to-all-start = ((bf16[16,3,128,128]{3,2,1,0:T(8,128)(2,1)}), bf16[16,3,128,128]{3,2,1,0:T(8,128)(2,1)}, u32[]{:S(2)}, u32[]{:S(2)}) async-start(bf16[16,3,128,128]{3,2,1,0:T(8,128)(2,1)} %pad_maximum_fusion.2), calls=%async_computation | async-start | bytes 3145728 | tf_op jit(solution)/shard_map/all_to_all | solution.py:416
  54.1 32.4 %all-to-all-done.qkv = bf16[16,3,128,128]{3,2,1,0:T(8,128)(2,1)} async-done(((bf16[16,3,128,128]{3,2,1,0:T(8,128)(2,1)}), bf16[16,3,128,128]{3,2,1,0:T(8,128)(2,1)}, u32[]{:S(2)}, u32[]{:S(2)}) %all-to-all-start) | async-done | bytes 1572896 | tf_op jit(solution)/shard_map/all_to_all | solution.py:416
  86.5 4.6 dynamic_slice.112
  94.3 13.4 %attf.1 = (bf16[16,128,128]{2,1,0:T(8,128)(2,1)}, bf16[3,2,1024,128]{3,2,1,0:T(8,128)(2,1)}, bf16[2,1024,128]{2,1,0:T(8,128)(2,1)}, f32[2,1024,128]{2,1,0:T(8,128)}) custom-call(s32[2,32]{1,0:T(2,128)} %order.3, bf16[16,3,128,128]{3,2,1,0:T(8,128)(2,1)} %all-to-all-done.qkv), custom_call_target="tpu_custom_call" | custom-call | tf_op jit(solution)/shard_map/attf/pallas_call | solution.py:252
  107.8 7.9 %all-to-all-start.1 = ((bf16[16,128,128]{2,1,0:T(8,128)(2,1)}), bf16[16,128,128]{2,1,0:T(8,128)(2,1)}, u32[]{:S(2)}, u32[]{:S(2)}) async-start(bf16[16,128,128]{2,1,0:T(8,128)(2,1)} %get-tuple-element.63), calls=%async_computation.1 | async-start | bytes 1048576 | tf_op jit(solution)/shard_map/all_to_all | solution.py:416
  116.0 63.7 %collective-permute-done.2 = bf16[800,800]{0,1:T(8,128)(2,1)} collective-permute-done((bf16[800,800]{0,1:T(8,128)(2,1)}, bf16[800,800]{0,1:T(8,128)(2,1)}, u32[]{:S(2)}, u32[]{:S(2)}) %collective-permute-start.2) | collective-permute-done | bytes 1280032 | tf_op jit(solution)/shard_map/ppermute | solution.py:407
  182.8 9.6 %collective-permute-done.5 = bf16[1600,128]{1,0:T(8,128)(2,1)S(1)} collective-permute-done((bf16[1600,128]{1,0:T(8,128)(2,1)S(1)}, bf16[1600,128]{1,0:T(8,128)(2,1)S(1)}, u32[]{:S(2)}, u32[]{:S(2)}) %collective-permute-start.5) | collective-permute-done | bytes 409632 | tf_op jit(solution)/shard_map/ppermute | solution.py:407
  196.7 2.8 collective-permute-start.11
  207.8 4.4 fusion.5
  212.2 2.9 convolution_add_fusion.1
  215.1 2.2 collective-permute-done.4
  217.3 8.4 %multiply_convert_fusion = (bf16[3200,256]{1,0:T(8,128)(2,1)S(1)}, f32[3200,256]{1,0:T(8,128)S(1)}) fusion(f32[3200]{0:T(1024)S(1)} %dynamic_slice.110, bf16[1600,3200]{1,0:T(8,128)(2,1)} %param.28, bf16[1600,128]{1,0:T(8,128)(2,1)S(1)} %collective-permute-done.4, bf16[1600,128]{1,0:T(8,128)(2,1)S(1)} %add_convert_fusion.2), kind=kOutput, calls=%fused_computation.24 | convolution fusion | flops 2631270400 | bytes 15987200 | tf_op jit(solution)/shard_map/df,dt->ft/dot_general | solution.py:436
  229.2 4.1 convert_reduce_fusion
  233.4 3.1 convolution_bitcast_fusion.1
  246.1 15.7 %collective-permute-done.10 = bf16[2,1,1,400,512]{4,3,0,2,1:T(8,128)(2,1)S(1)} collective-permute-done((bf16[2,1,1,400,512]{4,3,0,2,1:T(8,128)(2,1)S(1)}, bf16[2,1,1,400,512]{4,3,0,2,1:T(8,128)(2,1)S(1)}, u32[]{:S(2)}, u32[]{:S(2)}) %collective-permute-start.10) | collective-permute-done | bytes 819232 | tf_op jit(solution)/shard_map/ppermute | solution.py:413
  262.7 8.0 %prod.2 = bf16[2,800,896]{2,1,0:T(8,128)(2,1)} custom-call(s32[1]{0:T(128)} %constant.165.clone.1.flip, bf16[800,512]{1,0:T(8,128)(2,1)} %bitcast.174, bf16[800,512]{1,0:T(8,128)(2,1)} %bitcast.188, bf16[1600,256]{1,0:T(8,128)(2,1)} %copy-done.22, bf16[1600,256]{1,0:T(8,128)(2,1)} %copy-done.23, bf16[1600,512]{1,0:T(8,128)(2,1)} %collective-permute-done.12.core), custom_call_target="tpu_custom_call" | custom-call | tf_op jit(solution)/shard_map/prod/pallas_call | solution.py:326
  270.8 2.4 constant_dynamic-slice_fusion.2
  274.1 2.2 collective-permute-start.31
  276.4 3.1 collective-permute-done.33.side
  288.5 6.0 %all-to-all-start.2 = ((bf16[16,128,128]{2,1,0:T(8,128)(2,1)}), bf16[16,128,128]{2,1,0:T(8,128)(2,1)}, u32[]{:S(2)}, u32[]{:S(2)}) async-start(bf16[16,128,128]{2,1,0:T(8,128)(2,1)} %bitcast.14), calls=%async_computation.2 | async-start | bytes 1048576 | tf_op jit(solution)/shard_map/all_to_all | solution.py:416
  294.6 2.5 pad_maximum_fusion.1
  301.2 18.6 %all-to-all-done.2.grad_slots = bf16[16,128,128]{2,1,0:T(8,128)(2,1)} async-done(((bf16[16,128,128]{2,1,0:T(8,128)(2,1)}), bf16[16,128,128]{2,1,0:T(8,128)(2,1)}, u32[]{:S(2)}, u32[]{:S(2)}) %all-to-all-start.2) | async-done | bytes 524320 | tf_op jit(solution)/shard_map/all_to_all | solution.py:416
  320.5 8.9 %all-to-all-start.4 = ((f32[32,4,128]{2,1,0:T(4,128)}), f32[32,4,128]{2,1,0:T(4,128)S(1)}, u32[]{:S(2)}, u32[]{:S(2)}) async-start(f32[32,4,128]{2,1,0:T(4,128)} %bitcast.27), calls=%async_computation.4 | async-start | bytes 131072 | tf_op jit(solution)/shard_map/all_to_all | solution.py:695
  329.3 17.8 %attb.1 = bf16[16,3,128,128]{3,2,1,0:T(8,128)(2,1)} custom-call(s32[2,32]{1,0:T(2,128)} %order.3, bf16[3,2,1024,128]{3,2,1,0:T(8,128)(2,1)} %get-tuple-element.66.natural, bf16[2,1024,128]{2,1,0:T(8,128)(2,1)} %get-tuple-element.67.out_rows, f32[2,1024,128]{2,1,0:T(8,128)} %get-tuple-element.68.log_rows, bf16[16,128,128]{2,1,0:T(8,128)(2,1)} %all-to-all-done.2.grad_slots), custom_call_target="tpu_custom_call" | custom-call | tf_op jit(solution)/shard_map/attb/pallas_call | solution.py:270
  347.1 6.2 %all-to-all-start.3 = ((bf16[16,3,128,128]{3,2,1,0:T(8,128)(2,1)}), bf16[16,3,128,128]{3,2,1,0:T(8,128)(2,1)}, u32[]{:S(2)}, u32[]{:S(2)}) async-start(bf16[16,3,128,128]{3,2,1,0:T(8,128)(2,1)} %attb.1), calls=%async_computation.3 | async-start | bytes 3145728 | tf_op jit(solution)/shard_map/all_to_all | solution.py:416
  354.5 8.8 %prod.3 = (bf16[800,896]{1,0:T(8,128)(2,1)}, bf16[800,896]{1,0:T(8,128)(2,1)}) custom-call(s32[1]{0:T(128)} %bitcast.62.flip, bf16[800,512]{1,0:T(8,128)(2,1)} %bitcast.173, bf16[800,512]{1,0:T(8,128)(2,1)} %bitcast.187, bf16[1600,256]{1,0:T(8,128)(2,1)} %pad_maximum_fusion.6.own, bf16[1600,256]{1,0:T(8,128)(2,1)} %collective-permute-done.33.side, ...), custom_call_target="tpu_custom_call" | custom-call | tf_op jit(solution)/shard_map/prod/pallas_call | solution.py:326
  374.8 6.9 %convolution_bitcast_fusion = f32[1600,3,128]{2,0,1:T(8,128)S(1)} fusion(bf16[16,128,1600,1]{2,1,3,0:T(8,128)(2,1)} %bitcast.200, bf16[16,3,128,128]{3,2,1,0:T(8,128)(2,1)S(1)} %copy-done.5), kind=kOutput, calls=%fused_computation.26 | convolution fusion | flops 2516582400 | bytes 10584064 | tf_op jit(solution)/shard_map/sklt,std->dkl/dot_general | solution.py:436
  384.4 11.7 %collective-permute-done.35 = bf16[800,896]{1,0:T(8,128)(2,1)} collective-permute-done((bf16[800,896]{1,0:T(8,128)(2,1)}, bf16[800,896]{1,0:T(8,128)(2,1)}, u32[]{:S(2)}, u32[]{:S(2)}) %collective-permute-start.35) | collective-permute-done | bytes 1433632 | tf_op jit(solution)/shard_map/ppermute | solution.py:407
  396.1 4.4 maximum_select_fusion
  408.2 2.6 collective-permute-start.23
  410.8 11.6 %collective-permute-done.16 = bf16[800,3,128]{2,0,1:T(8,128)(2,1)} collective-permute-done((bf16[800,3,128]{2,0,1:T(8,128)(2,1)}, bf16[800,3,128]{2,0,1:T(8,128)(2,1)}, u32[]{:S(2)}, u32[]{:S(2)}) %collective-permute-start.16) | collective-permute-done | bytes 614432 | tf_op jit(solution)/shard_map/ppermute | solution.py:407
  430.9 4.7 collective-permute-done.13
  435.6 5.7 %convolution_bitcast_fusion.2 = f32[1600,256]{1,0:T(8,128)S(1)} fusion(bf16[1600,2400]{1,0:T(8,128)(2,1)} %param.22, bf16[2400,128]{1,0:T(8,128)(2,1)} %collective-permute-done.13, bf16[2400,128]{1,0:T(8,128)(2,1)S(1)} %copy-done.47), kind=kOutput, calls=%fused_computation.29 | convolution fusion | flops 1968537600 | bytes 10547200 | tf_op jit(solution)/shard_map/de,et->dt/dot_general | solution.py:436
  454.9 2.6 fusion.102
  457.5 2.6 fusion.101
  460.2 4.0 fusion.3
  469.3 13.8 %all-to-all-start.5 = ((f32[32,31,128]{2,1,0:T(8,128)}), f32[32,31,128]{2,1,0:T(8,128)}, u32[]{:S(2)}, u32[]{:S(2)}) async-start(f32[32,31,128]{2,1,0:T(8,128)} %broadcast_in_dim.22), calls=%async_computation.5 | async-start | bytes 1048576 | tf_op jit(solution)/shard_map/all_to_all | solution.py:695
  489.7 2.4 fusion.19
  494.0 2.3 fusion.20
  499.0 2.8 collective-permute-start.28
  501.9 2.5 fusion.57
  508.4 3.3 collective-permute-start.36
  515.9 2.4 convert_bitcast_fusion
  518.3 30.2 %collective-permute-done.36 = bf16[400,800]{1,0:T(8,128)(2,1)S(1)} collective-permute-done((bf16[400,800]{1,0:T(8,128)(2,1)}, bf16[400,800]{1,0:T(8,128)(2,1)S(1)}, u32[]{:S(2)}, u32[]{:S(2)}) %collective-permute-start.36) | collective-permute-done | bytes 640032 | tf_op jit(solution)/shard_map/ppermute | solution.py:589
  (348 shorter events, 122.0 us)
Async XLA Ops:
  7.2 85.2 %copy-start = (bf16[1600,800]{0,1:T(8,128)(2,1)S(1)}, bf16[1600,800]{0,1:T(8,128)(2,1)}, u32[]{:S(2)}) copy-start(bf16[1600,800]{0,1:T(8,128)(2,1)} %param.24) | copy-start | bytes 7680004
  8.6 10.4 %collective-permute-start = (bf16[1600,128]{1,0:T(8,128)(2,1)S(1)}, bf16[1600,128]{1,0:T(8,128)(2,1)S(1)}, u32[]{:S(2)}, u32[]{:S(2)}) collective-permute-start(bf16[1600,128]{1,0:T(8,128)(2,1)S(1)} %bitcast.167), channel_id=1, source_target_pairs={{0,16},{16,0},{1,17},{17,1},{2,18},{18,2},{3,19},{19,3},{4,20},{20... | collective-permute-start | bytes 1228808 | tf_op jit(solution)/shard_map/ppermute | solution.py:407
  27.3 14.2 %collective-permute-start.1 = (bf16[2400,128]{1,0:T(8,128)(2,1)}, bf16[2400,128]{1,0:T(8,128)(2,1)}, u32[]{:S(2)}, u32[]{:S(2)}) collective-permute-start(bf16[2400,128]{1,0:T(8,128)(2,1)} %fusion.9), channel_id=1, source_target_pairs={{0,16},{16,0},{1,17},{17,1},{2,18},{18,2},{3,19},{19,3},{4,20},{20... | collective-permute-start | bytes 1843208 | tf_op jit(solution)/shard_map/ppermute | solution.py:407
  44.5 42.0 %all-to-all-start = ((bf16[16,3,128,128]{3,2,1,0:T(8,128)(2,1)}), bf16[16,3,128,128]{3,2,1,0:T(8,128)(2,1)}, u32[]{:S(2)}, u32[]{:S(2)}) async-start(bf16[16,3,128,128]{3,2,1,0:T(8,128)(2,1)} %pad_maximum_fusion.2), calls=%async_computation | async-start | bytes 3145728 | tf_op jit(solution)/shard_map/all_to_all | solution.py:416
  52.7 218.0 %all-gather.2.cloned.1.call-start = ((), (), s32[]{:S(2)}) async-start(), calls=%async_computation.8 | async-start | bytes 7241728 | tf_op jit(solution)/shard_map/all_gather | solution.py:470
  91.1 103.1 %collective-permute-start.6 = (bf16[3200,400]{0,1:T(8,128)(2,1)}, bf16[3200,400]{0,1:T(8,128)(2,1)}, u32[]{:S(2)}, u32[]{:S(2)}) collective-permute-start(bf16[3200,400]{0,1:T(8,128)(2,1)} %dynamic_slice.112), channel_id=1, source_target_pairs={{0,16},{16,0},{1,17},{17,1},{2,18},{18,2},{3,19},{19,3},{4,20},{20... | collective-permute-start | bytes 7680008 | tf_op jit(solution)/shard_map/ppermute | solution.py:407
  94.1 88.6 %copy-start.57 = (f32[6400]{0:T(1024)S(1)}, f32[6400]{0:T(1024)}, u32[]{:S(2)}) copy-start(f32[6400]{0:T(1024)} %param.29) | copy-start | bytes 76804
  94.1 85.6 %collective-permute-start.2 = (bf16[800,800]{0,1:T(8,128)(2,1)}, bf16[800,800]{0,1:T(8,128)(2,1)}, u32[]{:S(2)}, u32[]{:S(2)}) collective-permute-start(bf16[800,800]{0,1:T(8,128)(2,1)} %constant_dynamic-slice_fusion.14), channel_id=1, source_target_pairs={{0,16},{16,0},{1,17},{17,1},{2,18},{18,2},{3,19},{19,3},{4,20},{20... | collective-permute-start | bytes 3840008 | tf_op jit(solution)/shard_map/ppermute | solution.py:407
  107.8 84.6 %all-to-all-start.1 = ((bf16[16,128,128]{2,1,0:T(8,128)(2,1)}), bf16[16,128,128]{2,1,0:T(8,128)(2,1)}, u32[]{:S(2)}, u32[]{:S(2)}) async-start(bf16[16,128,128]{2,1,0:T(8,128)(2,1)} %get-tuple-element.63), calls=%async_computation.1 | async-start | bytes 1048576 | tf_op jit(solution)/shard_map/all_to_all | solution.py:416
  115.7 392.7 %reduce-scatter.5.cloned.1.call-start = ((), (), s32[]{:S(2)}) async-start(), calls=%async_computation.10 | async-start | bytes 3584000 | tf_op jit(solution)/shard_map/reduce_scatter | solution.py:549
  179.7 21.6 %collective-permute-start.3 = (bf16[800,800]{0,1:T(8,128)(2,1)}, bf16[800,800]{0,1:T(8,128)(2,1)}, u32[]{:S(2)}, u32[]{:S(2)}) collective-permute-start(bf16[800,800]{0,1:T(8,128)(2,1)} %collective-permute-done.2), channel_id=1, source_target_pairs={{0,1},{1,0},{2,3},{3,2},{4,5},{5,4},{6,7},{7,6},{8,9},{9,8},{10,11... | collective-permute-start | bytes 3840008 | tf_op jit(solution)/shard_map/ppermute | solution.py:410
  181.4 11.0 %collective-permute-start.5 = (bf16[1600,128]{1,0:T(8,128)(2,1)S(1)}, bf16[1600,128]{1,0:T(8,128)(2,1)S(1)}, u32[]{:S(2)}, u32[]{:S(2)}) collective-permute-start(bf16[1600,128]{1,0:T(8,128)(2,1)S(1)} %bitcast.170), channel_id=1, source_target_pairs={{0,16},{16,0},{1,17},{17,1},{2,18},{18,2},{3,19},{19,3},{4,20},{20... | collective-permute-start | bytes 1228808 | tf_op jit(solution)/shard_map/ppermute | solution.py:407
  194.2 35.0 %collective-permute-start.7 = (bf16[3200,400]{0,1:T(8,128)(2,1)}, bf16[3200,400]{0,1:T(8,128)(2,1)S(1)}, u32[]{:S(2)}, u32[]{:S(2)}) collective-permute-start(bf16[3200,400]{0,1:T(8,128)(2,1)} %collective-permute-done.6), channel_id=1, source_target_pairs={{0,1},{1,0},{2,3},{3,2},{4,5},{5,4},{6,7},{7,6},{8,9},{9,8},{10,11... | collective-permute-start | bytes 7680008 | tf_op jit(solution)/shard_map/ppermute | solution.py:410
  196.7 40.8 %collective-permute-start.11 = (bf16[1600,256]{1,0:T(8,128)(2,1)S(1)}, bf16[1600,256]{1,0:T(8,128)(2,1)S(1)}, u32[]{:S(2)}, u32[]{:S(2)}) collective-permute-start(bf16[1600,256]{1,0:T(8,128)(2,1)S(1)} %get-tuple-element.173.own), channel_id=1, source_target_pairs={{0,2},{1,3},{2,0},{3,1},{4,6},{5,7},{6,4},{7,5},{8,10},{9,11},{10,... | collective-permute-start | bytes 2457608 | tf_op jit(solution)/shard_map/ppermute | solution.py:413
  206.5 10.8 %collective-permute-start.4 = (bf16[1600,128]{1,0:T(8,128)(2,1)S(1)}, bf16[1600,128]{1,0:T(8,128)(2,1)S(1)}, u32[]{:S(2)}, u32[]{:S(2)}) collective-permute-start(bf16[1600,128]{1,0:T(8,128)(2,1)S(1)} %add_convert_fusion.2), channel_id=1, source_target_pairs={{0,16},{16,0},{1,17},{17,1},{2,18},{18,2},{3,19},{19,3},{4,20},{20... | collective-permute-start | bytes 1228808 | tf_op jit(solution)/shard_map/ppermute | solution.py:407
  228.1 12.1 %collective-permute-start.9 = (bf16[2,2,1,400,256]{4,3,0,2,1:T(8,128)(2,1)}, bf16[2,2,1,400,256]{4,3,0,2,1:T(8,128)(2,1)}, u32[]{:S(2)}, u32[]{:S(2)}) collective-permute-start(bf16[2,2,1,400,256]{4,3,0,2,1:T(8,128)(2,1)} %copy.107), channel_id=1, source_target_pairs={{0,1},{1,0},{2,3},{3,2},{4,5},{5,4},{6,7},{7,6},{8,9},{9,8},{10,11... | collective-permute-start | bytes 2457608 | tf_op jit(solution)/shard_map/ppermute | solution.py:410
  238.9 23.7 %collective-permute-start.12 = (bf16[1600,512]{1,0:T(8,128)(2,1)}, bf16[1600,512]{1,0:T(8,128)(2,1)}, u32[]{:S(2)}, u32[]{:S(2)}) collective-permute-start(bf16[1600,512]{1,0:T(8,128)(2,1)} %pad_maximum_fusion), channel_id=1, source_target_pairs={{0,1},{1,0},{2,3},{3,2},{4,5},{5,4},{6,7},{7,6},{8,9},{9,8},{10,11... | collective-permute-start | bytes 4915208 | tf_op jit(solution)/shard_map/ppermute | solution.py:410
  242.5 19.3 %collective-permute-start.10 = (bf16[2,1,1,400,512]{4,3,0,2,1:T(8,128)(2,1)S(1)}, bf16[2,1,1,400,512]{4,3,0,2,1:T(8,128)(2,1)S(1)}, u32[]{:S(2)}, u32[]{:S(2)}) collective-permute-start(bf16[2,1,1,400,512]{4,3,0,2,1:T(8,128)(2,1)S(1)} %get-tuple-element.147), channel_id=1, source_target_pairs={{0,2},{1,3},{2,0},{3,1},{4,6},{5,7},{6,4},{7,5},{8,10},{9,11},{10,... | collective-permute-start | bytes 2457608 | tf_op jit(solution)/shard_map/ppermute | solution.py:413
  243.8 35.7 %collective-permute-start.33 = (bf16[1600,256]{1,0:T(8,128)(2,1)}, bf16[1600,256]{1,0:T(8,128)(2,1)}, u32[]{:S(2)}, u32[]{:S(2)}) collective-permute-start(bf16[1600,256]{1,0:T(8,128)(2,1)} %pad_maximum_fusion.6.own), channel_id=1, source_target_pairs={{0,2},{1,3},{2,0},{3,1},{4,6},{5,7},{6,4},{7,5},{8,10},{9,11},{10,... | collective-permute-start | bytes 2457608 | tf_op jit(solution)/shard_map/ppermute | solution.py:413
  244.9 34.6 %collective-permute-start.8 = (bf16[1600,128]{1,0:T(8,128)(2,1)}, bf16[1600,128]{1,0:T(8,128)(2,1)}, u32[]{:S(2)}, u32[]{:S(2)}) collective-permute-start(bf16[1600,128]{1,0:T(8,128)(2,1)} %slice.324), channel_id=1, source_target_pairs={{0,16},{16,0},{1,17},{17,1},{2,18},{18,2},{3,19},{19,3},{4,20},{20... | collective-permute-start | bytes 1228808 | tf_op jit(solution)/shard_map/ppermute | solution.py:407
  274.1 23.5 %collective-permute-start.31 = (bf16[2,2,1,400,256]{4,3,0,2,1:T(8,128)(2,1)}, bf16[2,2,1,400,256]{4,3,0,2,1:T(8,128)(2,1)}, u32[]{:S(2)}, u32[]{:S(2)}) collective-permute-start(bf16[2,2,1,400,256]{4,3,0,2,1:T(8,128)(2,1)} %copy.109), channel_id=1, source_target_pairs={{0,1},{1,0},{2,3},{3,2},{4,5},{5,4},{6,7},{7,6},{8,9},{9,8},{10,11... | collective-permute-start | bytes 2457608 | tf_op jit(solution)/shard_map/ppermute | solution.py:410
  288.5 31.3 %all-to-all-start.2 = ((bf16[16,128,128]{2,1,0:T(8,128)(2,1)}), bf16[16,128,128]{2,1,0:T(8,128)(2,1)}, u32[]{:S(2)}, u32[]{:S(2)}) async-start(bf16[16,128,128]{2,1,0:T(8,128)(2,1)} %bitcast.14), calls=%async_computation.2 | async-start | bytes 1048576 | tf_op jit(solution)/shard_map/all_to_all | solution.py:416
  297.1 56.4 %collective-permute-start.34 = (bf16[1600,512]{1,0:T(8,128)(2,1)}, bf16[1600,512]{1,0:T(8,128)(2,1)}, u32[]{:S(2)}, u32[]{:S(2)}) collective-permute-start(bf16[1600,512]{1,0:T(8,128)(2,1)} %pad_maximum_fusion.1), channel_id=1, source_target_pairs={{0,1},{1,0},{2,3},{3,2},{4,5},{5,4},{6,7},{7,6},{8,9},{9,8},{10,11... | collective-permute-start | bytes 4915208 | tf_op jit(solution)/shard_map/ppermute | solution.py:410
  299.9 53.6 %collective-permute-start.32 = (bf16[2,1,1,400,512]{4,3,0,2,1:T(8,128)(2,1)S(1)}, bf16[2,1,1,400,512]{4,3,0,2,1:T(8,128)(2,1)S(1)}, u32[]{:S(2)}, u32[]{:S(2)}) collective-permute-start(bf16[2,1,1,400,512]{4,3,0,2,1:T(8,128)(2,1)S(1)} %get-tuple-element.143), channel_id=1, source_target_pairs={{0,2},{1,3},{2,0},{3,1},{4,6},{5,7},{6,4},{7,5},{8,10},{9,11},{10,... | collective-permute-start | bytes 2457608 | tf_op jit(solution)/shard_map/ppermute | solution.py:413
  320.5 26.7 %all-to-all-start.4 = ((f32[32,4,128]{2,1,0:T(4,128)}), f32[32,4,128]{2,1,0:T(4,128)S(1)}, u32[]{:S(2)}, u32[]{:S(2)}) async-start(f32[32,4,128]{2,1,0:T(4,128)} %bitcast.27), calls=%async_computation.4 | async-start | bytes 131072 | tf_op jit(solution)/shard_map/all_to_all | solution.py:695
  347.1 53.7 %all-to-all-start.3 = ((bf16[16,3,128,128]{3,2,1,0:T(8,128)(2,1)}), bf16[16,3,128,128]{3,2,1,0:T(8,128)(2,1)}, u32[]{:S(2)}, u32[]{:S(2)}) async-start(bf16[16,3,128,128]{3,2,1,0:T(8,128)(2,1)} %attb.1), calls=%async_computation.3 | async-start | bytes 3145728 | tf_op jit(solution)/shard_map/all_to_all | solution.py:416
  353.3 162.5 %reduce-scatter.3.cloned.1.call-start = ((), (), s32[]{:S(2)}) async-start(), calls=%async_computation.9 | async-start | bytes 3584000 | tf_op jit(solution)/shard_map/reduce_scatter | solution.py:549
  363.2 32.9 %collective-permute-start.35 = (bf16[800,896]{1,0:T(8,128)(2,1)}, bf16[800,896]{1,0:T(8,128)(2,1)}, u32[]{:S(2)}, u32[]{:S(2)}) collective-permute-start(bf16[800,896]{1,0:T(8,128)(2,1)} %get-tuple-element.107), channel_id=1, source_target_pairs={{0,16},{16,0},{1,17},{17,1},{2,18},{18,2},{3,19},{19,3},{4,20},{20... | collective-permute-start | bytes 4300808 | tf_op jit(solution)/shard_map/ppermute | solution.py:407
  372.7 32.2 %collective-permute-start.22 = (bf16[1600,128]{1,0:T(8,128)(2,1)S(1)}, bf16[1600,128]{1,0:T(8,128)(2,1)}, u32[]{:S(2)}, u32[]{:S(2)}) collective-permute-start(bf16[1600,128]{1,0:T(8,128)(2,1)S(1)} %copy-done.18), channel_id=1, source_target_pairs={{0,16},{16,0},{1,17},{17,1},{2,18},{18,2},{3,19},{19,3},{4,20},{20... | collective-permute-start | bytes 1228808 | tf_op jit(solution)/shard_map/ppermute | solution.py:407
  373.0 54.6 %collective-permute-start.24 = (bf16[800,128]{1,0:T(8,128)(2,1)S(1)}, bf16[800,128]{1,0:T(8,128)(2,1)S(1)}, u32[]{:S(2)}, u32[]{:S(2)}) collective-permute-start(bf16[800,128]{1,0:T(8,128)(2,1)S(1)} %copy-done.27), channel_id=1, source_target_pairs={{0,16},{16,0},{1,17},{17,1},{2,18},{18,2},{3,19},{19,3},{4,20},{20... | collective-permute-start | bytes 614408 | tf_op jit(solution)/shard_map/ppermute | solution.py:407
  384.1 38.3 %collective-permute-start.16 = (bf16[800,3,128]{2,0,1:T(8,128)(2,1)}, bf16[800,3,128]{2,0,1:T(8,128)(2,1)}, u32[]{:S(2)}, u32[]{:S(2)}) collective-permute-start(bf16[800,3,128]{2,0,1:T(8,128)(2,1)} %dynamic-slice_convert_fusion), channel_id=1, source_target_pairs={{0,16},{16,0},{1,17},{17,1},{2,18},{18,2},{3,19},{19,3},{4,20},{20... | collective-permute-start | bytes 1843208 | tf_op jit(solution)/shard_map/ppermute | solution.py:407
  403.6 32.0 %collective-permute-start.13 = (bf16[2400,128]{1,0:T(8,128)(2,1)}, bf16[2400,128]{1,0:T(8,128)(2,1)}, u32[]{:S(2)}, u32[]{:S(2)}) collective-permute-start(bf16[2400,128]{1,0:T(8,128)(2,1)} %get-tuple-element.155), channel_id=1, source_target_pairs={{0,16},{16,0},{1,17},{17,1},{2,18},{18,2},{3,19},{19,3},{4,20},{20... | collective-permute-start | bytes 1843208 | tf_op jit(solution)/shard_map/ppermute | solution.py:407
  408.2 21.4 %collective-permute-start.23 = (bf16[4,2,1,100,256]{4,3,2,1,0:T(8,128)(2,1)S(1)}, bf16[4,2,1,100,256]{4,3,2,1,0:T(8,128)(2,1)S(1)}, u32[]{:S(2)}, u32[]{:S(2)}) collective-permute-start(bf16[4,2,1,100,256]{4,3,2,1,0:T(8,128)(2,1)S(1)} %get-tuple-element.160), channel_id=1, source_target_pairs={{0,1},{1,0},{2,3},{3,2},{4,5},{5,4},{6,7},{7,6},{8,9},{9,8},{10,11... | collective-permute-start | bytes 1228808 | tf_op jit(solution)/shard_map/ppermute | solution.py:410
  425.0 58.0 %collective-permute-start.21 = (bf16[800,128]{1,0:T(8,128)(2,1)}, bf16[800,128]{1,0:T(8,128)(2,1)}, u32[]{:S(2)}, u32[]{:S(2)}) collective-permute-start(bf16[800,128]{1,0:T(8,128)(2,1)} %get-tuple-element.170), channel_id=1, source_target_pairs={{3,12},{7,14},{10,15},{19,28},{23,30},{26,31}} | collective-permute-start | bytes 614408 | tf_op jit(solution)/shard_map/ppermute | solution.py:671
  426.3 57.2 %collective-permute-start.20 = (bf16[800,128]{1,0:T(8,128)(2,1)}, bf16[800,128]{1,0:T(8,128)(2,1)}, u32[]{:S(2)}, u32[]{:S(2)}) collective-permute-start(bf16[800,128]{1,0:T(8,128)(2,1)} %get-tuple-element.169), channel_id=1, source_target_pairs={{0,10},{1,5},{2,6},{3,11},{4,12},{5,7},{6,2},{7,13},{8,9},{9,4},{1... | collective-permute-start | bytes 614408 | tf_op jit(solution)/shard_map/ppermute | solution.py:671
  428.5 18.4 %collective-permute-start.25 = (bf16[800,256]{1,0:T(8,128)(2,1)}, bf16[800,256]{1,0:T(8,128)(2,1)}, u32[]{:S(2)}, u32[]{:S(2)}) collective-permute-start(bf16[800,256]{1,0:T(8,128)(2,1)} %pad_maximum_fusion.9), channel_id=1, source_target_pairs={{0,2},{1,3},{2,0},{3,1},{4,6},{5,7},{6,4},{7,5},{8,10},{9,11},{10,... | collective-permute-start | bytes 1228808 | tf_op jit(solution)/shard_map/ppermute | solution.py:413
  430.6 19.6 %collective-permute-start.27 = (bf16[4,1,1,100,512]{4,3,2,1,0:T(8,128)(2,1)}, bf16[4,1,1,100,512]{4,3,2,1,0:T(8,128)(2,1)}, u32[]{:S(2)}, u32[]{:S(2)}) collective-permute-start(bf16[4,1,1,100,512]{4,3,2,1,0:T(8,128)(2,1)} %get-tuple-element.159), channel_id=1, source_target_pairs={{0,2},{1,3},{2,0},{3,1},{4,6},{5,7},{6,4},{7,5},{8,10},{9,11},{10,... | collective-permute-start | bytes 1228808 | tf_op jit(solution)/shard_map/ppermute | solution.py:413
  442.2 11.2 %collective-permute-start.14 = (bf16[1600,128]{1,0:T(8,128)(2,1)}, bf16[1600,128]{1,0:T(8,128)(2,1)}, u32[]{:S(2)}, u32[]{:S(2)}) collective-permute-start(bf16[1600,128]{1,0:T(8,128)(2,1)} %slice.323), channel_id=1, source_target_pairs={{0,16},{16,0},{1,17},{17,1},{2,18},{18,2},{3,19},{19,3},{4,20},{20... | collective-permute-start | bytes 1228808 | tf_op jit(solution)/shard_map/ppermute | solution.py:407
  446.8 37.9 %collective-permute-start.19 = (bf16[800,128]{1,0:T(8,128)(2,1)}, bf16[800,128]{1,0:T(8,128)(2,1)}, u32[]{:S(2)}, u32[]{:S(2)}) collective-permute-start(bf16[800,128]{1,0:T(8,128)(2,1)} %get-tuple-element.172), channel_id=1, source_target_pairs={{0,5},{1,0},{2,11},{3,1},{4,7},{5,2},{6,13},{7,8},{8,14},{9,3},{10... | collective-permute-start | bytes 614408 | tf_op jit(solution)/shard_map/ppermute | solution.py:671
  450.2 34.5 %collective-permute-start.18 = (bf16[800,128]{1,0:T(8,128)(2,1)}, bf16[800,128]{1,0:T(8,128)(2,1)S(1)}, u32[]{:S(2)}, u32[]{:S(2)}) collective-permute-start(bf16[800,128]{1,0:T(8,128)(2,1)} %get-tuple-element.171), channel_id=1, source_target_pairs={{0,0},{1,11},{2,1},{3,6},{4,2},{5,13},{6,7},{7,3},{8,8},{9,14},{10... | collective-permute-start | bytes 614408 | tf_op jit(solution)/shard_map/ppermute | solution.py:671
  453.4 31.4 %collective-permute-start.17 = (bf16[800,128]{1,0:T(8,128)(2,1)}, bf16[800,128]{1,0:T(8,128)(2,1)}, u32[]{:S(2)}, u32[]{:S(2)}) collective-permute-start(bf16[800,128]{1,0:T(8,128)(2,1)} %get-tuple-element.168), channel_id=1, source_target_pairs={{0,11},{1,6},{2,0},{3,7},{4,1},{5,12},{6,8},{7,2},{8,3},{9,9},{10,... | collective-permute-start | bytes 614408 | tf_op jit(solution)/shard_map/ppermute | solution.py:671
  469.3 37.1 %all-to-all-start.5 = ((f32[32,31,128]{2,1,0:T(8,128)}), f32[32,31,128]{2,1,0:T(8,128)}, u32[]{:S(2)}, u32[]{:S(2)}) async-start(f32[32,31,128]{2,1,0:T(8,128)} %broadcast_in_dim.22), calls=%async_computation.5 | async-start | bytes 1048576 | tf_op jit(solution)/shard_map/all_to_all | solution.py:695
  483.1 9.1 %collective-permute-start.26 = (bf16[800,512]{1,0:T(8,128)(2,1)}, bf16[800,512]{1,0:T(8,128)(2,1)S(1)}, u32[]{:S(2)}, u32[]{:S(2)}) collective-permute-start(bf16[800,512]{1,0:T(8,128)(2,1)} %pad_maximum_fusion.8), channel_id=1, source_target_pairs={{0,1},{1,0},{2,3},{3,2},{4,5},{5,4},{6,7},{7,6},{8,9},{9,8},{10,11... | collective-permute-start | bytes 2457608 | tf_op jit(solution)/shard_map/ppermute | solution.py:410
  483.5 18.3 %collective-permute-start.15 = (bf16[1600,128]{1,0:T(8,128)(2,1)}, bf16[1600,128]{1,0:T(8,128)(2,1)}, u32[]{:S(2)}, u32[]{:S(2)}) collective-permute-start(bf16[1600,128]{1,0:T(8,128)(2,1)} %slice.322), channel_id=1, source_target_pairs={{0,16},{16,0},{1,17},{17,1},{2,18},{18,2},{3,19},{19,3},{4,20},{20... | collective-permute-start | bytes 1228808 | tf_op jit(solution)/shard_map/ppermute | solution.py:407
  498.5 15.2 %collective-permute-start.30 = (bf16[100,800]{1,0:T(8,128)(2,1)}, bf16[100,800]{1,0:T(8,128)(2,1)}, u32[]{:S(2)}, u32[]{:S(2)}) collective-permute-start(bf16[100,800]{1,0:T(8,128)(2,1)} %get-tuple-element.165), channel_id=1, source_target_pairs={{0,12},{1,13},{2,14},{3,15},{4,0},{5,1},{6,2},{7,3},{8,4},{9,5},{1... | collective-permute-start | bytes 480008 | tf_op jit(solution)/shard_map/ppermute | solution.py:634
  498.8 15.2 %collective-permute-start.29 = (bf16[100,800]{1,0:T(8,128)(2,1)}, bf16[100,800]{1,0:T(8,128)(2,1)}, u32[]{:S(2)}, u32[]{:S(2)}) collective-permute-start(bf16[100,800]{1,0:T(8,128)(2,1)} %get-tuple-element.166), channel_id=1, source_target_pairs={{0,8},{1,9},{2,10},{3,11},{4,12},{5,13},{6,14},{7,15},{8,0},{9,1},... | collective-permute-start | bytes 480008 | tf_op jit(solution)/shard_map/ppermute | solution.py:634
  499.0 14.9 %collective-permute-start.28 = (bf16[100,800]{1,0:T(8,128)(2,1)}, bf16[100,800]{1,0:T(8,128)(2,1)}, u32[]{:S(2)}, u32[]{:S(2)}) collective-permute-start(bf16[100,800]{1,0:T(8,128)(2,1)} %get-tuple-element.167), channel_id=1, source_target_pairs={{0,4},{1,5},{2,6},{3,7},{4,8},{5,9},{6,10},{7,11},{8,12},{9,13},{1... | collective-permute-start | bytes 480008 | tf_op jit(solution)/shard_map/ppermute | solution.py:634
  508.4 40.1 %collective-permute-start.36 = (bf16[400,800]{1,0:T(8,128)(2,1)}, bf16[400,800]{1,0:T(8,128)(2,1)S(1)}, u32[]{:S(2)}, u32[]{:S(2)}) collective-permute-start(bf16[400,800]{1,0:T(8,128)(2,1)} %bitcast.201), channel_id=1, source_target_pairs={{0,0},{1,1},{2,2},{3,3},{4,4},{5,5},{6,6},{7,7},{8,16},{9,17},{10,... | collective-permute-start | bytes 1920008 | tf_op jit(solution)/shard_map/ppermute | solution.py:589
  (77 other events, 665.7 us)
Sparse Core Ops, SparseCore 0:
  86.6 71.3 all-gather.1
  270.9 65.8 reduce-scatter.4
  400.7 65.2 reduce-scatter.2
